TPU v7x, 256 devices: a whole 4x4x8 slice. The times are simulated.
256 devices in a mesh: seq: 128 (over y, z, x), head: 2 (over core).
Axes of the slice: x: 4, y: 4, z: 8, core: 2. Of those that a mesh axis runs over, the one named last changes fastest.
Arguments:
- queries: bfloat16 [8192, 1536], P('seq', 'head'), may hold values from -6 to 6
- key_vectors: bfloat16 [8192, 512], P('seq', 'head'), may hold values from -6 to 6
- value_vectors: bfloat16 [8192, 512], P('seq', 'head'), may hold values from -6 to 6
- lengths: int32 [64], replicated, may hold values from 1 to 256, 8192 in all
- out_weight: bfloat16 [1536, 1536], P('head', 'seq'), may hold values from -0.15625 to 0.15625
- residual: bfloat16 [8192, 1536], P(('seq', 'head')), may hold values from -6 to 6
- norm_gain: float32 [1536], replicated, may hold values from 0.1 to 1.9
- route_ids: int32 [8192, 6], P(('seq', 'head')), may hold values from 0 to 63, all different within a row; in each aligned block of 32 rows (0 to 31, 32 to 63, ...) at most 6 rows name the same one
- route_logits: float32 [8192, 6], P(('seq', 'head')), may hold values from -8 to 340
- shared_gate_up: bfloat16 [1536, 2, 1024], P(None, None, ('seq', 'head')), may hold values from -0.15625 to 0.15625
- shared_down: bfloat16 [1024, 1536], P(('seq', 'head')), may hold values from -0.1875 to 0.1875
- expert_gate_up: bfloat16 [128, 1536, 2, 256], P('seq'), may hold values from -0.15625 to 0.15625
- expert_down: bfloat16 [128, 256, 1536], P('seq'), may hold values from -0.25 to 0.25
- cache_blocks: bfloat16 [128, 128, 8, 4, 128], P('seq', None, None, 'head'), may hold values from -6 to 6
- block_table: int32 [128], replicated, may hold values from 0 to 127, each once
Outputs:
- layer_out: bfloat16 [8192, 1536], P(('seq', 'head'))
- cache_out: bfloat16 [128, 128, 8, 4, 128], P(None, 'seq', None, 'head')
Inputs may be any that keep to these rules, and one draw needn't show every extreme that they name: The lengths sum to 8192. `route_ids`: each token names 6 different experts; among the tokens of one device no expert is named more than 6 times. `block_table`: every block appears once.
All inputs are finite; a program needn't handle non-finite values.
Results may differ from a plain program's by a relative error of at most 0.0095.
Values may be sent and summed in bfloat16 or wider, within the bound.
A program may use at most 64 MiB of HBM per device.

v0:
```python
import math

import jax
import jax.numpy as jnp
from jax import lax
from jax.sharding import PartitionSpec as P

HD = 128
EXPERTS = 64
TOP = 6
REACH = 4
HALVES = 128
CAP = 6


NEGATIVE = -1e30
EPSILON = 1e-05


def from_behind(shard, axis, by):
    devices = lax.axis_size(axis)
    pairs = [(i, i + by) for i in range(devices) if 0 <= i + by < devices]
    return lax.ppermute(shard, axis, pairs)


def segment_of(positions, lengths):
    request_ends = jnp.cumsum(lengths)
    passed = (request_ends[None, :] <= positions[:, None]).astype(jnp.int32)
    return jnp.sum(passed, axis=1)


def shared_ffn(rows_in, gate_up_part, down_part):
    shared_both = jnp.einsum(
        "td,dcf->tcf", rows_in, gate_up_part, preferred_element_type=jnp.float32
    )
    shared_act = (jax.nn.silu(shared_both[:, 0]) * shared_both[:, 1]).astype(jnp.bfloat16)
    return jnp.dot(shared_act, down_part, preferred_element_type=jnp.float32)


def shards(
    queries,
    key_vectors,
    value_vectors,
    lengths,
    out_weight,
    residual,
    norm_gain,
    route_ids,
    route_logits,
    shared_gate_up,
    shared_down,
    expert_gate_up,
    expert_down,
    cache_blocks,
    block_table,
):
    handed = lax.all_to_all(cache_blocks, "seq", split_axis=1, concat_axis=0, tiled=True)
    cache_out = jnp.take(handed, block_table, axis=0)
    tok_rows = queries.shape[0]
    seq_index = lax.axis_index("seq")
    earlier = [
        from_behind((key_vectors, value_vectors), "seq", offset) for offset in range(REACH, 0, -1)
    ]
    window_keys = jnp.concatenate([member[0] for member in earlier] + [key_vectors], axis=0)
    window_values = jnp.concatenate([member[1] for member in earlier] + [value_vectors], axis=0)
    key_count = window_keys.shape[0]
    kv_heads = key_vectors.shape[1] // HD
    query_heads = queries.shape[1] // HD
    group_size = query_heads // kv_heads
    query_pos = seq_index * tok_rows + jnp.arange(tok_rows, dtype=jnp.int32)
    key_pos = (seq_index - REACH) * tok_rows + jnp.arange(key_count, dtype=jnp.int32)
    visible = (key_pos[None, :] >= 0) & (key_pos[None, :] <= query_pos[:, None])
    visible = visible & (
        segment_of(key_pos, lengths)[None, :] == segment_of(query_pos, lengths)[:, None]
    )
    query_part = queries.reshape(tok_rows, kv_heads, group_size, HD)
    key_part = window_keys.reshape(key_count, kv_heads, HD)
    value_part = window_values.reshape(key_count, kv_heads, HD)
    scores = jnp.einsum(
        "tkgd,wkd->kgtw", query_part, key_part, preferred_element_type=jnp.float32
    ) * (1.0 / math.sqrt(HD))
    scores = jnp.where(visible[None, None], scores, NEGATIVE)
    row_max = jnp.max(scores, axis=-1, keepdims=True)
    weights = jnp.exp(scores - row_max)
    row_total = jnp.sum(weights, axis=-1)
    weighted = jnp.einsum(
        "kgtw,wkd->tkgd",
        weights.astype(jnp.bfloat16),
        value_part,
        preferred_element_type=jnp.float32,
    )
    heads = (weighted / jnp.transpose(row_total, (2, 0, 1))[..., None]).astype(jnp.bfloat16)
    heads = heads.reshape(tok_rows, query_heads * HD)
    partial_out = jnp.dot(
        heads,
        lax.all_gather(out_weight, "seq", axis=1, tiled=True),
        preferred_element_type=jnp.float32,
    )
    attn_out = lax.psum_scatter(partial_out, "head", scatter_dimension=0, tiled=True)
    mixed = residual.astype(jnp.float32) + attn_out
    mean_square = jnp.mean(mixed * mixed, axis=-1, keepdims=True)
    normed = (mixed * lax.rsqrt(mean_square + EPSILON) * norm_gain).astype(jnp.bfloat16)
    gate_up_all, down_all = (
        lax.all_gather(shared_gate_up, ("seq", "head"), axis=2, tiled=True),
        lax.all_gather(shared_down, ("seq", "head"), axis=0, tiled=True),
    )
    shared_part = shared_ffn(normed, gate_up_all, down_all)
    own_tokens = normed.shape[0]
    width_model = normed.shape[1]
    flat_ids = route_ids.reshape(-1)
    onehot = (flat_ids[:, None] == jnp.arange(EXPERTS, dtype=jnp.int32)[None, :]).astype(jnp.int32)
    slot_rank = jnp.sum((jnp.cumsum(onehot, axis=0) - 1) * onehot, axis=1)
    first_slot = flat_ids * CAP + slot_rank
    second_slot = (flat_ids + EXPERTS) * CAP + slot_rank
    token_of = jnp.arange(flat_ids.shape[0], dtype=jnp.int32) // TOP
    routed_rows = normed[token_of]
    outgoing = jnp.zeros((HALVES * CAP, width_model), jnp.bfloat16)
    outgoing = outgoing.at[jnp.concatenate([first_slot, second_slot])].set(
        jnp.concatenate([routed_rows, routed_rows], axis=0)
    )
    local_halves = expert_gate_up.shape[0]
    outgoing = outgoing.reshape(HALVES // local_halves, local_halves, CAP, width_model)
    gate_up = jnp.einsum(
        "nsjd,sdcf->nsjcf",
        lax.all_to_all(outgoing, "seq", split_axis=0, concat_axis=0, tiled=True),
        expert_gate_up,
        preferred_element_type=jnp.float32,
    )
    expert_act = (jax.nn.silu(gate_up[:, :, :, 0]) * gate_up[:, :, :, 1]).astype(jnp.bfloat16)
    half_out = jnp.einsum(
        "nsjf,sfd->nsjd", expert_act, expert_down, preferred_element_type=jnp.float32
    ).astype(jnp.bfloat16)
    returned = lax.all_to_all(half_out, "seq", split_axis=0, concat_axis=0, tiled=True)
    returned = returned.reshape(HALVES * CAP, width_model)
    pair_sum = returned[first_slot].astype(jnp.float32) + returned[second_slot].astype(jnp.float32)
    route_probs = jax.nn.softmax(route_logits, axis=-1)
    routed = jnp.sum(
        route_probs[:, :, None] * pair_sum.reshape(own_tokens, TOP, width_model), axis=1
    )
    layer_out = (mixed + shared_part + routed).astype(jnp.bfloat16)
    return (layer_out, cache_out)


def solution(mesh):
    in_specs = (
        P("seq", "head"),
        P("seq", "head"),
        P("seq", "head"),
        P(),
        P("head", "seq"),
        P(("seq", "head"), None),
        P(),
        P(("seq", "head"), None),
        P(("seq", "head"), None),
        P(None, None, ("seq", "head")),
        P(("seq", "head"), None),
        P("seq", None, None, None),
        P("seq", None, None),
        P("seq", None, None, "head", None),
        P(),
    )
    out_specs = (P(("seq", "head"), None), P(None, "seq", None, "head", None))
    return jax.shard_map(shards, mesh=mesh, in_specs=in_specs, out_specs=out_specs, check_vma=False)
```

profile of v0, /device:TPU:4, one launch (start us, length us, event | category | flops | bytes accessed | tf_op | source)
XLA Modules:
  0.0 409.2 jit_solution(4338545764262982124)
XLA Ops:
  8.8 3.8 collective-permute-start.4
  12.6 3.8 collective-permute-start.5
  16.4 4.6 %collective-permute-start.6 = (bf16[64,256]{1,0:T(8,128)(2,1)}, bf16[64,256]{1,0:T(8,128)(2,1)S(1)}, u32[]{:S(2)}, u32[]{:S(2)}) collective-permute-start(bf16[64,256]{1,0:T(8,128)(2,1)} %param.16), channel_id=1, source_target_pairs={{0,4},{2,6},{4,8},{6,10},{8,12},{10,14},{12,16},{14,18},{16,20},{1... | collective-permute-start | bytes 98312 | tf_op jit(solution)/shard_map/ppermute | solution.py:23
  21.1 3.1 collective-permute-start.7
  24.2 5.0 %collective-permute-start = (bf16[64,256]{1,0:T(8,128)(2,1)}, bf16[64,256]{1,0:T(8,128)(2,1)S(1)}, u32[]{:S(2)}, u32[]{:S(2)}) collective-permute-start(bf16[64,256]{1,0:T(8,128)(2,1)} %param.17), channel_id=1, source_target_pairs={{0,8},{2,10},{4,12},{6,14},{8,16},{10,18},{12,20},{14,22},{16,24},... | collective-permute-start | bytes 98312 | tf_op jit(solution)/shard_map/ppermute | solution.py:23
  31.6 4.1 collective-permute-start.1
  35.7 4.4 %collective-permute-start.2 = (bf16[64,256]{1,0:T(8,128)(2,1)}, bf16[64,256]{1,0:T(8,128)(2,1)S(1)}, u32[]{:S(2)}, u32[]{:S(2)}) collective-permute-start(bf16[64,256]{1,0:T(8,128)(2,1)} %param.17), channel_id=1, source_target_pairs={{0,4},{2,6},{4,8},{6,10},{8,12},{10,14},{12,16},{14,18},{16,20},{1... | collective-permute-start | bytes 98312 | tf_op jit(solution)/shard_map/ppermute | solution.py:23
  43.4 2.7 collective-permute-done.3
  48.0 82.4 %all-gather.8.cloned.1.call-done = bf16[128,12,768]{2,1,0:T(8,128)(2,1)} async-done(((bf16[1,12,768]{2,1,0:T(8,128)(2,1)}), bf16[128,12,768]{2,1,0:T(8,128)(2,1)}) %all-gather.8.cloned.1.call-update) | async-done | bytes 2359312 | tf_op jit(solution)/shard_map/all_gather | solution.py:96
  130.5 3.6 reshape.454
  138.4 8.1 %reduce-scatter.2.cloned.1.call-done = f32[32,1536]{1,0:T(8,128)} async-done(((f32[64,1536]{1,0:T(8,128)}), f32[32,1536]{1,0:T(8,128)}) %reduce-scatter.2.cloned.1.call-update) | async-done | bytes 196624 | tf_op jit(solution)/shard_map/reduce_scatter | solution.py:99
  150.5 3.9 scatter_custom_fusion
  154.4 2.5 reshape.403
  156.8 91.5 %all_to_all.22 = bf16[128,1,6,1536]{3,2,1,0:T(8,128)(2,1)} all-to-all(bf16[128,1,6,1536]{3,2,1,0:T(8,128)(2,1)} %bitcast.96), channel_id=1, replica_groups=mesh['seq'=128,'head'=2] {'seq'}, dimensions={0} | all-to-all | bytes 4718592 | tf_op jit(solution)/shard_map/all_to_all | solution.py:125
  248.3 9.2 %all-to-all-start.2 = ((bf16[1,128,8,2,128]{4,3,2,0,1:T(2,128)(2,1)}), bf16[1,128,8,2,128]{4,3,2,0,1:T(2,128)(2,1)S(1)}, u32[]{:S(2)}, u32[]{:S(2)}) async-start(bf16[1,128,8,2,128]{4,3,2,0,1:T(2,128)(2,1)} %bitcast.36), calls=%async_computation.3 | async-start | bytes 1048576 | tf_op jit(solution)/shard_map/all_to_all | solution.py:57
  257.5 3.3 fusion.10
  261.7 3.0 copy.68
  264.6 10.9 %all-to-all-done.2 = bf16[1,128,8,2,128]{4,3,2,0,1:T(2,128)(2,1)S(1)} async-done(((bf16[1,128,8,2,128]{4,3,2,0,1:T(2,128)(2,1)}), bf16[1,128,8,2,128]{4,3,2,0,1:T(2,128)(2,1)S(1)}, u32[]{:S(2)}, u32[]{:S(2)}) %all-to-all-start.2) | async-done | bytes 524320 | tf_op jit(solution)/shard_map/all_to_all | solution.py:57
  275.5 8.3 %all-to-all-start.1 = ((bf16[128,1,6,1536]{3,2,1,0:T(8,128)(2,1)}), bf16[128,1,6,1536]{3,2,1,0:T(8,128)(2,1)}, u32[]{:S(2)}, u32[]{:S(2)}) async-start(bf16[128,1,6,1536]{3,2,1,0:T(8,128)(2,1)} %copy.68), calls=%async_computation.2 | async-start | bytes 6291456 | tf_op jit(solution)/shard_map/all_to_all | solution.py:133
  287.5 5.9 %reshape.456 = bf16[1024,1536]{1,0:T(8,128)(2,1)} reshape(bf16[256,4,1536]{2,1,0:T(4,128)(2,1)} %all-gather.10.cloned.1.call-done) | data formatting | bytes 6291456
  293.4 89.9 %all-gather.6.cloned.1.call-done = bf16[1536,2,1024]{0,1,2:T(2,128)(2,1)} async-done(((bf16[1536,2,4]{0,1,2:T(2,128)(2,1)}), bf16[1536,2,1024]{0,1,2:T(2,128)(2,1)}) %all-gather.6.cloned.1.call-update) | async-done | bytes 6291472 | tf_op jit(solution)/shard_map/all_gather | solution.py:104
  383.3 5.5 %fusion = f32[32,2,1024]{2,0,1:T(8,128)} fusion(bf16[1536,2,1024]{0,1,2:T(2,128)(2,1)} %all-gather.6.cloned.1.call-done, bf16[32,1536]{1,0:T(8,128)(2,1)S(1)} %multiply_convert_fusion), kind=kOutput, calls=%fused_computation.5 | convolution fusion | flops 201326592 | bytes 6651904 | tf_op jit(solution)/shard_map/td,dcf->tcf/dot_general | solution.py:33
  388.7 3.7 reshape.407
  398.3 3.4 fusion.7
  (103 shorter events, 26.5 us)
Async XLA Ops:
  8.0 252.8 %copy-start = (bf16[1,256,1536]{2,1,0:T(8,128)(2,1)S(1)}, bf16[1,256,1536]{2,1,0:T(8,128)(2,1)}, u32[]{:S(2)}) copy-start(bf16[1,256,1536]{2,1,0:T(8,128)(2,1)} %param.27) | copy-start | bytes 2359300
  8.0 122.5 %all-gather.8.cloned.1.call-start = ((), (), s32[]{:S(2)}) async-start(), calls=%async_computation.6 | async-start | bytes 3170304 | tf_op jit(solution)/shard_map/all_gather | solution.py:96
  8.7 137.7 %reduce-scatter.2.cloned.1.call-start = ((), (), s32[]{:S(2)}) async-start(), calls=%async_computation.4 | async-start | bytes 589824 | tf_op jit(solution)/shard_map/reduce_scatter | solution.py:99
  8.8 22.8 %collective-permute-start.4 = (bf16[64,256]{1,0:T(8,128)(2,1)}, bf16[64,256]{1,0:T(8,128)(2,1)S(1)}, u32[]{:S(2)}, u32[]{:S(2)}) collective-permute-start(bf16[64,256]{1,0:T(8,128)(2,1)} %param.16), channel_id=1, source_target_pairs={{0,8},{2,10},{4,12},{6,14},{8,16},{10,18},{12,20},{14,22},{16,24},... | collective-permute-start | bytes 98312 | tf_op jit(solution)/shard_map/ppermute | solution.py:23
  12.6 23.1 %collective-permute-start.5 = (bf16[64,256]{1,0:T(8,128)(2,1)}, bf16[64,256]{1,0:T(8,128)(2,1)S(1)}, u32[]{:S(2)}, u32[]{:S(2)}) collective-permute-start(bf16[64,256]{1,0:T(8,128)(2,1)} %param.16), channel_id=1, source_target_pairs={{0,6},{2,8},{4,10},{6,12},{8,14},{10,16},{12,18},{14,20},{16,22},{... | collective-permute-start | bytes 98312 | tf_op jit(solution)/shard_map/ppermute | solution.py:23
  16.4 23.7 %collective-permute-start.6 = (bf16[64,256]{1,0:T(8,128)(2,1)}, bf16[64,256]{1,0:T(8,128)(2,1)S(1)}, u32[]{:S(2)}, u32[]{:S(2)}) collective-permute-start(bf16[64,256]{1,0:T(8,128)(2,1)} %param.16), channel_id=1, source_target_pairs={{0,4},{2,6},{4,8},{6,10},{8,12},{10,14},{12,16},{14,18},{16,20},{1... | collective-permute-start | bytes 98312 | tf_op jit(solution)/shard_map/ppermute | solution.py:23
  21.1 21.2 %collective-permute-start.7 = (bf16[64,256]{1,0:T(8,128)(2,1)}, bf16[64,256]{1,0:T(8,128)(2,1)S(1)}, u32[]{:S(2)}, u32[]{:S(2)}) collective-permute-start(bf16[64,256]{1,0:T(8,128)(2,1)} %param.16), channel_id=1, source_target_pairs={{0,2},{2,4},{4,6},{6,8},{8,10},{10,12},{12,14},{14,16},{16,18},{18... | collective-permute-start | bytes 98312 | tf_op jit(solution)/shard_map/ppermute | solution.py:23
  24.2 18.9 %collective-permute-start = (bf16[64,256]{1,0:T(8,128)(2,1)}, bf16[64,256]{1,0:T(8,128)(2,1)S(1)}, u32[]{:S(2)}, u32[]{:S(2)}) collective-permute-start(bf16[64,256]{1,0:T(8,128)(2,1)} %param.17), channel_id=1, source_target_pairs={{0,8},{2,10},{4,12},{6,14},{8,16},{10,18},{12,20},{14,22},{16,24},... | collective-permute-start | bytes 98312 | tf_op jit(solution)/shard_map/ppermute | solution.py:23
  31.6 11.5 %collective-permute-start.1 = (bf16[64,256]{1,0:T(8,128)(2,1)}, bf16[64,256]{1,0:T(8,128)(2,1)S(1)}, u32[]{:S(2)}, u32[]{:S(2)}) collective-permute-start(bf16[64,256]{1,0:T(8,128)(2,1)} %param.17), channel_id=1, source_target_pairs={{0,6},{2,8},{4,10},{6,12},{8,14},{10,16},{12,18},{14,20},{16,22},{... | collective-permute-start | bytes 98312 | tf_op jit(solution)/shard_map/ppermute | solution.py:23
  35.7 7.6 %collective-permute-start.2 = (bf16[64,256]{1,0:T(8,128)(2,1)}, bf16[64,256]{1,0:T(8,128)(2,1)S(1)}, u32[]{:S(2)}, u32[]{:S(2)}) collective-permute-start(bf16[64,256]{1,0:T(8,128)(2,1)} %param.17), channel_id=1, source_target_pairs={{0,4},{2,6},{4,8},{6,10},{8,12},{10,14},{12,16},{14,18},{16,20},{1... | collective-permute-start | bytes 98312 | tf_op jit(solution)/shard_map/ppermute | solution.py:23
  40.1 6.0 %collective-permute-start.3 = (bf16[64,256]{1,0:T(8,128)(2,1)}, bf16[64,256]{1,0:T(8,128)(2,1)S(1)}, u32[]{:S(2)}, u32[]{:S(2)}) collective-permute-start(bf16[64,256]{1,0:T(8,128)(2,1)} %param.17), channel_id=1, source_target_pairs={{0,2},{2,4},{4,6},{6,8},{8,10},{10,12},{12,14},{14,16},{16,18},{18... | collective-permute-start | bytes 98312 | tf_op jit(solution)/shard_map/ppermute | solution.py:23
  134.1 2.3 copy-start.3
  134.1 2.9 copy-start.4
  134.1 12.4 %copy-start.1 = (bf16[32,1536]{1,0:T(8,128)(2,1)S(1)}, bf16[32,1536]{1,0:T(8,128)(2,1)}, u32[]{:S(2)}) copy-start(bf16[32,1536]{1,0:T(8,128)(2,1)} %param.20) | copy-start | bytes 294916
  134.1 13.4 %copy-start.5 = (f32[1536]{0:T(1024)S(1)}, f32[1536]{0:T(1024)}, u32[]{:S(2)}) copy-start(f32[1536]{0:T(1024)} %param.21) | copy-start | bytes 18436
  135.8 151.7 %all-gather.10.cloned.1.call-start = ((), (), s32[]{:S(2)}) async-start(), calls=%async_computation.7 | async-start | bytes 3158016 | tf_op jit(solution)/shard_map/all_gather | solution.py:105
  136.3 246.9 %all-gather.6.cloned.1.call-start = ((), (), s32[]{:S(2)}) async-start(), calls=%async_computation.5 | async-start | bytes 6316032 | tf_op jit(solution)/shard_map/all_gather | solution.py:104
  156.8 100.7 %copy-start.6 = (bf16[1,1536,2,256]{3,2,1,0:T(2,128)(2,1)S(1)}, bf16[1,1536,2,256]{3,2,1,0:T(2,128)(2,1)}, u32[]{:S(2)}) copy-start(bf16[1,1536,2,256]{3,2,1,0:T(2,128)(2,1)} %param.26) | copy-start | bytes 4718596
  248.3 27.2 %all-to-all-start.2 = ((bf16[1,128,8,2,128]{4,3,2,0,1:T(2,128)(2,1)}), bf16[1,128,8,2,128]{4,3,2,0,1:T(2,128)(2,1)S(1)}, u32[]{:S(2)}, u32[]{:S(2)}) async-start(bf16[1,128,8,2,128]{4,3,2,0,1:T(2,128)(2,1)} %bitcast.36), calls=%async_computation.3 | async-start | bytes 1048576 | tf_op jit(solution)/shard_map/all_to_all | solution.py:57
  264.6 19.6 %copy-start.2 = (f32[32,6]{0,1:T(8,128)S(1)}, f32[32,6]{0,1:T(8,128)}, u32[]{:S(2)}) copy-start(f32[32,6]{0,1:T(8,128)} %param.23) | copy-start | bytes 2308
  264.6 19.8 %copy-start.7 = (s32[128]{0:T(128)S(1)}, s32[128]{0:T(128)}, u32[]{:S(2)}) copy-start(s32[128]{0:T(128)} %param.29) | copy-start | bytes 1540
  275.5 113.2 %all-to-all-start.1 = ((bf16[128,1,6,1536]{3,2,1,0:T(8,128)(2,1)}), bf16[128,1,6,1536]{3,2,1,0:T(8,128)(2,1)}, u32[]{:S(2)}, u32[]{:S(2)}) async-start(bf16[128,1,6,1536]{3,2,1,0:T(8,128)(2,1)} %copy.68), calls=%async_computation.2 | async-start | bytes 6291456 | tf_op jit(solution)/shard_map/all_to_all | solution.py:133
Sparse Core Ops, SparseCore 0:
  12.5 117.8 all-gather.7
  135.9 10.5 reduce-scatter.1
Sparse Core Ops, SparseCore 1:
  140.6 117.3 all-gather.9
  262.9 120.3 all-gather.5
where the time goes:
time: 412 us; the launch traced here: 409 us
  waiting for transfers between devices  195 us (47%)
  blocking collectives  91.5 us (22%)
  starting transfers between devices  48.8 us (12%)
  local copies, waits for them, and re-layouts  31.2 us (8%)
  between operations  16 us (4%)
  matrix products  15.2 us (4%)
  other arithmetic  11.1 us (3%)
    all_to_all x1, blocking collectives, shards(): lax.all_to_all(outgoing, 'seq', split_axis=0, concat_axis=0, tiled=True)  91.5 us
    all_gather x1, waiting for transfers between devices, shards(): lax.all_gather(shared_gate_up, ('seq', 'head'), axis=2, tiled=True)  89.9 us
    all_gather x1, waiting for transfers between devices, shards(): lax.all_gather(out_weight, 'seq', axis=1, tiled=True)  82.4 us
    ppermute x8, starting transfers between devices, from_behind(): return lax.ppermute(shard, axis, pairs)  31.1 us
    all_to_all x1, waiting for transfers between devices, shards(): lax.all_to_all(cache_blocks, 'seq', split_axis=1, concat_axis=0, tiled=True)  10.9 us
    unnamed x28, local copies, waits for them, and re-layouts  10.3 us
    all_to_all x1, starting transfers between devices, shards(): lax.all_to_all(cache_blocks, 'seq', split_axis=1, concat_axis=0, tiled=True)  9.21 us
    all_to_all x1, starting transfers between devices, shards(): lax.all_to_all(half_out, 'seq', split_axis=0, concat_axis=0, tiled=True)  8.31 us
  transfers between devices with their start and end apart: 14, of which 6 were waited for; matrix products, arithmetic and copies ran while one was open for 10% of the time, Pallas kernels for 0%

commit v1 on v0

v1 whole, which is shorter than its diff:
```python
import functools
import math

import jax
import jax.numpy as jnp
from jax import lax
from jax.experimental import pallas as pl
from jax.experimental.pallas import tpu as pltpu
from jax.sharding import PartitionSpec as P

MESH = pl.DeviceIdType.MESH
HD = 128
NY, NZ, NX = 4, 8, 4
TOP = 6
CAP = 6
EXPERTS = 64
NEGATIVE = -1e30
EPSILON = 1e-05
F32 = jnp.float32
BF16 = jnp.bfloat16
ZORDER = (1, 7, 2, 6, 3, 5, 4)
NT = (((1,), (1,)), ((), ()))


def place():
    s = lax.axis_index("seq")
    h = lax.axis_index("head")
    y = lax.div(s, NZ * NX)
    z = lax.rem(lax.div(s, NX), NZ)
    x = lax.rem(s, NX)
    return s, h, y, z, x


def seq_of(y, z, x):
    return y * (NZ * NX) + z * NX + x


def up(i, by, n):
    return lax.rem(i + by, n)


def rcopy(src, dst, ssem, rsem, dev):
    return pltpu.make_async_remote_copy(
        src_ref=src, dst_ref=dst, send_sem=ssem, recv_sem=rsem, device_id=dev, device_id_type=MESH
    )


def greet(peers):
    barrier = pltpu.get_barrier_semaphore()
    for dev in peers:
        pl.semaphore_signal(barrier, inc=1, device_id=dev, device_id_type=MESH)
    pl.semaphore_wait(barrier, len(peers))


def iota(shape, axis):
    return lax.broadcasted_iota(jnp.int32, shape, axis)


def silu(v):
    return v / (1.0 + jnp.exp(-v))


def routing_table(ids, logits):
    tok = ids.shape[0]
    lane = iota((tok, 128), 1)
    top = jnp.max(logits, axis=-1, keepdims=True)
    e = jnp.exp(logits - top)
    probs = e / jnp.sum(e, axis=-1, keepdims=True)
    named = jnp.zeros((tok, 128), F32)
    weight = jnp.zeros((tok, 128), F32)
    for r in range(TOP):
        idr = ids[:, r : r + 1]
        named = named + jnp.where(lane == idr, 1.0, 0.0)
        weight = weight + jnp.where(lane - EXPERTS == idr, probs[:, r : r + 1], 0.0)
    before = jnp.where(iota((tok, tok), 1) < iota((tok, tok), 0), 1.0, 0.0)
    rank = jnp.dot(before.astype(BF16), named.astype(BF16), preferred_element_type=F32)
    return jnp.where(lane < EXPERTS, jnp.where(named > 0.5, rank, -1.0), weight)


def front_kernel(
    q_ref, k_ref, v_ref, len_ref, ow_ref, res_ref, gain_ref, ids_ref, log_ref,
    sh_ref, wg_ref, wd_ref, cache_ref,
    mixed_ref, xall_ref, rpall_ref, shall_ref, wgo_ref, wdo_ref, cmid_ref, chand_ref,
    kwin, vwin, owbuf, wc, hbuf, part, rbuf, nbuf, rpbuf,
    kv_s, kv_r, owz_s, owz_r, owx_s, owx_r, rp_s, rp_r, sh_s, sh_r, cz_s, cz_r, cp_s, cp_r,
    ex_s, ex_r, sib_s, sib_r, hy_s, hy_r, rs_s, rs_r, xz_s, xz_r, loc,
):
    s, h, y, z, x = place()
    seqs = NY * NZ * NX
    zdev = [(seq_of(y, up(z, d, NZ), x), h) for d in ZORDER]
    plane = [
        (dy, dx) for dy in range(NY) for dx in range(NX) if (dy, dx) != (0, 0)
    ]
    pdev = [(seq_of(up(y, dy, NY), z, up(x, dx, NX)), h) for dy, dx in plane]
    sib = (s, 1 - h)
    cross = [(seq_of(up(y, dy, NY), z, x), 1 - h) for dy in (1, 2, 3)]
    ahead = [(lax.rem(s + by, seqs), h) for by in range(1, 5)]
    behind = [(lax.rem(s + seqs - by, seqs), h) for by in range(1, 5)]
    greet(zdev + pdev + [sib] + cross + ahead + behind)

    pending = []

    def go(copy):
        copy.start()
        pending.append(copy)
        return copy

    kv = []
    for by in range(1, 5):
        rows = pl.ds(64 * (4 - by), 64)
        kv.append(go(rcopy(k_ref, kwin.at[rows], kv_s.at[0, by - 1], kv_r.at[0, by - 1], ahead[by - 1])))
        kv.append(go(rcopy(v_ref, vwin.at[rows], kv_s.at[1, by - 1], kv_r.at[1, by - 1], ahead[by - 1])))
    own = [
        pltpu.make_async_copy(k_ref, kwin.at[pl.ds(256, 64)], loc.at[0]),
        pltpu.make_async_copy(v_ref, vwin.at[pl.ds(256, 64)], loc.at[1]),
        pltpu.make_async_copy(ow_ref, owbuf.at[z, x], loc.at[2]),
        pltpu.make_async_copy(sh_ref, shall_ref.at[y, x, h], loc.at[3]),
        pltpu.make_async_copy(cache_ref.at[:, z], cmid_ref.at[z], loc.at[4]),
    ]
    for c in own:
        c.start()
    owz = [
        go(rcopy(ow_ref, owbuf.at[z, x], owz_s.at[i], owz_r.at[i], zdev[i])) for i in range(7)
    ]
    pair = (seq_of(up(y, 2, NY), z, x), h)
    rows_g, rows_d = pl.ds(h * 768, 768), pl.ds(h * 128, 128)
    ex = [
        go(rcopy(wg_ref.at[rows_g], wgo_ref.at[rows_g], ex_s.at[0], ex_r.at[0], pair)),
        go(rcopy(wd_ref.at[rows_d], wdo_ref.at[rows_d], ex_s.at[1], ex_r.at[1], pair)),
    ]
    shp = [
        go(rcopy(sh_ref, shall_ref.at[y, x, h], sh_s.at[i], sh_r.at[i], pdev[i])) for i in range(15)
    ]
    cz = [
        go(rcopy(cache_ref.at[:, up(z, d, NZ)], cmid_ref.at[z], cz_s.at[i], cz_r.at[i], zdev[i]))
        for i, d in enumerate(ZORDER)
    ]

    rpbuf[...] = routing_table(ids_ref[...], log_ref[...])
    rp = [go(rcopy(rpbuf, rpall_ref.at[z], rp_s.at[i], rp_r.at[i], zdev[i])) for i in range(7)]
    rp_own = pltpu.make_async_copy(rpbuf, rpall_ref.at[z], loc.at[5])
    rp_own.start()

    upper = jnp.where(iota((128, 128), 0) <= iota((128, 128), 1), 1.0, 0.0).astype(BF16)
    lens = jnp.broadcast_to(len_ref[...], (16, 128)).astype(BF16)
    ends = jnp.dot(lens, upper, preferred_element_type=F32)[0:1, :]
    qpos = (s * 64 + iota((64, 128), 0)).astype(F32)
    first = jnp.max(jnp.where(ends <= qpos, ends, 0.0), axis=-1, keepdims=True)
    kpos = (s * 64 - 256 + iota((64, 320), 1)).astype(F32)
    qcol = (s * 64 + iota((64, 320), 0)).astype(F32)
    seen = jnp.where((kpos >= first) & (kpos <= qcol), 0.0, NEGATIVE)
    seen3 = jnp.concatenate([seen, seen, seen], axis=0)

    own[2].wait()
    for c in owz:
        c.wait_recv()
    owx = []
    for d in (1, 3, 2):
        dev = (seq_of(y, z, up(x, d, NX)), h)
        owx.append(go(rcopy(owbuf.at[:, x], owbuf.at[:, x], owx_s.at[d - 1], owx_r.at[d - 1], dev)))

    own[0].wait()
    own[1].wait()
    for c in kv:
        c.wait_recv()
    for g in range(2):
        cols = slice(g * HD, (g + 1) * HD)
        qs = jnp.concatenate(
            [q_ref[:, (3 * g + i) * HD : (3 * g + i + 1) * HD] for i in range(3)], axis=0
        )
        sc = lax.dot_general(qs, kwin[:, cols], NT, preferred_element_type=F32)
        sc = jnp.where(seen3 < -1.0, NEGATIVE, sc * (1.0 / math.sqrt(HD)))
        w = jnp.exp(sc - jnp.max(sc, axis=-1, keepdims=True))
        total = jnp.sum(w, axis=-1, keepdims=True)
        o = jnp.dot(w.astype(BF16), vwin[:, cols], preferred_element_type=F32)
        o = (o / total).astype(BF16)
        for i in range(3):
            hbuf[y, :, (3 * g + i) * HD : (3 * g + i + 1) * HD] = o[i * 64 : (i + 1) * 64]

    hy = []
    for d in (1, 3, 2):
        dev = (seq_of(up(y, d, NY), z, x), h)
        hy.append(go(rcopy(hbuf.at[y], hbuf.at[y], hy_s.at[d - 1], hy_r.at[d - 1], dev)))

    own[4].wait()
    for c in cz:
        c.wait_recv()
    cp = []
    for i, (dy, dx) in enumerate(plane):
        src = cmid_ref.at[:, up(y, dy, NY), up(x, dx, NX)]
        cp.append(go(rcopy(src, chand_ref.at[y, :, x], cp_s.at[i], cp_r.at[i], pdev[i])))
    cp_own = pltpu.make_async_copy(cmid_ref.at[:, y, x], chand_ref.at[y, :, x], loc.at[6])
    cp_own.start()

    for c in owx:
        c.wait_recv()
    col, row = iota((384, 512), 0), iota((384, 512), 1)
    pick = jnp.where(row == lax.div(col, 12) * 16 + lax.rem(col, 12), 1.0, 0.0).astype(BF16)
    wc[...] = jnp.dot(pick, owbuf[...].reshape(512, 768), preferred_element_type=F32).astype(BF16)

    for c in hy:
        c.wait_recv()
    po = lax.dot_general(hbuf[...].reshape(256, 768), wc[...], NT, preferred_element_type=F32)
    part[...] = po.reshape(4, 2, 32, 384)
    rs = []
    for d in (1, 3, 2):
        yd = up(y, d, NY)
        for i, hd in enumerate((h, 1 - h)):
            rs.append(
                go(rcopy(part.at[yd, hd], rbuf.at[y, h], rs_s.at[i, d], rs_r.at[i, d], (seq_of(yd, z, x), hd)))
            )
    rs.append(go(rcopy(part.at[y, 1 - h], rbuf.at[y, h], rs_s.at[1, 0], rs_r.at[1, 0], sib)))
    rbuf[y, h] = part[y, h]
    for c in rs:
        c.wait_recv()
    attn = [rbuf[j, 0] + rbuf[j, 1] for j in range(NY)]
    mixed = res_ref[...].astype(F32) + jnp.concatenate(attn, axis=1)
    mixed_ref[...] = mixed
    ms = jnp.mean(mixed * mixed, axis=-1, keepdims=True)
    nbuf[...] = (mixed * lax.rsqrt(ms + EPSILON) * gain_ref[...]).astype(BF16)
    xz = [go(rcopy(nbuf, xall_ref.at[z], xz_s.at[i], xz_r.at[i], zdev[i])) for i in range(7)]
    x_own = pltpu.make_async_copy(nbuf, xall_ref.at[z], loc.at[7])
    x_own.start()

    own[3].wait()
    for c in shp:
        c.wait_recv()
    last = [go(rcopy(shall_ref.at[:, :, h], shall_ref.at[:, :, h], sib_s.at[0], sib_r.at[0], sib))]
    for c in ex:
        c.wait_recv()
    last.append(go(rcopy(wgo_ref.at[rows_g], wgo_ref.at[rows_g], sib_s.at[1], sib_r.at[1], sib)))
    last.append(go(rcopy(wdo_ref.at[rows_d], wdo_ref.at[rows_d], sib_s.at[2], sib_r.at[2], sib)))
    rp_own.wait()
    cp_own.wait()
    x_own.wait()
    for c in rp + cp + xz + last:
        c.wait_recv()
    for c in pending:
        c.wait_send()


def moe_kernel(
    x_hbm, rp_ref, sh_hbm, wg_hbm, wd_hbm, wgo_hbm, wdo_hbm, mixed_ref,
    out_ref,
    xb, shb, wgb, wdb, dsend, drecv, rsend, rrecv, pz, racc,
    d_s, d_r, r_s, r_r, z_s, z_r, loc,
):
    s, h, y, z, x = place()
    copies = [
        pltpu.make_async_copy(x_hbm, xb, loc.at[0]),
        pltpu.make_async_copy(sh_hbm, shb, loc.at[1]),
        pltpu.make_async_copy(wg_hbm, wgb.at[0], loc.at[2]),
        pltpu.make_async_copy(wgo_hbm, wgb.at[1], loc.at[3]),
        pltpu.make_async_copy(wd_hbm, wdb.at[0], loc.at[4]),
        pltpu.make_async_copy(wdo_hbm, wdb.at[1], loc.at[5]),
    ]
    for c in copies:
        c.start()
    zdev = [(seq_of(y, up(z, d, NZ), x), h) for d in ZORDER]
    hops = [(p, d) for p in range(2) for d in range(NX) if (p, d) != (0, 0)]
    dests = [(seq_of(up(y, p, NY), z, up(x, d, NX)), h) for p, d in hops]
    sources = [(seq_of(up(y, NY - p, NY), z, up(x, NX - d, NX)), h) for p, d in hops]
    greet(zdev + dests + sources)

    cols = 8 * 48
    lane = iota((128, cols), 1)
    half = lax.div(lane, 192)
    expert = lax.rem(y + half, 2) * 32 + z * NX + lax.rem(lax.div(lane, 48), NX)
    row = iota((128, cols), 0)
    rp = rp_ref[...].reshape(256, 128).astype(BF16)
    rank = jnp.dot(rp, jnp.where(row == expert, 1.0, 0.0).astype(BF16), preferred_element_type=F32)
    prob = jnp.dot(
        rp, jnp.where(row == expert + EXPERTS, 1.0, 0.0).astype(BF16), preferred_element_type=F32
    )
    tok = iota((256, cols), 0)
    slot = lax.rem(iota((256, cols), 1), 48)
    hit = (lax.div(tok, 32) == lax.div(slot, CAP)) & (rank == lax.rem(slot, CAP).astype(F32))
    pick = jnp.transpose(jnp.where(hit, 1.0, 0.0)).astype(BF16)
    weight = jnp.where(hit, prob, 0.0).astype(BF16)
    copies[0].wait()
    xs = xb[...].reshape(256, 1536)
    dsend[...] = (
        jnp.dot(pick, xs, preferred_element_type=F32).astype(BF16).reshape(8, 48, 1536)
    )
    pending = []

    def go(copy):
        copy.start()
        pending.append(copy)
        return copy

    sent = []
    for i, (p, d) in enumerate(hops):
        sent.append(
            go(rcopy(dsend.at[p * NX + up(x, d, NX)], drecv.at[p * NX + x], d_s.at[i], d_r.at[i], dests[i]))
        )
    drecv[x] = dsend[x]

    copies[1].wait()
    sh = shb[...].reshape(512, 1536)
    both = lax.dot_general(xs, sh, NT, preferred_element_type=F32)
    act = silu(pltpu.roll(both, 8, 1)) * pltpu.roll(both, 4, 1)
    live = lax.rem(lax.div(iota((256, 512), 1), 4), 4) == 2
    act = jnp.where(live, act, 0.0).astype(BF16)
    shared = jnp.dot(act, sh, preferred_element_type=F32)

    for c in copies[2:]:
        c.wait()
    for c in sent:
        c.wait_recv()
    rows = drecv[...].reshape(cols, 1536)
    acc = None
    for j in range(2):
        gu = jnp.dot(rows, wgb[j], preferred_element_type=F32)
        a = (silu(gu[:, :256]) * gu[:, 256:]).astype(BF16)
        o = jnp.dot(a, wdb[j], preferred_element_type=F32)
        acc = o if acc is None else acc + o
    rsend[...] = acc.astype(BF16).reshape(8, 48, 1536)
    back = []
    for i, (p, d) in enumerate(hops):
        src = rsend.at[p * NX + up(x, NX - d, NX)]
        back.append(go(rcopy(src, rrecv.at[p * NX + x], r_s.at[i], r_r.at[i], sources[i])))
    rrecv[x] = rsend[x]
    for c in back:
        c.wait_recv()
    tot = shared + jnp.dot(weight, rrecv[...].reshape(cols, 1536), preferred_element_type=F32)
    pz[...] = tot.astype(BF16).reshape(8, 32, 1536)
    red = [
        go(rcopy(pz.at[up(z, d, NZ)], racc.at[z], z_s.at[i], z_r.at[i], zdev[i]))
        for i, d in enumerate(ZORDER)
    ]
    racc[z] = pz[z]
    for c in red:
        c.wait_recv()
    out = mixed_ref[...]
    for j in range(NZ):
        out = out + racc[j].astype(F32)
    out_ref[...] = out.astype(BF16)
    for c in pending:
        c.wait_send()


def shards(
    queries, key_vectors, value_vectors, lengths, out_weight, residual, norm_gain, route_ids,
    route_logits, shared_gate_up, shared_down, expert_gate_up, expert_down, cache_blocks, block_table,
):
    any_, vmem = pl.BlockSpec(memory_space=pl.ANY), pl.BlockSpec(memory_space=pltpu.VMEM)
    dma = pltpu.SemaphoreType.DMA
    lens = jnp.pad(lengths.astype(F32), (0, 64)).reshape(1, 128)
    ow = jnp.pad(out_weight.T, ((0, 4), (0, 0)))
    sh = jnp.concatenate(
        [
            jnp.transpose(shared_gate_up, (1, 2, 0)).reshape(8, 1536),
            shared_down,
            jnp.zeros((4, 1536), BF16),
        ],
        axis=0,
    )
    wg = expert_gate_up.reshape(1536, 512)
    wd = expert_down.reshape(256, 1536)
    cache = cache_blocks.reshape(NY, NZ, NX, 8, 2, HD)
    sds = jax.ShapeDtypeStruct
    mixed, xall, rpall, shall, wgo, wdo, _, chand = pl.pallas_call(
        front_kernel,
        out_shape=(
            sds((32, 1536), F32),
            sds((NZ, 32, 1536), BF16),
            sds((NZ, 32, 128), F32),
            sds((NY, NX, 2, 16, 1536), BF16),
            sds((1536, 512), BF16),
            sds((256, 1536), BF16),
            sds((NZ, NY, NX, 8, 2, HD), BF16),
            sds((NY, NZ, NX, 8, 2, HD), BF16),
        ),
        in_specs=[vmem, any_, any_, vmem, any_, vmem, vmem, vmem, vmem, any_, any_, any_, any_],
        out_specs=(vmem, any_, any_, any_, any_, any_, any_, any_),
        scratch_shapes=[
            pltpu.VMEM((320, 256), BF16),
            pltpu.VMEM((320, 256), BF16),
            pltpu.VMEM((NZ, NX, 16, 768), BF16),
            pltpu.VMEM((384, 768), BF16),
            pltpu.VMEM((NY, 64, 768), BF16),
            pltpu.VMEM((NY, 2, 32, 384), F32),
            pltpu.VMEM((NY, 2, 32, 384), F32),
            pltpu.VMEM((32, 1536), BF16),
            pltpu.VMEM((32, 128), F32),
            dma((2, 4)), dma((2, 4)),
            dma((7,)), dma((7,)),
            dma((3,)), dma((3,)),
            dma((7,)), dma((7,)),
            dma((15,)), dma((15,)),
            dma((7,)), dma((7,)),
            dma((15,)), dma((15,)),
            dma((2,)), dma((2,)),
            dma((3,)), dma((3,)),
            dma((3,)), dma((3,)),
            dma((2, 4)), dma((2, 4)),
            dma((7,)), dma((7,)),
            dma((8,)),
        ],
        compiler_params=pltpu.CompilerParams(
            collective_id=0, has_side_effects=True, vmem_limit_bytes=40 << 20
        ),
        name="front",
    )(
        queries, key_vectors, value_vectors, lens, ow, residual, norm_gain.reshape(1, 1536),
        route_ids, route_logits, sh, wg, wd, cache,
    )
    cache_out = jnp.take(chand.reshape(128, 1, 8, 2, HD), block_table, axis=0)
    layer_out = pl.pallas_call(
        moe_kernel,
        out_shape=sds((32, 1536), BF16),
        in_specs=[any_, vmem, any_, any_, any_, any_, any_, vmem],
        out_specs=vmem,
        scratch_shapes=[
            pltpu.VMEM((NZ, 32, 1536), BF16),
            pltpu.VMEM((NY, NX, 2, 16, 1536), BF16),
            pltpu.VMEM((2, 1536, 512), BF16),
            pltpu.VMEM((2, 256, 1536), BF16),
            pltpu.VMEM((8, 48, 1536), BF16),
            pltpu.VMEM((8, 48, 1536), BF16),
            pltpu.VMEM((8, 48, 1536), BF16),
            pltpu.VMEM((8, 48, 1536), BF16),
            pltpu.VMEM((NZ, 32, 1536), BF16),
            pltpu.VMEM((NZ, 32, 1536), BF16),
            dma((7,)), dma((7,)),
            dma((7,)), dma((7,)),
            dma((7,)), dma((7,)),
            dma((6,)),
        ],
        compiler_params=pltpu.CompilerParams(
            collective_id=1, has_side_effects=True, vmem_limit_bytes=50 << 20
        ),
        name="moe",
    )(xall, rpall, shall, wg, wd, wgo, wdo, mixed)
    return layer_out, cache_out


def solution(mesh):
    in_specs = (
        P("seq", "head"),
        P("seq", "head"),
        P("seq", "head"),
        P(),
        P("head", "seq"),
        P(("seq", "head"), None),
        P(),
        P(("seq", "head"), None),
        P(("seq", "head"), None),
        P(None, None, ("seq", "head")),
        P(("seq", "head"), None),
        P("seq", None, None, None),
        P("seq", None, None),
        P("seq", None, None, "head", None),
        P(),
    )
    out_specs = (P(("seq", "head"), None), P(None, "seq", None, "head", None))
    return jax.shard_map(shards, mesh=mesh, in_specs=in_specs, out_specs=out_specs, check_vma=False)
```

time: 412 us -> 159 us (0.39)
  the two profiles are of different devices: /device:TPU:4 before, /device:TPU:24 now
where the time goes in v1:
time: 159 us
  Pallas kernels  147 us (92%)
  local copies, waits for them, and re-layouts  9.32 us (6%)
    pallas_call x1, Pallas kernels, shards(): pl.pallas_call(front_kernel, out_shape=(sds((32, 1536), F32), sds((NZ, 32...  82 us
    pallas_call x1, Pallas kernels, shards(): pl.pallas_call(moe_kernel, out_shape=sds((32, 1536), BF16), in_specs=[any...  64.8 us
    unnamed x38, local copies, waits for them, and re-layouts  7.58 us

profile of v1, /device:TPU:24, one launch (start us, length us, event | category | flops | bytes accessed | tf_op | source)
XLA Modules:
  0.0 158.6 jit_solution(886009405126291935)
XLA Ops:
  0.6 0.0 copy-start.9
  0.6 0.0 copy-start.11
  0.7 0.0 copy-start.10
  0.7 0.0 copy-start.13
  0.7 0.0 copy-start.14
  0.7 0.0 copy-start.12
  0.7 0.0 copy-start.15
  0.7 0.0 copy-start.1
  0.7 1.8 %copy.19 = bf16[192,8,2,256]{3,1,2,0:T(8,128)(2,1)S(1)} copy(bf16[192,8,2,256]{3,2,1,0:T(2,128)(2,1)} %bitcast.18) | data formatting | bytes 3145728
  2.6 0.1 pad.12.clone
  2.7 0.1 maximum_maximum_fusion.sh_ref
  2.8 0.1 copy.17.ids_ref
  2.9 0.1 copy.18.log_ref
  3.1 0.0 copy-start.5
  3.1 0.9 copy-done.5
  4.0 0.9 copy-done.6
  4.9 0.8 copy-done.8
  5.7 82.0 %front.1 = (f32[32,1536]{1,0:T(8,128)S(1)}, bf16[8,32,1536]{2,1,0:T(8,128)(2,1)S(1)}, f32[8,32,128]{2,1,0:T(8,128)S(1)}, bf16[4,4,2,16,1536]{4,3,2,1,0:T(8,128)(...) custom-call(bf16[64,768]{1,0:T(8,128)(2,1)S(1)} %copy-done.5, ...), custom_call_target="tpu_custom_call" | custom-call | tf_op jit(solution)/shard_map/front/pallas_call | solution.py:363
  87.7 1.1 copy-done.2
  88.9 1.2 copy-done.3
  90.0 64.8 %moe.1 = bf16[32,1536]{1,0:T(8,128)(2,1)S(1)} custom-call(bf16[8,32,1536]{2,1,0:T(8,128)(2,1)S(1)} %get-tuple-element.9.x_hbm, f32[8,32,128]{2,1,0:T(8,128)S(1)} %get-tuple-element.10.rp_ref, bf16[4,4,2,16,1536]{4,3,2,1,0:T(8,128)(2,1)} %copy-done.2, bf16[1536,512]{1,0:T(8,128)(2,1)} %bitcast.13, bf16[256,1536]{1,0:T(8,128)(2,1)S(1)} %bitcast.15, ...), custom_call_target="tpu_custom_call" | custom-call | tf_op jit(solution)/shard_map/moe/pallas_call | solution.py:410
  154.9 1.6 %gather_fusion = bf16[128,8,2,128]{3,2,1,0:T(2,128)(2,1)S(1)} fusion(bf16[128,8,2,128]{3,2,1,0:T(2,128)(2,1)S(1)} %bitcast.16, s32[1024]{0:T(1024)S(1)} %pad_clamp_fusion), kind=kCustom, calls=%fused_computation | custom fusion | bytes 1049088 | tf_op jit(solution)/shard_map/jit(_take)/gather | solution.py:409
  156.6 1.4 broadcast_select_fusion
  157.9 0.6 copy.21
  (29 shorter events, 0.1 us)
Async XLA Ops:
  0.6 2.0 %copy-start.9 = (bf16[1536,2,4]{0,2,1:T(4,128)(2,1)S(1)}, bf16[1536,2,4]{0,2,1:T(4,128)(2,1)}, u32[]{:S(2)}) copy-start(bf16[1536,2,4]{0,2,1:T(4,128)(2,1)} %param.24) | copy-start | bytes 73732
  0.6 2.1 %copy-start.11 = (bf16[4,1536]{1,0:T(4,128)(2,1)S(1)}, bf16[4,1536]{1,0:T(4,128)(2,1)}, u32[]{:S(2)}) copy-start(bf16[4,1536]{1,0:T(4,128)(2,1)} %param.25) | copy-start | bytes 36868
  0.7 2.1 %copy-start.10 = (bf16[768,12]{0,1:T(8,128)(2,1)S(1)}, bf16[768,12]{0,1:T(8,128)(2,1)}, u32[]{:S(2)}) copy-start(bf16[768,12]{0,1:T(8,128)(2,1)} %param.19) | copy-start | bytes 55300
  0.7 2.1 %copy-start.13 = (s32[32,6]{0,1:T(8,128)S(1)}, s32[32,6]{0,1:T(8,128)}, u32[]{:S(2)}) copy-start(s32[32,6]{0,1:T(8,128)} %param.22) | copy-start | bytes 2308
  0.7 2.2 %copy-start.14 = (f32[32,6]{0,1:T(8,128)S(1)}, f32[32,6]{0,1:T(8,128)}, u32[]{:S(2)}) copy-start(f32[32,6]{0,1:T(8,128)} %param.23) | copy-start | bytes 2308
  0.7 2.3 %copy-start.12 = (f32[1536]{0:T(1024)S(1)}, f32[1536]{0:T(1024)}, u32[]{:S(2)}) copy-start(f32[1536]{0:T(1024)} %param.21) | copy-start | bytes 18436
  0.7 2.3 %copy-start.15 = (s32[64]{0:T(128)S(1)}, s32[64]{0:T(128)}, u32[]{:S(2)}) copy-start(s32[64]{0:T(128)} %param.18) | copy-start | bytes 772
  0.7 2.3 %copy-start.1 = (bf16[1,256,1536]{2,1,0:T(8,128)(2,1)S(1)}, bf16[1,256,1536]{2,1,0:T(8,128)(2,1)}, u32[]{:S(2)}) copy-start(bf16[1,256,1536]{2,1,0:T(8,128)(2,1)} %param.27) | copy-start | bytes 2359300
  0.7 2.3 %copy-start.4 = (bf16[1,128,8,2,128]{4,3,2,1,0:T(2,128)(2,1)S(1)}, bf16[1,128,8,2,128]{4,3,2,1,0:T(2,128)(2,1)}, u32[]{:S(2)}) copy-start(bf16[1,128,8,2,128]{4,3,2,1,0:T(2,128)(2,1)} %param.28) | copy-start | bytes 1572868
  0.7 2.3 %copy-start.7 = (bf16[64,256]{1,0:T(8,128)(2,1)S(1)}, bf16[64,256]{1,0:T(8,128)(2,1)}, u32[]{:S(2)}) copy-start(bf16[64,256]{1,0:T(8,128)(2,1)} %k_ref.1) | copy-start | bytes 98308
  2.6 85.1 %copy-start = (bf16[192,8,2,256]{3,1,2,0:T(8,128)(2,1)}, bf16[192,8,2,256]{3,1,2,0:T(8,128)(2,1)S(1)}, u32[]{:S(2)}) copy-start(bf16[192,8,2,256]{3,1,2,0:T(8,128)(2,1)S(1)} %copy.19) | copy-start | bytes 4718596
  3.1 0.9 copy-start.5
  4.0 0.9 copy-start.6
  4.9 0.8 copy-start.8
  87.7 1.1 copy-start.2
  88.9 1.2 copy-start.3
  90.0 64.8 %copy-start.16 = (s32[128]{0:T(128)S(1)}, s32[128]{0:T(128)}, u32[]{:S(2)}) copy-start(s32[128]{0:T(128)} %param.29) | copy-start | bytes 1540

commit v2 on v0

v2 whole, which is shorter than its diff:
```python
import functools
import math

import jax
import jax.numpy as jnp
from jax import lax
from jax.experimental import pallas as pl
from jax.experimental.pallas import tpu as pltpu
from jax.sharding import PartitionSpec as P

MESH = pl.DeviceIdType.MESH
HD = 128
NY, NZ, NX = 4, 8, 4
TOP = 6
CAP = 6
EXPERTS = 64
NEGATIVE = -1e30
EPSILON = 1e-05
F32 = jnp.float32
BF16 = jnp.bfloat16
ZORDER = (1, 7, 2, 6, 3, 5, 4)
OFF = (0, 1, 4, 3, 7, 6, 2, 5)
SLOT = {o: k for k, o in enumerate(OFF)}
ROWS = 24
COLS = 8 * ROWS
NT = (((1,), (1,)), ((), ()))


def place():
    s = lax.axis_index("seq")
    h = lax.axis_index("head")
    y = lax.div(s, NZ * NX)
    z = lax.rem(lax.div(s, NX), NZ)
    x = lax.rem(s, NX)
    return s, h, y, z, x


def seq_of(y, z, x):
    return y * (NZ * NX) + z * NX + x


def up(i, by, n):
    return lax.rem(i + by, n)


def rcopy(src, dst, ssem, rsem, dev):
    return pltpu.make_async_remote_copy(
        src_ref=src, dst_ref=dst, send_sem=ssem, recv_sem=rsem, device_id=dev, device_id_type=MESH
    )


def greet(peers):
    barrier = pltpu.get_barrier_semaphore()
    for dev in peers:
        pl.semaphore_signal(barrier, inc=1, device_id=dev, device_id_type=MESH)
    pl.semaphore_wait(barrier, len(peers))


def iota(shape, axis):
    return lax.broadcasted_iota(jnp.int32, shape, axis)


def silu(v):
    return v / (1.0 + jnp.exp(-v))


def routing_table(ids, logits):
    tok = ids.shape[0]
    lane = iota((tok, 128), 1)
    top = jnp.max(logits, axis=-1, keepdims=True)
    e = jnp.exp(logits - top)
    probs = e / jnp.sum(e, axis=-1, keepdims=True)
    named = jnp.zeros((tok, 128), F32)
    weight = jnp.zeros((tok, 128), F32)
    for r in range(TOP):
        idr = ids[:, r : r + 1]
        named = named + jnp.where(lane == idr, 1.0, 0.0)
        weight = weight + jnp.where(lane - EXPERTS == idr, probs[:, r : r + 1], 0.0)
    before = jnp.where(iota((tok, tok), 1) < iota((tok, tok), 0), 1.0, 0.0)
    rank = jnp.dot(before.astype(BF16), named.astype(BF16), preferred_element_type=F32)
    return jnp.where(lane < EXPERTS, jnp.where(named > 0.5, rank, -1.0), weight)


def layer_kernel(
    q_hbm, k_hbm, v_hbm, len_ref, ow_hbm, res_hbm, gain_ref, ids_ref, log_ref,
    sh_hbm, wg_hbm, wd_hbm, cache_hbm,
    out_ref, cmid_ref, chand_ref,
    qbuf, kwin, vwin, resbuf, owbuf, wc, hbuf, part, rbuf, xb, rpb, shb, wgb, wdb,
    dsend, drecv, rsend, rrecv, pz, racc,
    kv_s, kv_r, owz_s, owz_r, owx_s, owx_r, rp_s, rp_r, sh_s, sh_r, cz_s, cz_r, cp_s, cp_r,
    ex_s, ex_r, sib_s, sib_r, hy_s, hy_r, rs_s, rs_r, xz_s, xz_r, d_s, d_r, r_s, r_r, z_s, z_r, loc,
):
    s, h, y, z, x = place()
    seqs = NY * NZ * NX
    zdev = {d: (seq_of(y, up(z, d, NZ), x), h) for d in range(1, NZ)}
    plane = [
        (dy, dx) for dy in range(NY) for dx in range(NX) if (dy, dx) != (0, 0)
    ]
    pdev = {at: (seq_of(up(y, at[0], NY), z, up(x, at[1], NX)), h) for at in plane}
    sib = (s, 1 - h)
    cross = [(seq_of(up(y, dy, NY), z, x), 1 - h) for dy in (1, 2, 3)]
    ahead = [(lax.rem(s + by, seqs), h) for by in range(1, 5)]
    behind = [(lax.rem(s + seqs - by, seqs), h) for by in range(1, 5)]

    local = []

    def here(src, dst):
        copy = pltpu.make_async_copy(src, dst, loc.at[len(local)])
        copy.start()
        local.append(copy)
        return copy

    own_k = here(k_hbm, kwin.at[pl.ds(256, 64)])
    own_v = here(v_hbm, vwin.at[pl.ds(256, 64)])
    own_q = here(q_hbm, qbuf)
    own_ow = here(ow_hbm, owbuf.at[z, x])
    own_cache = here(cache_hbm.at[:, z], cmid_ref.at[z])
    own_res = here(res_hbm, resbuf)
    own_sh = here(sh_hbm, shb.at[y, x, h])
    own_wg = here(wg_hbm, wgb.at[0])
    own_wd = here(wd_hbm, wdb.at[0])
    greet(list(zdev.values()) + list(pdev.values()) + [sib] + cross + ahead + behind)

    pending = []

    def go(*args):
        copy = rcopy(*args)
        copy.start()
        pending.append(copy)
        return copy

    kv = []
    for by in range(1, 5):
        rows = pl.ds(64 * (4 - by), 64)
        kv.append(go(k_hbm, kwin.at[rows], kv_s.at[0, by - 1], kv_r.at[0, by - 1], ahead[by - 1]))
        kv.append(go(v_hbm, vwin.at[rows], kv_s.at[1, by - 1], kv_r.at[1, by - 1], ahead[by - 1]))
    owz = [go(ow_hbm, owbuf.at[z, x], owz_s.at[d], owz_r.at[d], zdev[d]) for d in ZORDER]
    with jax.named_scope("routing"):
        rpb[0] = routing_table(ids_ref[...], log_ref[...])
    rp = [
        go(rpb.at[0], rpb.at[SLOT[NZ - d]], rp_s.at[d], rp_r.at[d], zdev[d]) for d in ZORDER
    ]
    shp = [
        go(sh_hbm, shb.at[y, x, h], sh_s.at[i], sh_r.at[i], pdev[at]) for i, at in enumerate(plane)
    ]
    cz = [
        go(cache_hbm.at[:, up(z, d, NZ)], cmid_ref.at[z], cz_s.at[d], cz_r.at[d], zdev[d])
        for d in ZORDER
    ]
    pair = pdev[(2, 0)]
    rows_g, rows_d = pl.ds(h * 768, 768), pl.ds(h * 128, 128)
    ex = [
        go(wg_hbm.at[rows_g], wgb.at[1, rows_g], ex_s.at[0], ex_r.at[0], pair),
        go(wd_hbm.at[rows_d], wdb.at[1, rows_d], ex_s.at[1], ex_r.at[1], pair),
    ]

    with jax.named_scope("visible"):
        upper = jnp.where(iota((128, 128), 0) <= iota((128, 128), 1), 1.0, 0.0).astype(BF16)
        lens = jnp.broadcast_to(len_ref[...], (16, 128)).astype(BF16)
        ends = jnp.dot(lens, upper, preferred_element_type=F32)[0:1, :]
        qpos = (s * 64 + iota((64, 128), 0)).astype(F32)
        first = jnp.max(jnp.where(ends <= qpos, ends, 0.0), axis=-1, keepdims=True)
        kpos = (s * 64 - 256 + iota((64, 320), 1)).astype(F32)
        qcol = (s * 64 + iota((64, 320), 0)).astype(F32)
        seen = jnp.where((kpos >= first) & (kpos <= qcol), 0.0, NEGATIVE)
        seen3 = jnp.concatenate([seen, seen, seen], axis=0)

    with jax.named_scope("wait_keys"):
        own_k.wait()
        own_v.wait()
        own_q.wait()
        for c in kv:
            c.wait_recv()
    with jax.named_scope("attention"):
        for g in range(2):
            cols = slice(g * HD, (g + 1) * HD)
            qs = jnp.concatenate(
                [qbuf[:, (3 * g + i) * HD : (3 * g + i + 1) * HD] for i in range(3)], axis=0
            )
            sc = lax.dot_general(qs, kwin[:, cols], NT, preferred_element_type=F32)
            sc = jnp.where(seen3 < -1.0, NEGATIVE, sc * (1.0 / math.sqrt(HD)))
            w = jnp.exp(sc - jnp.max(sc, axis=-1, keepdims=True))
            total = jnp.sum(w, axis=-1, keepdims=True)
            o = jnp.dot(w.astype(BF16), vwin[:, cols], preferred_element_type=F32)
            o = (o / total).astype(BF16)
            for i in range(3):
                hbuf[y, :, (3 * g + i) * HD : (3 * g + i + 1) * HD] = o[i * 64 : (i + 1) * 64]
    hy = [
        go(hbuf.at[y], hbuf.at[y], hy_s.at[d], hy_r.at[d], pdev[(d, 0)]) for d in (1, 3, 2)
    ]

    with jax.named_scope("wait_columns"):
        own_ow.wait()
        for c in owz:
            c.wait_recv()
        owx = [
            go(owbuf.at[:, x], owbuf.at[:, x], owx_s.at[d], owx_r.at[d], pdev[(0, d)])
            for d in (1, 3, 2)
        ]
        for c in owx:
            c.wait_recv()
    with jax.named_scope("columns"):
        col, row = iota((384, 512), 0), iota((384, 512), 1)
        pick = jnp.where(row == lax.div(col, 12) * 16 + lax.rem(col, 12), 1.0, 0.0).astype(BF16)
        wc[...] = jnp.dot(
            pick, owbuf[...].reshape(512, 768), preferred_element_type=F32
        ).astype(BF16)

    with jax.named_scope("wait_heads"):
        for c in hy:
            c.wait_recv()
    with jax.named_scope("project"):
        po = lax.dot_general(hbuf[...].reshape(256, 768), wc[...], NT, preferred_element_type=F32)
        part[...] = po.reshape(4, 2, 32, 384)
    rs = []
    for d in (1, 3, 2):
        yd = up(y, d, NY)
        for i, hd in enumerate((h, 1 - h)):
            rs.append(
                go(part.at[yd, hd], rbuf.at[y, h], rs_s.at[i, d], rs_r.at[i, d], (seq_of(yd, z, x), hd))
            )
    rs.append(go(part.at[y, 1 - h], rbuf.at[y, h], rs_s.at[1, 0], rs_r.at[1, 0], sib))
    rbuf[y, h] = part[y, h]
    with jax.named_scope("cache_plane"):
        own_cache.wait()
        for c in cz:
            c.wait_recv()
        cp = [
            go(
                cmid_ref.at[:, up(y, at[0], NY), up(x, at[1], NX)], chand_ref.at[y, :, x],
                cp_s.at[i], cp_r.at[i], pdev[at],
            )
            for i, at in enumerate(plane)
        ]
        cp_own = here(cmid_ref.at[:, y, x], chand_ref.at[y, :, x])
    with jax.named_scope("wait_projected"):
        for c in rs:
            c.wait_recv()
    with jax.named_scope("norm"):
        own_res.wait()
        attn = [rbuf[j, 0] + rbuf[j, 1] for j in range(NY)]
        mixed = resbuf[...].astype(F32) + jnp.concatenate(attn, axis=1)
        ms = jnp.mean(mixed * mixed, axis=-1, keepdims=True)
        xb[0] = (mixed * lax.rsqrt(ms + EPSILON) * gain_ref[...]).astype(BF16)
    xz = {
        d: go(xb.at[0], xb.at[SLOT[NZ - d]], xz_s.at[d], xz_r.at[d], zdev[d])
        for d in [NZ - o for o in OFF[1:]]
    }

    with jax.named_scope("shared_weights"):
        own_sh.wait()
        for c in shp:
            c.wait_recv()
        sib_sh = go(shb.at[:, :, h], shb.at[:, :, h], sib_s.at[0], sib_r.at[0], sib)
        for c in rp:
            c.wait_recv()

    with jax.named_scope("choose"):
        lane = iota((128, COLS), 1)
        half = lax.div(lane, COLS // 2)
        expert = lax.rem(y + half, 2) * 32 + z * NX + lax.rem(lax.div(lane, ROWS), NX)
        row = iota((128, COLS), 0)
        of_rank = jnp.where(row == expert, 1.0, 0.0).astype(BF16)
        of_prob = jnp.where(row == expert + EXPERTS, 1.0, 0.0).astype(BF16)
        slot = lax.rem(iota((128, COLS), 1), ROWS)
        member = lax.div(row, 32) == lax.div(slot, CAP)
        number = lax.rem(slot, CAP).astype(F32)
        picks, weights = [], []
        for c in range(2):
            rpc = rpb[4 * c : 4 * c + 4].reshape(128, 128).astype(BF16)
            rank = jnp.dot(rpc, of_rank, preferred_element_type=F32)
            prob = jnp.dot(rpc, of_prob, preferred_element_type=F32)
            hit = member & (rank == number)
            picks.append(jnp.transpose(jnp.where(hit, 1.0, 0.0)).astype(BF16))
            weights.append(jnp.where(hit, prob, 0.0).astype(BF16))

    hops = [(p, d) for p in range(2) for d in (2, 1, 3, 0) if (p, d) != (0, 0)]
    sent = []
    for c in range(2):
        with jax.named_scope("wait_rows"):
            for o in OFF[4 * c : 4 * c + 4]:
                if o:
                    xz[NZ - o].wait_recv()
        with jax.named_scope("dispatch"):
            xc = xb[4 * c : 4 * c + 4].reshape(128, 1536)
            rows = jnp.dot(picks[c], xc, preferred_element_type=F32)
            for j in range(8):
                dsend[c, j] = rows[j * ROWS : (j + 1) * ROWS].astype(BF16)
            sent.append(
                [
                    go(
                        dsend.at[c, p * NX + up(x, d, NX)], drecv.at[c, p * NX + x],
                        d_s.at[c, i], d_r.at[c, i], pdev[(p, d)],
                    )
                    for i, (p, d) in enumerate(hops)
                ]
            )
            drecv[c, x] = dsend[c, x]

    with jax.named_scope("exchange_sibling"):
        for c in ex:
            c.wait_recv()
        sib_g = go(wgb.at[1, rows_g], wgb.at[1, rows_g], sib_s.at[1], sib_r.at[1], sib)
        sib_d = go(wdb.at[1, rows_d], wdb.at[1, rows_d], sib_s.at[2], sib_r.at[2], sib)
    with jax.named_scope("shared"):
        sib_sh.wait_recv()
        xs = xb[...].reshape(256, 1536)
        sh = shb[...].reshape(512, 1536)
        both = lax.dot_general(xs, sh, NT, preferred_element_type=F32)
        act = silu(pltpu.roll(both, 8, 1)) * pltpu.roll(both, 4, 1)
        live = lax.rem(lax.div(iota((256, 512), 1), 4), 4) == 2
        act = jnp.where(live, act, 0.0).astype(BF16)
        shared = jnp.dot(act, sh, preferred_element_type=F32)
    with jax.named_scope("wait_exchange"):
        own_wg.wait()
        own_wd.wait()
        sib_g.wait_recv()
        sib_d.wait_recv()

    back = []
    for c in range(2):
        with jax.named_scope("wait_dispatch"):
            for m in sent[c]:
                m.wait_recv()
        with jax.named_scope("experts"):
            rows = jnp.concatenate([drecv[c, j].astype(F32) for j in range(8)], axis=0).astype(BF16)
            acc = None
            for j in range(2):
                gu = jnp.dot(rows, wgb[j], preferred_element_type=F32)
                a = (silu(gu[:, :256]) * gu[:, 256:]).astype(BF16)
                o = jnp.dot(a, wdb[j], preferred_element_type=F32)
                acc = o if acc is None else acc + o
            for j in range(8):
                rsend[c, j] = acc[j * ROWS : (j + 1) * ROWS].astype(BF16)
            back.append(
                [
                    go(
                        rsend.at[c, p * NX + up(x, NX - d, NX)], rrecv.at[c, p * NX + x],
                        r_s.at[c, i], r_r.at[c, i],
                        pdev[((NY - p) % NY, (NX - d) % NX)],
                    )
                    for i, (p, d) in enumerate(hops)
                ]
            )
            rrecv[c, x] = rsend[c, x]
    red = []
    for c in range(2):
        with jax.named_scope("wait_return"):
            for m in back[c]:
                m.wait_recv()
        with jax.named_scope("combine"):
            rows = jnp.concatenate([rrecv[c, j].astype(F32) for j in range(8)], axis=0).astype(BF16)
            tot = shared[128 * c : 128 * c + 128] + jnp.dot(
                weights[c], rows, preferred_element_type=F32
            )
            pz[4 * c : 4 * c + 4] = tot.astype(BF16).reshape(4, 32, 1536)
            for o in OFF[4 * c : 4 * c + 4]:
                if o:
                    red.append(
                        go(pz.at[SLOT[o]], racc.at[SLOT[NZ - o]], z_s.at[o], z_r.at[o], zdev[o])
                    )
    racc[0] = pz[0]
    with jax.named_scope("wait_sum"):
        for c in red:
            c.wait_recv()
    out = mixed
    for j in range(NZ):
        out = out + racc[j].astype(F32)
    out_ref[...] = out.astype(BF16)
    with jax.named_scope("drain"):
        cp_own.wait()
        for c in cp:
            c.wait_recv()
        for c in pending:
            c.wait_send()


def shards(
    queries, key_vectors, value_vectors, lengths, out_weight, residual, norm_gain, route_ids,
    route_logits, shared_gate_up, shared_down, expert_gate_up, expert_down, cache_blocks, block_table,
):
    hbm, vmem = pl.BlockSpec(memory_space=pltpu.HBM), pl.BlockSpec(memory_space=pltpu.VMEM)
    dma = pltpu.SemaphoreType.DMA
    lens = jnp.pad(lengths.astype(F32), (0, 64)).reshape(1, 128)
    ow = jnp.pad(out_weight.T, ((0, 4), (0, 0)))
    sh = jnp.concatenate(
        [
            jnp.transpose(shared_gate_up, (1, 2, 0)).reshape(8, 1536),
            shared_down,
            jnp.zeros((4, 1536), BF16),
        ],
        axis=0,
    )
    wg = expert_gate_up.reshape(1536, 512)
    wd = expert_down.reshape(256, 1536)
    cache = cache_blocks.reshape(NY, NZ, NX, 8, 2, HD)
    sds = jax.ShapeDtypeStruct
    layer_out, _, chand = pl.pallas_call(
        layer_kernel,
        out_shape=(
            sds((32, 1536), BF16),
            sds((NZ, NY, NX, 8, 2, HD), BF16),
            sds((NY, NZ, NX, 8, 2, HD), BF16),
        ),
        in_specs=[hbm, hbm, hbm, vmem, hbm, hbm, vmem, vmem, vmem, hbm, hbm, hbm, hbm],
        out_specs=(vmem, hbm, hbm),
        scratch_shapes=[
            pltpu.VMEM((64, 768), BF16),
            pltpu.VMEM((320, 256), BF16),
            pltpu.VMEM((320, 256), BF16),
            pltpu.VMEM((32, 1536), BF16),
            pltpu.VMEM((NZ, NX, 16, 768), BF16),
            pltpu.VMEM((384, 768), BF16),
            pltpu.VMEM((NY, 64, 768), BF16),
            pltpu.VMEM((NY, 2, 32, 384), F32),
            pltpu.VMEM((NY, 2, 32, 384), F32),
            pltpu.VMEM((NZ, 32, 1536), BF16),
            pltpu.VMEM((NZ, 32, 128), F32),
            pltpu.VMEM((NY, NX, 2, 16, 1536), BF16),
            pltpu.VMEM((2, 1536, 512), BF16),
            pltpu.VMEM((2, 256, 1536), BF16),
            pltpu.VMEM((2, 8, ROWS, 1536), BF16),
            pltpu.VMEM((2, 8, ROWS, 1536), BF16),
            pltpu.VMEM((2, 8, ROWS, 1536), BF16),
            pltpu.VMEM((2, 8, ROWS, 1536), BF16),
            pltpu.VMEM((NZ, 32, 1536), BF16),
            pltpu.VMEM((NZ, 32, 1536), BF16),
            dma((2, 4)), dma((2, 4)),
            dma((8,)), dma((8,)),
            dma((4,)), dma((4,)),
            dma((8,)), dma((8,)),
            dma((15,)), dma((15,)),
            dma((8,)), dma((8,)),
            dma((15,)), dma((15,)),
            dma((2,)), dma((2,)),
            dma((3,)), dma((3,)),
            dma((4,)), dma((4,)),
            dma((2, 4)), dma((2, 4)),
            dma((8,)), dma((8,)),
            dma((2, 7)), dma((2, 7)),
            dma((2, 7)), dma((2, 7)),
            dma((8,)), dma((8,)),
            dma((10,)),
        ],
        compiler_params=pltpu.CompilerParams(
            collective_id=0, has_side_effects=True, vmem_limit_bytes=56 << 20
        ),
        name="layer",
    )(
        queries, key_vectors, value_vectors, lens, ow, residual, norm_gain.reshape(1, 1536),
        route_ids, route_logits, sh, wg, wd, cache,
    )
    cache_out = jnp.take(
        chand.reshape(128, 1, 8, 2, HD), block_table, axis=0, mode="clip"
    )
    return layer_out, cache_out


def solution(mesh):
    in_specs = (
        P("seq", "head"),
        P("seq", "head"),
        P("seq", "head"),
        P(),
        P("head", "seq"),
        P(("seq", "head"), None),
        P(),
        P(("seq", "head"), None),
        P(("seq", "head"), None),
        P(None, None, ("seq", "head")),
        P(("seq", "head"), None),
        P("seq", None, None, None),
        P("seq", None, None),
        P("seq", None, None, "head", None),
        P(),
    )
    out_specs = (P(("seq", "head"), None), P(None, "seq", None, "head", None))
    return jax.shard_map(shards, mesh=mesh, in_specs=in_specs, out_specs=out_specs, check_vma=False)
```

time: 412 us -> 140 us (0.34)
  the two profiles are of different devices: /device:TPU:4 before, /device:TPU:71 now
where the time goes in v2:
time: 140 us
  Pallas kernels  127 us (91%)
  local copies, waits for them, and re-layouts  11.2 us (8%)
    pallas_call x1, Pallas kernels, shards(): pl.pallas_call(layer_kernel, out_shape=(sds((32, 1536), BF16), sds((NZ, N...  127 us
    unnamed x20, local copies, waits for them, and re-layouts  5.86 us
    gather x1, local copies, waits for them, and re-layouts, shards(): jnp.take(chand.reshape(128, 1, 8, 2, HD), block_table, axis=0, mode='clip')  3.44 us

profile of v2, /device:TPU:71, one launch (start us, length us, event | category | flops | bytes accessed | tf_op | source)
XLA Modules:
  0.0 139.9 jit_solution(10266716084335073602)
XLA Ops:
  0.6 0.0 copy-start
  0.6 0.0 copy-start.2
  0.7 0.0 copy-start.1
  0.7 0.0 copy-start.4
  0.7 0.0 copy-start.5
  0.7 0.0 copy-start.3
  0.7 0.0 copy-start.7
  0.7 2.9 %copy.19 = bf16[192,8,2,256]{3,1,2,0:T(8,128)(2,1)} copy(bf16[192,8,2,256]{3,2,1,0:T(2,128)(2,1)} %bitcast.12) | data formatting | bytes 3145728
  3.6 0.0 copy-done
  3.7 0.1 pad.12.clone
  3.7 0.0 copy-done.2
  3.7 0.7 maximum_maximum_fusion.sh_hbm
  4.4 0.0 copy-done.1
  4.4 0.6 pad.9.ow_hbm
  5.0 0.0 copy-done.4
  5.1 0.7 copy.17.ids_ref
  5.7 0.0 copy-done.5
  5.7 0.7 copy.18.log_ref
  6.4 0.6 reshape.26.gain_ref
  7.0 0.6 pad_bitcast_fusion.len_ref
  7.6 127.3 %layer.1 = (bf16[32,1536]{1,0:T(8,128)(2,1)}, bf16[8,4,4,8,2,128]{5,4,3,2,1,0:T(2,128)(2,1)}, bf16[4,8,4,8,2,128]{5,4,3,2,1,0:T(2,128)(2,1)}) custom-call(bf16[64,768]{1,0:T(8,128)(2,1)} %q_hbm.1, bf16[64,256]{1,0:T(8,128)(2,1)} %k_hbm.1, bf16[64,256]{1,0:T(8,128)(2,1)} %v_hbm.1, f32[1,128]{1,0:T(1,128)} %pad_bitcast_fusion.len_ref, ...), custom_call_target="tpu_custom_call" | custom-call | tf_op jit(solution)/shard_map/layer/pallas_call | solution.py:398
  134.9 0.0 copy-done.6
  134.9 3.4 %gather_fusion = bf16[128,8,2,128]{3,2,1,0:T(2,128)(2,1)} fusion(bf16[128,8,2,128]{3,2,1,0:T(2,128)(2,1)} %bitcast.15, s32[1024]{0:T(1024)S(1)} %pad_clamp_fusion), kind=kCustom, calls=%fused_computation | custom fusion | bytes 1049088 | tf_op jit(solution)/shard_map/jit(_take)/gather | solution.py:453
  138.4 1.5 %copy.21 = bf16[32,1536]{1,0:T(8,128)(2,1)} copy(bf16[32,1536]{1,0:T(8,128)(2,1)} %get-tuple-element.8) | data formatting | bytes 196608
  (7 shorter events, 0.0 us)
Async XLA Ops:
  0.6 3.0 %copy-start = (bf16[1536,2,4]{0,2,1:T(4,128)(2,1)S(1)}, bf16[1536,2,4]{0,2,1:T(4,128)(2,1)}, u32[]{:S(2)}) copy-start(bf16[1536,2,4]{0,2,1:T(4,128)(2,1)} %param.24) | copy-start | bytes 73732
  0.6 3.1 %copy-start.2 = (bf16[4,1536]{1,0:T(4,128)(2,1)S(1)}, bf16[4,1536]{1,0:T(4,128)(2,1)}, u32[]{:S(2)}) copy-start(bf16[4,1536]{1,0:T(4,128)(2,1)} %param.25) | copy-start | bytes 36868
  0.7 3.8 %copy-start.1 = (bf16[768,12]{0,1:T(8,128)(2,1)S(1)}, bf16[768,12]{0,1:T(8,128)(2,1)}, u32[]{:S(2)}) copy-start(bf16[768,12]{0,1:T(8,128)(2,1)} %param.19) | copy-start | bytes 55300
  0.7 4.4 %copy-start.4 = (s32[32,6]{0,1:T(8,128)S(1)}, s32[32,6]{0,1:T(8,128)}, u32[]{:S(2)}) copy-start(s32[32,6]{0,1:T(8,128)} %param.22) | copy-start | bytes 2308
  0.7 5.1 %copy-start.5 = (f32[32,6]{0,1:T(8,128)S(1)}, f32[32,6]{0,1:T(8,128)}, u32[]{:S(2)}) copy-start(f32[32,6]{0,1:T(8,128)} %param.23) | copy-start | bytes 2308
  0.7 5.7 %copy-start.3 = (f32[1536]{0:T(1024)S(1)}, f32[1536]{0:T(1024)}, u32[]{:S(2)}) copy-start(f32[1536]{0:T(1024)} %param.21) | copy-start | bytes 18436
  0.7 6.3 %copy-start.7 = (s32[64]{0:T(128)S(1)}, s32[64]{0:T(128)}, u32[]{:S(2)}) copy-start(s32[64]{0:T(128)} %param.18) | copy-start | bytes 772
  7.6 127.3 %copy-start.6 = (s32[128]{0:T(128)S(1)}, s32[128]{0:T(128)}, u32[]{:S(2)}) copy-start(s32[128]{0:T(128)} %param.29) | copy-start | bytes 1540

commit v3 on v2

--- a/solution.py
+++ b/solution.py
@@ -49,13 +49,6 @@
     )
 
 
-def greet(peers):
-    barrier = pltpu.get_barrier_semaphore()
-    for dev in peers:
-        pl.semaphore_signal(barrier, inc=1, device_id=dev, device_id_type=MESH)
-    pl.semaphore_wait(barrier, len(peers))
-
-
 def iota(shape, axis):
     return lax.broadcasted_iota(jnp.int32, shape, axis)
 
@@ -65,30 +58,30 @@
 
 
 def routing_table(ids, logits):
-    tok = ids.shape[0]
-    lane = iota((tok, 128), 1)
-    top = jnp.max(logits, axis=-1, keepdims=True)
+    top = jnp.max(logits, axis=0, keepdims=True)
     e = jnp.exp(logits - top)
-    probs = e / jnp.sum(e, axis=-1, keepdims=True)
-    named = jnp.zeros((tok, 128), F32)
-    weight = jnp.zeros((tok, 128), F32)
+    probs = e / jnp.sum(e, axis=0, keepdims=True)
+    row = iota((128, 32), 0)
+    named = jnp.zeros((128, 32), F32)
+    weight = jnp.zeros((128, 32), F32)
     for r in range(TOP):
-        idr = ids[:, r : r + 1]
-        named = named + jnp.where(lane == idr, 1.0, 0.0)
-        weight = weight + jnp.where(lane - EXPERTS == idr, probs[:, r : r + 1], 0.0)
-    before = jnp.where(iota((tok, tok), 1) < iota((tok, tok), 0), 1.0, 0.0)
-    rank = jnp.dot(before.astype(BF16), named.astype(BF16), preferred_element_type=F32)
-    return jnp.where(lane < EXPERTS, jnp.where(named > 0.5, rank, -1.0), weight)
+        idr = jnp.broadcast_to(ids[r : r + 1, :], (128, 32))
+        named = named + jnp.where(row == idr, 1.0, 0.0)
+        weight = weight + jnp.where(row - EXPERTS == idr, probs[r : r + 1, :], 0.0)
+    before = jnp.where(iota((32, 32), 0) < iota((32, 32), 1), 1.0, 0.0)
+    rank = jnp.dot(named.astype(BF16), before.astype(BF16), preferred_element_type=F32)
+    table = jnp.where(row < EXPERTS, jnp.where(named > 0.5, rank, -1.0), weight)
+    return jnp.transpose(table)
 
 
 def layer_kernel(
-    q_hbm, k_hbm, v_hbm, len_ref, ow_hbm, res_hbm, gain_ref, ids_ref, log_ref,
-    sh_hbm, wg_hbm, wd_hbm, cache_hbm,
+    q_hbm, k_hbm, v_hbm, len_ref, ow_ref, res_hbm, gain_ref, ids_ref, log_ref,
+    sgu_ref, sd_ref, wg_hbm, wd_hbm, cache_hbm,
     out_ref, cmid_ref, chand_ref,
-    qbuf, kwin, vwin, resbuf, owbuf, wc, hbuf, part, rbuf, xb, rpb, shb, wgb, wdb,
-    dsend, drecv, rsend, rrecv, pz, racc,
-    kv_s, kv_r, owz_s, owz_r, owx_s, owx_r, rp_s, rp_r, sh_s, sh_r, cz_s, cz_r, cp_s, cp_r,
-    ex_s, ex_r, sib_s, sib_r, hy_s, hy_r, rs_s, rs_r, xz_s, xz_r, d_s, d_r, r_s, r_r, z_s, z_r, loc,
+    qbuf, kwin, vwin, resbuf, owpad, owbuf, wc, hbuf, part, rbuf, xb, rpb, shpad, shb, raw, wgb, wdb,
+    relay_g, relay_d, dsend, drecv, rsend, rrecv, pz, racc,
+    kv_s, kv_r, owz_s, owz_r, owx_s, owx_r, rp_s, rp_r, shy_s, shy_r, shx_s, shx_r, cz_s, cz_r, cp_s, cp_r,
+    e1_s, e1_r, e2_s, e2_r, sib_s, sib_r, hy_s, hy_r, rs_s, rs_r, xz_s, xz_r, d_s, d_r, r_s, r_r, z_s, z_r, loc,
 ):
     s, h, y, z, x = place()
     seqs = NY * NZ * NX
@@ -110,16 +103,40 @@
         local.append(copy)
         return copy
 
+    own_wg = here(wg_hbm, raw)
     own_k = here(k_hbm, kwin.at[pl.ds(256, 64)])
     own_v = here(v_hbm, vwin.at[pl.ds(256, 64)])
     own_q = here(q_hbm, qbuf)
-    own_ow = here(ow_hbm, owbuf.at[z, x])
     own_cache = here(cache_hbm.at[:, z], cmid_ref.at[z])
     own_res = here(res_hbm, resbuf)
-    own_sh = here(sh_hbm, shb.at[y, x, h])
-    own_wg = here(wg_hbm, wgb.at[0])
     own_wd = here(wd_hbm, wdb.at[0])
-    greet(list(zdev.values()) + list(pdev.values()) + [sib] + cross + ahead + behind)
+    peers = list(zdev.values()) + list(pdev.values()) + [sib] + cross + ahead + behind
+    barrier = pltpu.get_barrier_semaphore()
+    for dev in peers:
+        pl.semaphore_signal(barrier, inc=1, device_id=dev, device_id_type=MESH)
+
+    with jax.named_scope("pack"):
+        owpad[...] = jnp.concatenate(
+            [ow_ref[...].astype(F32), jnp.zeros((4, 768), F32)], axis=0
+        ).astype(BF16)
+        owbuf[z, x] = owpad[...]
+        shpad[...] = jnp.concatenate(
+            [
+                sgu_ref[...].astype(F32).reshape(8, 1536),
+                sd_ref[...].astype(F32),
+                jnp.zeros((4, 1536), F32),
+            ],
+            axis=0,
+        ).astype(BF16)
+        shb[y, x, h] = shpad[...]
+    with jax.named_scope("routing"):
+        rpb[0] = routing_table(ids_ref[...], log_ref[...])
+    with jax.named_scope("gate_up"):
+        own_wg.wait()
+        wgb[0, :, 0:256] = raw[:, 0, :]
+        wgb[0, :, 256:512] = raw[:, 1, :]
+    with jax.named_scope("enter"):
+        pl.semaphore_wait(barrier, len(peers))
 
     pending = []
 
@@ -134,31 +151,41 @@
         rows = pl.ds(64 * (4 - by), 64)
         kv.append(go(k_hbm, kwin.at[rows], kv_s.at[0, by - 1], kv_r.at[0, by - 1], ahead[by - 1]))
         kv.append(go(v_hbm, vwin.at[rows], kv_s.at[1, by - 1], kv_r.at[1, by - 1], ahead[by - 1]))
-    owz = [go(ow_hbm, owbuf.at[z, x], owz_s.at[d], owz_r.at[d], zdev[d]) for d in ZORDER]
-    with jax.named_scope("routing"):
-        rpb[0] = routing_table(ids_ref[...], log_ref[...])
+    owz = [go(owpad, owbuf.at[z, x], owz_s.at[d], owz_r.at[d], zdev[d]) for d in ZORDER]
     rp = [
         go(rpb.at[0], rpb.at[SLOT[NZ - d]], rp_s.at[d], rp_r.at[d], zdev[d]) for d in ZORDER
     ]
-    shp = [
-        go(sh_hbm, shb.at[y, x, h], sh_s.at[i], sh_r.at[i], pdev[at]) for i, at in enumerate(plane)
-    ]
-    cz = [
-        go(cache_hbm.at[:, up(z, d, NZ)], cmid_ref.at[z], cz_s.at[d], cz_r.at[d], zdev[d])
-        for d in ZORDER
-    ]
-    pair = pdev[(2, 0)]
+    shy = [
+        go(shpad, shb.at[y, x, h], shy_s.at[d], shy_r.at[d], pdev[(d, 0)]) for d in (1, 3, 2)
+    ]
+    sides = (pdev[(1, 0)], pdev[(3, 0)])
     rows_g, rows_d = pl.ds(h * 768, 768), pl.ds(h * 128, 128)
-    ex = [
-        go(wg_hbm.at[rows_g], wgb.at[1, rows_g], ex_s.at[0], ex_r.at[0], pair),
-        go(wd_hbm.at[rows_d], wdb.at[1, rows_d], ex_s.at[1], ex_r.at[1], pair),
-    ]
+
+    def piece(i):
+        if i < 4:
+            return pl.ds(h * 768 + i * 192, 192)
+        return pl.ds(h * 128 + (i - 4) * 64, 64)
+
+    def first_hop(i):
+        sem = e1_s.at[i], e1_r.at[i], sides[i % 2]
+        if i < 4:
+            return go(wgb.at[0, piece(i)], relay_g.at[i], *sem)
+        return go(wd_hbm.at[piece(i)], relay_d.at[i - 4], *sem)
+
+    def second_hop(i, arrived):
+        arrived.wait_recv()
+        sem = e2_s.at[i], e2_r.at[i], sides[i % 2]
+        if i < 4:
+            return go(relay_g.at[i], wgb.at[1, piece(i)], *sem)
+        return go(relay_d.at[i - 4], wdb.at[1, piece(i)], *sem)
+
+    ex1 = [first_hop(i) for i in range(4)]
 
     with jax.named_scope("visible"):
-        upper = jnp.where(iota((128, 128), 0) <= iota((128, 128), 1), 1.0, 0.0).astype(BF16)
-        lens = jnp.broadcast_to(len_ref[...], (16, 128)).astype(BF16)
+        upper = jnp.where(iota((64, 64), 0) <= iota((64, 64), 1), 1.0, 0.0).astype(BF16)
+        lens = jnp.broadcast_to(len_ref[...].astype(F32).reshape(1, 64), (16, 64)).astype(BF16)
         ends = jnp.dot(lens, upper, preferred_element_type=F32)[0:1, :]
-        qpos = (s * 64 + iota((64, 128), 0)).astype(F32)
+        qpos = (s * 64 + iota((64, 64), 0)).astype(F32)
         first = jnp.max(jnp.where(ends <= qpos, ends, 0.0), axis=-1, keepdims=True)
         kpos = (s * 64 - 256 + iota((64, 320), 1)).astype(F32)
         qcol = (s * 64 + iota((64, 320), 0)).astype(F32)
@@ -171,6 +198,16 @@
         own_q.wait()
         for c in kv:
             c.wait_recv()
+        for c in owz:
+            c.wait_recv()
+    owx = [
+        go(owbuf.at[:, x], owbuf.at[:, x], owx_s.at[d], owx_r.at[d], pdev[(0, d)])
+        for d in (1, 3, 2)
+    ]
+    cz = [
+        go(cache_hbm.at[:, up(z, d, NZ)], cmid_ref.at[z], cz_s.at[d], cz_r.at[d], zdev[d])
+        for d in ZORDER
+    ]
     with jax.named_scope("attention"):
         for g in range(2):
             cols = slice(g * HD, (g + 1) * HD)
@@ -190,15 +227,14 @@
     ]
 
     with jax.named_scope("wait_columns"):
-        own_ow.wait()
-        for c in owz:
-            c.wait_recv()
-        owx = [
-            go(owbuf.at[:, x], owbuf.at[:, x], owx_s.at[d], owx_r.at[d], pdev[(0, d)])
-            for d in (1, 3, 2)
-        ]
         for c in owx:
             c.wait_recv()
+        for c in shy:
+            c.wait_recv()
+    shx = [
+        go(shb.at[:, x, h], shb.at[:, x, h], shx_s.at[d], shx_r.at[d], pdev[(0, d)])
+        for d in (1, 3, 2)
+    ]
     with jax.named_scope("columns"):
         col, row = iota((384, 512), 0), iota((384, 512), 1)
         pick = jnp.where(row == lax.div(col, 12) * 16 + lax.rem(col, 12), 1.0, 0.0).astype(BF16)
@@ -211,7 +247,7 @@
             c.wait_recv()
     with jax.named_scope("project"):
         po = lax.dot_general(hbuf[...].reshape(256, 768), wc[...], NT, preferred_element_type=F32)
-        part[...] = po.reshape(4, 2, 32, 384)
+        part[...] = po.reshape(4, 2, 32, 384).astype(BF16)
     rs = []
     for d in (1, 3, 2):
         yd = up(y, d, NY)
@@ -221,35 +257,25 @@
             )
     rs.append(go(part.at[y, 1 - h], rbuf.at[y, h], rs_s.at[1, 0], rs_r.at[1, 0], sib))
     rbuf[y, h] = part[y, h]
-    with jax.named_scope("cache_plane"):
-        own_cache.wait()
-        for c in cz:
-            c.wait_recv()
-        cp = [
-            go(
-                cmid_ref.at[:, up(y, at[0], NY), up(x, at[1], NX)], chand_ref.at[y, :, x],
-                cp_s.at[i], cp_r.at[i], pdev[at],
-            )
-            for i, at in enumerate(plane)
-        ]
-        cp_own = here(cmid_ref.at[:, y, x], chand_ref.at[y, :, x])
     with jax.named_scope("wait_projected"):
         for c in rs:
             c.wait_recv()
     with jax.named_scope("norm"):
         own_res.wait()
-        attn = [rbuf[j, 0] + rbuf[j, 1] for j in range(NY)]
+        attn = [rbuf[j, 0].astype(F32) + rbuf[j, 1].astype(F32) for j in range(NY)]
         mixed = resbuf[...].astype(F32) + jnp.concatenate(attn, axis=1)
         ms = jnp.mean(mixed * mixed, axis=-1, keepdims=True)
-        xb[0] = (mixed * lax.rsqrt(ms + EPSILON) * gain_ref[...]).astype(BF16)
+        xb[0] = (mixed * lax.rsqrt(ms + EPSILON) * gain_ref[...].reshape(1, 1536)).astype(BF16)
     xz = {
         d: go(xb.at[0], xb.at[SLOT[NZ - d]], xz_s.at[d], xz_r.at[d], zdev[d])
         for d in [NZ - o for o in OFF[1:]]
     }
 
+    with jax.named_scope("relay"):
+        ex2 = [second_hop(i, ex1[i]) for i in range(4)]
+        ex1 += [first_hop(i) for i in range(4, 6)]
     with jax.named_scope("shared_weights"):
-        own_sh.wait()
-        for c in shp:
+        for c in shx:
             c.wait_recv()
         sib_sh = go(shb.at[:, :, h], shb.at[:, :, h], sib_s.at[0], sib_r.at[0], sib)
         for c in rp:
@@ -274,6 +300,17 @@
             picks.append(jnp.transpose(jnp.where(hit, 1.0, 0.0)).astype(BF16))
             weights.append(jnp.where(hit, prob, 0.0).astype(BF16))
 
+    turn = 1 + 2 * lax.rem(x, 2)
+
+    def to_expert(p, d):
+        return pdev[(0, d)] if p == 0 else (seq_of(up(y, turn, NY), z, up(x, d, NX)), h)
+
+    def to_source(p, d):
+        xs = up(x, NX - d, NX)
+        if p == 0:
+            return pdev[(0, NX - d)]
+        return (seq_of(up(y, 3 - 2 * lax.rem(xs, 2), NY), z, xs), h)
+
     hops = [(p, d) for p in range(2) for d in (2, 1, 3, 0) if (p, d) != (0, 0)]
     sent = []
     for c in range(2):
@@ -290,15 +327,18 @@
                 [
                     go(
                         dsend.at[c, p * NX + up(x, d, NX)], drecv.at[c, p * NX + x],
-                        d_s.at[c, i], d_r.at[c, i], pdev[(p, d)],
+                        d_s.at[c, i], d_r.at[c, i], to_expert(p, d),
                     )
                     for i, (p, d) in enumerate(hops)
                 ]
             )
             drecv[c, x] = dsend[c, x]
+        if c == 0:
+            with jax.named_scope("relay_down"):
+                ex2 += [second_hop(i, ex1[i]) for i in range(4, 6)]
 
     with jax.named_scope("exchange_sibling"):
-        for c in ex:
+        for c in ex2:
             c.wait_recv()
         sib_g = go(wgb.at[1, rows_g], wgb.at[1, rows_g], sib_s.at[1], sib_r.at[1], sib)
         sib_d = go(wdb.at[1, rows_d], wdb.at[1, rows_d], sib_s.at[2], sib_r.at[2], sib)
@@ -312,7 +352,6 @@
         act = jnp.where(live, act, 0.0).astype(BF16)
         shared = jnp.dot(act, sh, preferred_element_type=F32)
     with jax.named_scope("wait_exchange"):
-        own_wg.wait()
         own_wd.wait()
         sib_g.wait_recv()
         sib_d.wait_recv()
@@ -336,8 +375,7 @@
                 [
                     go(
                         rsend.at[c, p * NX + up(x, NX - d, NX)], rrecv.at[c, p * NX + x],
-                        r_s.at[c, i], r_r.at[c, i],
-                        pdev[((NY - p) % NY, (NX - d) % NX)],
+                        r_s.at[c, i], r_r.at[c, i], to_source(p, d),
                     )
                     for i, (p, d) in enumerate(hops)
                 ]
@@ -360,6 +398,18 @@
                         go(pz.at[SLOT[o]], racc.at[SLOT[NZ - o]], z_s.at[o], z_r.at[o], zdev[o])
                     )
     racc[0] = pz[0]
+    with jax.named_scope("cache_plane"):
+        own_cache.wait()
+        for c in cz:
+            c.wait_recv()
+        cp = [
+            go(
+                cmid_ref.at[:, up(y, at[0], NY), up(x, at[1], NX)], chand_ref.at[y, :, x],
+                cp_s.at[i], cp_r.at[i], pdev[at],
+            )
+            for i, at in enumerate(plane)
+        ]
+        cp_own = here(cmid_ref.at[:, y, x], chand_ref.at[y, :, x])
     with jax.named_scope("wait_sum"):
         for c in red:
             c.wait_recv()
@@ -381,17 +431,8 @@
 ):
     hbm, vmem = pl.BlockSpec(memory_space=pltpu.HBM), pl.BlockSpec(memory_space=pltpu.VMEM)
     dma = pltpu.SemaphoreType.DMA
-    lens = jnp.pad(lengths.astype(F32), (0, 64)).reshape(1, 128)
-    ow = jnp.pad(out_weight.T, ((0, 4), (0, 0)))
-    sh = jnp.concatenate(
-        [
-            jnp.transpose(shared_gate_up, (1, 2, 0)).reshape(8, 1536),
-            shared_down,
-            jnp.zeros((4, 1536), BF16),
-        ],
-        axis=0,
-    )
-    wg = expert_gate_up.reshape(1536, 512)
+    sgu = jnp.transpose(shared_gate_up, (1, 2, 0))
+    wg = expert_gate_up.reshape(1536, 2, 256)
     wd = expert_down.reshape(256, 1536)
     cache = cache_blocks.reshape(NY, NZ, NX, 8, 2, HD)
     sds = jax.ShapeDtypeStruct
@@ -402,23 +443,28 @@
             sds((NZ, NY, NX, 8, 2, HD), BF16),
             sds((NY, NZ, NX, 8, 2, HD), BF16),
         ),
-        in_specs=[hbm, hbm, hbm, vmem, hbm, hbm, vmem, vmem, vmem, hbm, hbm, hbm, hbm],
+        in_specs=[hbm, hbm, hbm, vmem, vmem, hbm, vmem, vmem, vmem, vmem, vmem, hbm, hbm, hbm],
         out_specs=(vmem, hbm, hbm),
         scratch_shapes=[
             pltpu.VMEM((64, 768), BF16),
             pltpu.VMEM((320, 256), BF16),
             pltpu.VMEM((320, 256), BF16),
             pltpu.VMEM((32, 1536), BF16),
+            pltpu.VMEM((16, 768), BF16),
             pltpu.VMEM((NZ, NX, 16, 768), BF16),
             pltpu.VMEM((384, 768), BF16),
             pltpu.VMEM((NY, 64, 768), BF16),
-            pltpu.VMEM((NY, 2, 32, 384), F32),
-            pltpu.VMEM((NY, 2, 32, 384), F32),
+            pltpu.VMEM((NY, 2, 32, 384), BF16),
+            pltpu.VMEM((NY, 2, 32, 384), BF16),
             pltpu.VMEM((NZ, 32, 1536), BF16),
             pltpu.VMEM((NZ, 32, 128), F32),
+            pltpu.VMEM((16, 1536), BF16),
             pltpu.VMEM((NY, NX, 2, 16, 1536), BF16),
+            pltpu.VMEM((1536, 2, 256), BF16),
             pltpu.VMEM((2, 1536, 512), BF16),
             pltpu.VMEM((2, 256, 1536), BF16),
+            pltpu.VMEM((4, 192, 512), BF16),
+            pltpu.VMEM((2, 64, 1536), BF16),
             pltpu.VMEM((2, 8, ROWS, 1536), BF16),
             pltpu.VMEM((2, 8, ROWS, 1536), BF16),
             pltpu.VMEM((2, 8, ROWS, 1536), BF16),
@@ -429,10 +475,12 @@
             dma((8,)), dma((8,)),
             dma((4,)), dma((4,)),
             dma((8,)), dma((8,)),
-            dma((15,)), dma((15,)),
+            dma((4,)), dma((4,)),
+            dma((4,)), dma((4,)),
             dma((8,)), dma((8,)),
             dma((15,)), dma((15,)),
-            dma((2,)), dma((2,)),
+            dma((6,)), dma((6,)),
+            dma((6,)), dma((6,)),
             dma((3,)), dma((3,)),
             dma((4,)), dma((4,)),
             dma((2, 4)), dma((2, 4)),
@@ -440,15 +488,15 @@
             dma((2, 7)), dma((2, 7)),
             dma((2, 7)), dma((2, 7)),
             dma((8,)), dma((8,)),
-            dma((10,)),
+            dma((8,)),
         ],
         compiler_params=pltpu.CompilerParams(
             collective_id=0, has_side_effects=True, vmem_limit_bytes=56 << 20
         ),
         name="layer",
     )(
-        queries, key_vectors, value_vectors, lens, ow, residual, norm_gain.reshape(1, 1536),
-        route_ids, route_logits, sh, wg, wd, cache,
+        queries, key_vectors, value_vectors, lengths, out_weight.T, residual, norm_gain,
+        route_ids.T, route_logits.T, sgu, shared_down, wg, wd, cache,
     )
     cache_out = jnp.take(
         chand.reshape(128, 1, 8, 2, HD), block_table, axis=0, mode="clip"

time: 140 us -> 113 us (0.81)
  the two profiles are of different devices: /device:TPU:71 before, /device:TPU:33 now
where the time goes in v3:
time: 113 us; the launch traced here: 112 us
  Pallas kernels  107 us (95%)
  local copies, waits for them, and re-layouts  4.98 us (4%)
    pallas_call x1, Pallas kernels, shards(): pl.pallas_call(layer_kernel, out_shape=(sds((32, 1536), BF16), sds((NZ, N...  107 us
    gather x1, local copies, waits for them, and re-layouts, shards(): jnp.take(chand.reshape(128, 1, 8, 2, HD), block_table, axis=0, mode='clip')  3.44 us

profile of v3, /device:TPU:33, one launch (start us, length us, event | category | flops | bytes accessed | tf_op | source)
XLA Modules:
  0.0 112.4 jit_solution(15863396246406610054)
XLA Ops:
  0.6 0.0 copy-start
  0.6 106.8 %layer.1 = (bf16[32,1536]{1,0:T(8,128)(2,1)}, bf16[8,4,4,8,2,128]{5,4,3,2,1,0:T(2,128)(2,1)}, bf16[4,8,4,8,2,128]{5,4,3,2,1,0:T(2,128)(2,1)}) custom-call(bf16[64,768]{1,0:T(8,128)(2,1)} %q_hbm.1, bf16[64,256]{1,0:T(8,128)(2,1)} %k_hbm.1, bf16[64,256]{1,0:T(8,128)(2,1)} %v_hbm.1, s32[64]{0:T(128)} %len_ref.1, bf16[12,768]{1,0:T(8,128)(2,1)} %bitcast.14, ...), custom_call_target="tpu_custom_call" | custom-call | tf_op jit(solution)/shard_map/layer/pallas_call | solution.py:439
  107.4 0.0 copy-done
  107.4 3.4 %gather_fusion = bf16[128,8,2,128]{3,2,1,0:T(2,128)(2,1)} fusion(bf16[128,8,2,128]{3,2,1,0:T(2,128)(2,1)} %bitcast.12, s32[1024]{0:T(1024)S(1)} %pad_clamp_fusion), kind=kCustom, calls=%fused_computation | custom fusion | bytes 1049088 | tf_op jit(solution)/shard_map/jit(_take)/gather | solution.py:501
  110.9 1.5 %copy.18 = bf16[32,1536]{1,0:T(8,128)(2,1)} copy(bf16[32,1536]{1,0:T(8,128)(2,1)} %get-tuple-element.8) | data formatting | bytes 196608
  (1 shorter events, 0.0 us)
Async XLA Ops:
  0.6 106.8 %copy-start = (s32[128]{0:T(128)S(1)}, s32[128]{0:T(128)}, u32[]{:S(2)}) copy-start(s32[128]{0:T(128)} %param.29) | copy-start | bytes 1540

commit v4 on v3

--- a/solution.py
+++ b/solution.py
@@ -19,7 +19,7 @@
 F32 = jnp.float32
 BF16 = jnp.bfloat16
 ZORDER = (1, 7, 2, 6, 3, 5, 4)
-OFF = (0, 1, 4, 3, 7, 6, 2, 5)
+OFF = (0, 1, 7, 4, 2, 6, 3, 5)
 SLOT = {o: k for k, o in enumerate(OFF)}
 ROWS = 24
 COLS = 8 * ROWS
@@ -79,7 +79,7 @@
     sgu_ref, sd_ref, wg_hbm, wd_hbm, cache_hbm,
     out_ref, cmid_ref, chand_ref,
     qbuf, kwin, vwin, resbuf, owpad, owbuf, wc, hbuf, part, rbuf, xb, rpb, shpad, shb, raw, wgb, wdb,
-    relay_g, relay_d, dsend, drecv, rsend, rrecv, pz, racc,
+    relay_g, relay_d, relay_z, dsend, drecv, rsend, rrecv, pz, racc,
     kv_s, kv_r, owz_s, owz_r, owx_s, owx_r, rp_s, rp_r, shy_s, shy_r, shx_s, shx_r, cz_s, cz_r, cp_s, cp_r,
     e1_s, e1_r, e2_s, e2_r, sib_s, sib_r, hy_s, hy_r, rs_s, rs_r, xz_s, xz_r, d_s, d_r, r_s, r_r, z_s, z_r, loc,
 ):
@@ -103,7 +103,7 @@
         local.append(copy)
         return copy
 
-    own_wg = here(wg_hbm, raw)
+    own_wg = here(wg_hbm, raw.at[0])
     own_k = here(k_hbm, kwin.at[pl.ds(256, 64)])
     own_v = here(v_hbm, vwin.at[pl.ds(256, 64)])
     own_q = here(q_hbm, qbuf)
@@ -131,10 +131,6 @@
         shb[y, x, h] = shpad[...]
     with jax.named_scope("routing"):
         rpb[0] = routing_table(ids_ref[...], log_ref[...])
-    with jax.named_scope("gate_up"):
-        own_wg.wait()
-        wgb[0, :, 0:256] = raw[:, 0, :]
-        wgb[0, :, 256:512] = raw[:, 1, :]
     with jax.named_scope("enter"):
         pl.semaphore_wait(barrier, len(peers))
 
@@ -169,14 +165,14 @@
     def first_hop(i):
         sem = e1_s.at[i], e1_r.at[i], sides[i % 2]
         if i < 4:
-            return go(wgb.at[0, piece(i)], relay_g.at[i], *sem)
+            return go(wg_hbm.at[piece(i)], relay_g.at[i], *sem)
         return go(wd_hbm.at[piece(i)], relay_d.at[i - 4], *sem)
 
     def second_hop(i, arrived):
         arrived.wait_recv()
         sem = e2_s.at[i], e2_r.at[i], sides[i % 2]
         if i < 4:
-            return go(relay_g.at[i], wgb.at[1, piece(i)], *sem)
+            return go(relay_g.at[i], raw.at[1, piece(i)], *sem)
         return go(relay_d.at[i - 4], wdb.at[1, piece(i)], *sem)
 
     ex1 = [first_hop(i) for i in range(4)]
@@ -192,22 +188,19 @@
         seen = jnp.where((kpos >= first) & (kpos <= qcol), 0.0, NEGATIVE)
         seen3 = jnp.concatenate([seen, seen, seen], axis=0)
 
+    with jax.named_scope("wait_first_columns"):
+        for c in owz:
+            c.wait_recv()
+    owx = {
+        d: go(owbuf.at[:, x], owbuf.at[:, x], owx_s.at[d], owx_r.at[d], pdev[(0, d)])
+        for d in (1, 3)
+    }
     with jax.named_scope("wait_keys"):
         own_k.wait()
         own_v.wait()
         own_q.wait()
         for c in kv:
             c.wait_recv()
-        for c in owz:
-            c.wait_recv()
-    owx = [
-        go(owbuf.at[:, x], owbuf.at[:, x], owx_s.at[d], owx_r.at[d], pdev[(0, d)])
-        for d in (1, 3, 2)
-    ]
-    cz = [
-        go(cache_hbm.at[:, up(z, d, NZ)], cmid_ref.at[z], cz_s.at[d], cz_r.at[d], zdev[d])
-        for d in ZORDER
-    ]
     with jax.named_scope("attention"):
         for g in range(2):
             cols = slice(g * HD, (g + 1) * HD)
@@ -226,10 +219,24 @@
         go(hbuf.at[y], hbuf.at[y], hy_s.at[d], hy_r.at[d], pdev[(d, 0)]) for d in (1, 3, 2)
     ]
 
+    with jax.named_scope("gate_up"):
+        own_wg.wait()
+        wgb[0, 0:768, 0:256] = raw[0, 0:768, 0, :]
+        wgb[0, 0:768, 256:512] = raw[0, 0:768, 1, :]
     with jax.named_scope("wait_columns"):
-        for c in owx:
-            c.wait_recv()
+        left, right = up(x, 3, NX), up(x, 1, NX)
+        owx[1].wait_recv()
+        lower = owbuf.at[0:4, left]
+        fwd = [go(lower, lower, owx_s.at[0], owx_r.at[0], pdev[(0, 1)])]
+        owx[3].wait_recv()
+        higher = owbuf.at[4:8, right]
+        fwd.append(go(higher, higher, owx_s.at[2], owx_r.at[2], pdev[(0, 3)]))
         for c in shy:
+            c.wait_recv()
+    with jax.named_scope("relay_gate"):
+        ex2 = [second_hop(i, ex1[i]) for i in range(2)]
+    with jax.named_scope("wait_far_columns"):
+        for c in fwd:
             c.wait_recv()
     shx = [
         go(shb.at[:, x, h], shb.at[:, x, h], shx_s.at[d], shx_r.at[d], pdev[(0, d)])
@@ -257,6 +264,9 @@
             )
     rs.append(go(part.at[y, 1 - h], rbuf.at[y, h], rs_s.at[1, 0], rs_r.at[1, 0], sib))
     rbuf[y, h] = part[y, h]
+    with jax.named_scope("gate_up_rest"):
+        wgb[0, 768:1536, 0:256] = raw[0, 768:1536, 0, :]
+        wgb[0, 768:1536, 256:512] = raw[0, 768:1536, 1, :]
     with jax.named_scope("wait_projected"):
         for c in rs:
             c.wait_recv()
@@ -267,21 +277,14 @@
         ms = jnp.mean(mixed * mixed, axis=-1, keepdims=True)
         xb[0] = (mixed * lax.rsqrt(ms + EPSILON) * gain_ref[...].reshape(1, 1536)).astype(BF16)
     xz = {
-        d: go(xb.at[0], xb.at[SLOT[NZ - d]], xz_s.at[d], xz_r.at[d], zdev[d])
-        for d in [NZ - o for o in OFF[1:]]
+        d: go(xb.at[0], xb.at[SLOT[NZ - d]], xz_s.at[d], xz_r.at[d], zdev[d]) for d in (2, 6, 1, 7)
     }
-
     with jax.named_scope("relay"):
-        ex2 = [second_hop(i, ex1[i]) for i in range(4)]
+        ex2 += [second_hop(i, ex1[i]) for i in range(2, 4)]
         ex1 += [first_hop(i) for i in range(4, 6)]
-    with jax.named_scope("shared_weights"):
-        for c in shx:
-            c.wait_recv()
-        sib_sh = go(shb.at[:, :, h], shb.at[:, :, h], sib_s.at[0], sib_r.at[0], sib)
+    with jax.named_scope("choose"):
         for c in rp:
             c.wait_recv()
-
-    with jax.named_scope("choose"):
         lane = iota((128, COLS), 1)
         half = lax.div(lane, COLS // 2)
         expert = lax.rem(y + half, 2) * 32 + z * NX + lax.rem(lax.div(lane, ROWS), NX)
@@ -300,6 +303,20 @@
             picks.append(jnp.transpose(jnp.where(hit, 1.0, 0.0)).astype(BF16))
             weights.append(jnp.where(hit, prob, 0.0).astype(BF16))
 
+    with jax.named_scope("wait_near_rows"):
+        xz[2].wait_recv()
+        low = pl.ds(0, 16)
+        xz[4] = go(
+            xb.at[SLOT[6], low], xb.at[SLOT[4], low], xz_s.at[4], xz_r.at[4], zdev[2]
+        )
+        xz[3] = go(xb.at[SLOT[6]], xb.at[SLOT[5]], xz_s.at[3], xz_r.at[3], zdev[1])
+        xz[6].wait_recv()
+        high = pl.ds(16, 16)
+        xz[0] = go(
+            xb.at[SLOT[2], high], xb.at[SLOT[4], high], xz_s.at[0], xz_r.at[0], zdev[6]
+        )
+        xz[5] = go(xb.at[SLOT[2]], xb.at[SLOT[3]], xz_s.at[5], xz_r.at[5], zdev[7])
+
     turn = 1 + 2 * lax.rem(x, 2)
 
     def to_expert(p, d):
@@ -315,9 +332,8 @@
     sent = []
     for c in range(2):
         with jax.named_scope("wait_rows"):
-            for o in OFF[4 * c : 4 * c + 4]:
-                if o:
-                    xz[NZ - o].wait_recv()
+            for d in ((1, 7, 4, 0), (3, 5))[c]:
+                xz[d].wait_recv()
         with jax.named_scope("dispatch"):
             xc = xb[4 * c : 4 * c + 4].reshape(128, 1536)
             rows = jnp.dot(picks[c], xc, preferred_element_type=F32)
@@ -336,11 +352,21 @@
         if c == 0:
             with jax.named_scope("relay_down"):
                 ex2 += [second_hop(i, ex1[i]) for i in range(4, 6)]
-
+            with jax.named_scope("shared_weights"):
+                for m in shx:
+                    m.wait_recv()
+                sib_sh = go(shb.at[:, :, h], shb.at[:, :, h], sib_s.at[0], sib_r.at[0], sib)
+
+    cz = [
+        go(cache_hbm.at[:, up(z, d, NZ)], cmid_ref.at[z], cz_s.at[d], cz_r.at[d], zdev[d])
+        for d in ZORDER
+    ]
     with jax.named_scope("exchange_sibling"):
-        for c in ex2:
-            c.wait_recv()
-        sib_g = go(wgb.at[1, rows_g], wgb.at[1, rows_g], sib_s.at[1], sib_r.at[1], sib)
+        for c in ex2[:4]:
+            c.wait_recv()
+        sib_g = go(raw.at[1, rows_g], raw.at[1, rows_g], sib_s.at[1], sib_r.at[1], sib)
+        for c in ex2[4:]:
+            c.wait_recv()
         sib_d = go(wdb.at[1, rows_d], wdb.at[1, rows_d], sib_s.at[2], sib_r.at[2], sib)
     with jax.named_scope("shared"):
         sib_sh.wait_recv()
@@ -354,6 +380,8 @@
     with jax.named_scope("wait_exchange"):
         own_wd.wait()
         sib_g.wait_recv()
+        wgb[1, :, 0:256] = raw[1, :, 0, :]
+        wgb[1, :, 256:512] = raw[1, :, 1, :]
         sib_d.wait_recv()
 
     back = []
@@ -392,11 +420,21 @@
                 weights[c], rows, preferred_element_type=F32
             )
             pz[4 * c : 4 * c + 4] = tot.astype(BF16).reshape(4, 32, 1536)
-            for o in OFF[4 * c : 4 * c + 4]:
-                if o:
-                    red.append(
-                        go(pz.at[SLOT[o]], racc.at[SLOT[NZ - o]], z_s.at[o], z_r.at[o], zdev[o])
-                    )
+            for o in ((1, 7), (3, 5, 2, 6))[c]:
+                red.append(
+                    go(pz.at[SLOT[o]], racc.at[SLOT[NZ - o]], z_s.at[o], z_r.at[o], zdev[o])
+                )
+            if c == 0:
+                by = go(pz.at[SLOT[4], high], relay_z, z_s.at[8], z_r.at[8], zdev[6])
+                red.append(
+                    go(pz.at[SLOT[4], low], racc.at[SLOT[4], low], z_s.at[4], z_r.at[4], zdev[4])
+                )
+        if c == 0:
+            with jax.named_scope("relay_sum"):
+                by.wait_recv()
+                red.append(
+                    go(relay_z, racc.at[SLOT[4], high], z_s.at[0], z_r.at[0], zdev[6])
+                )
     racc[0] = pz[0]
     with jax.named_scope("cache_plane"):
         own_cache.wait()
@@ -444,7 +482,7 @@
             sds((NY, NZ, NX, 8, 2, HD), BF16),
         ),
         in_specs=[hbm, hbm, hbm, vmem, vmem, hbm, vmem, vmem, vmem, vmem, vmem, hbm, hbm, hbm],
-        out_specs=(vmem, hbm, hbm),
+        out_specs=(vmem, hbm, vmem),
         scratch_shapes=[
             pltpu.VMEM((64, 768), BF16),
             pltpu.VMEM((320, 256), BF16),
@@ -460,11 +498,12 @@
             pltpu.VMEM((NZ, 32, 128), F32),
             pltpu.VMEM((16, 1536), BF16),
             pltpu.VMEM((NY, NX, 2, 16, 1536), BF16),
-            pltpu.VMEM((1536, 2, 256), BF16),
+            pltpu.VMEM((2, 1536, 2, 256), BF16),
             pltpu.VMEM((2, 1536, 512), BF16),
             pltpu.VMEM((2, 256, 1536), BF16),
-            pltpu.VMEM((4, 192, 512), BF16),
+            pltpu.VMEM((4, 192, 2, 256), BF16),
             pltpu.VMEM((2, 64, 1536), BF16),
+            pltpu.VMEM((16, 1536), BF16),
             pltpu.VMEM((2, 8, ROWS, 1536), BF16),
             pltpu.VMEM((2, 8, ROWS, 1536), BF16),
             pltpu.VMEM((2, 8, ROWS, 1536), BF16),
@@ -487,7 +526,7 @@
             dma((8,)), dma((8,)),
             dma((2, 7)), dma((2, 7)),
             dma((2, 7)), dma((2, 7)),
-            dma((8,)), dma((8,)),
+            dma((9,)), dma((9,)),
             dma((8,)),
         ],
         compiler_params=pltpu.CompilerParams(

time: 113 us -> 107 us (0.947)
  the two profiles are of different devices: /device:TPU:33 before, /device:TPU:4 now
where the time goes in v4:
time: 107 us; the launch traced here: 106 us
  Pallas kernels  101 us (94%)
  local copies, waits for them, and re-layouts  4.98 us (5%)
    pallas_call x1, Pallas kernels, shards(): pl.pallas_call(layer_kernel, out_shape=(sds((32, 1536), BF16), sds((NZ, N...  101 us
    gather x1, local copies, waits for them, and re-layouts, shards(): jnp.take(chand.reshape(128, 1, 8, 2, HD), block_table, axis=0, mode='clip')  3.43 us

profile of v4, /device:TPU:4, one launch (start us, length us, event | category | flops | bytes accessed | tf_op | source)
XLA Modules:
  0.0 106.4 jit_solution(2225400667702941993)
XLA Ops:
  0.6 0.0 copy-start
  0.6 100.7 %layer.1 = (bf16[32,1536]{1,0:T(8,128)(2,1)}, bf16[8,4,4,8,2,128]{5,4,3,2,1,0:T(2,128)(2,1)}, bf16[4,8,4,8,2,128]{5,4,3,2,1,0:T(2,128)(2,1)}) custom-call(bf16[64,768]{1,0:T(8,128)(2,1)} %q_hbm.1, bf16[64,256]{1,0:T(8,128)(2,1)} %k_hbm.1, bf16[64,256]{1,0:T(8,128)(2,1)} %v_hbm.1, s32[64]{0:T(128)} %len_ref.1, bf16[12,768]{1,0:T(8,128)(2,1)} %bitcast.14, ...), custom_call_target="tpu_custom_call" | custom-call | tf_op jit(solution)/shard_map/layer/pallas_call | solution.py:477
  101.4 0.0 copy-done
  101.4 3.4 %gather_fusion = bf16[128,8,2,128]{3,2,1,0:T(2,128)(2,1)} fusion(bf16[128,8,2,128]{3,2,1,0:T(2,128)(2,1)} %bitcast.12, s32[1024]{0:T(1024)S(1)} %pad_clamp_fusion), kind=kCustom, calls=%fused_computation | custom fusion | bytes 1049088 | tf_op jit(solution)/shard_map/jit(_take)/gather | solution.py:540
  104.9 1.5 %copy.18 = bf16[32,1536]{1,0:T(8,128)(2,1)} copy(bf16[32,1536]{1,0:T(8,128)(2,1)} %get-tuple-element.8) | data formatting | bytes 196608
  (1 shorter events, 0.0 us)
Async XLA Ops:
  0.6 100.8 %copy-start = (s32[128]{0:T(128)S(1)}, s32[128]{0:T(128)}, u32[]{:S(2)}) copy-start(s32[128]{0:T(128)} %param.29) | copy-start | bytes 1540

commit v5 on v4

--- a/solution.py
+++ b/solution.py
@@ -19,7 +19,7 @@
 F32 = jnp.float32
 BF16 = jnp.bfloat16
 ZORDER = (1, 7, 2, 6, 3, 5, 4)
-OFF = (0, 1, 7, 4, 2, 6, 3, 5)
+OFF = (0, 3, 5, 4, 1, 7, 2, 6)
 SLOT = {o: k for k, o in enumerate(OFF)}
 ROWS = 24
 COLS = 8 * ROWS
@@ -79,9 +79,9 @@
     sgu_ref, sd_ref, wg_hbm, wd_hbm, cache_hbm,
     out_ref, cmid_ref, chand_ref,
     qbuf, kwin, vwin, resbuf, owpad, owbuf, wc, hbuf, part, rbuf, xb, rpb, shpad, shb, raw, wgb, wdb,
-    relay_g, relay_d, relay_z, dsend, drecv, rsend, rrecv, pz, racc,
+    relay_g, relay_d, relay_x, relay_b, relay_3, relay_4, dsend, drecv, rsend, rrecv, pz, racc,
     kv_s, kv_r, owz_s, owz_r, owx_s, owx_r, rp_s, rp_r, shy_s, shy_r, shx_s, shx_r, cz_s, cz_r, cp_s, cp_r,
-    e1_s, e1_r, e2_s, e2_r, sib_s, sib_r, hy_s, hy_r, rs_s, rs_r, xz_s, xz_r, d_s, d_r, r_s, r_r, z_s, z_r, loc,
+    e1_s, e1_r, e2_s, e2_r, sib_s, sib_r, hy_s, hy_r, rs_s, rs_r, xz_s, xz_r, d_s, d_r, q_s, q_r, r_s, r_r, z_s, z_r, loc,
 ):
     s, h, y, z, x = place()
     seqs = NY * NZ * NX
@@ -148,9 +148,6 @@
         kv.append(go(k_hbm, kwin.at[rows], kv_s.at[0, by - 1], kv_r.at[0, by - 1], ahead[by - 1]))
         kv.append(go(v_hbm, vwin.at[rows], kv_s.at[1, by - 1], kv_r.at[1, by - 1], ahead[by - 1]))
     owz = [go(owpad, owbuf.at[z, x], owz_s.at[d], owz_r.at[d], zdev[d]) for d in ZORDER]
-    rp = [
-        go(rpb.at[0], rpb.at[SLOT[NZ - d]], rp_s.at[d], rp_r.at[d], zdev[d]) for d in ZORDER
-    ]
     shy = [
         go(shpad, shb.at[y, x, h], shy_s.at[d], shy_r.at[d], pdev[(d, 0)]) for d in (1, 3, 2)
     ]
@@ -195,6 +192,9 @@
         d: go(owbuf.at[:, x], owbuf.at[:, x], owx_s.at[d], owx_r.at[d], pdev[(0, d)])
         for d in (1, 3)
     }
+    rp = [
+        go(rpb.at[0], rpb.at[SLOT[NZ - d]], rp_s.at[d], rp_r.at[d], zdev[d]) for d in ZORDER
+    ]
     with jax.named_scope("wait_keys"):
         own_k.wait()
         own_v.wait()
@@ -219,6 +219,8 @@
         go(hbuf.at[y], hbuf.at[y], hy_s.at[d], hy_r.at[d], pdev[(d, 0)]) for d in (1, 3, 2)
     ]
 
+    with jax.named_scope("relay_gate"):
+        ex2 = [second_hop(i, ex1[i]) for i in range(4)]
     with jax.named_scope("gate_up"):
         own_wg.wait()
         wgb[0, 0:768, 0:256] = raw[0, 0:768, 0, :]
@@ -233,8 +235,6 @@
         fwd.append(go(higher, higher, owx_s.at[2], owx_r.at[2], pdev[(0, 3)]))
         for c in shy:
             c.wait_recv()
-    with jax.named_scope("relay_gate"):
-        ex2 = [second_hop(i, ex1[i]) for i in range(2)]
     with jax.named_scope("wait_far_columns"):
         for c in fwd:
             c.wait_recv()
@@ -264,6 +264,7 @@
             )
     rs.append(go(part.at[y, 1 - h], rbuf.at[y, h], rs_s.at[1, 0], rs_r.at[1, 0], sib))
     rbuf[y, h] = part[y, h]
+    ex1 += [first_hop(i) for i in range(4, 6)]
     with jax.named_scope("gate_up_rest"):
         wgb[0, 768:1536, 0:256] = raw[0, 768:1536, 0, :]
         wgb[0, 768:1536, 256:512] = raw[0, 768:1536, 1, :]
@@ -279,9 +280,10 @@
     xz = {
         d: go(xb.at[0], xb.at[SLOT[NZ - d]], xz_s.at[d], xz_r.at[d], zdev[d]) for d in (2, 6, 1, 7)
     }
-    with jax.named_scope("relay"):
-        ex2 += [second_hop(i, ex1[i]) for i in range(2, 4)]
-        ex1 += [first_hop(i) for i in range(4, 6)]
+    with jax.named_scope("gate_sibling"):
+        for c in ex2:
+            c.wait_recv()
+        sib_g = go(raw.at[1, rows_g], raw.at[1, rows_g], sib_s.at[1], sib_r.at[1], sib)
     with jax.named_scope("choose"):
         for c in rp:
             c.wait_recv()
@@ -316,6 +318,8 @@
             xb.at[SLOT[2], high], xb.at[SLOT[4], high], xz_s.at[0], xz_r.at[0], zdev[6]
         )
         xz[5] = go(xb.at[SLOT[2]], xb.at[SLOT[3]], xz_s.at[5], xz_r.at[5], zdev[7])
+        xz[1].wait_recv()
+        xz[7].wait_recv()
 
     turn = 1 + 2 * lax.rem(x, 2)
 
@@ -329,43 +333,58 @@
         return (seq_of(up(y, 3 - 2 * lax.rem(xs, 2), NY), z, xs), h)
 
     hops = [(p, d) for p in range(2) for d in (2, 1, 3, 0) if (p, d) != (0, 0)]
-    sent = []
-    for c in range(2):
-        with jax.named_scope("wait_rows"):
-            for d in ((1, 7, 4, 0), (3, 5))[c]:
-                xz[d].wait_recv()
-        with jax.named_scope("dispatch"):
-            xc = xb[4 * c : 4 * c + 4].reshape(128, 1536)
-            rows = jnp.dot(picks[c], xc, preferred_element_type=F32)
-            for j in range(8):
-                dsend[c, j] = rows[j * ROWS : (j + 1) * ROWS].astype(BF16)
-            sent.append(
-                [
-                    go(
-                        dsend.at[c, p * NX + up(x, d, NX)], drecv.at[c, p * NX + x],
-                        d_s.at[c, i], d_r.at[c, i], to_expert(p, d),
-                    )
-                    for i, (p, d) in enumerate(hops)
-                ]
+    before = pdev[(0, 3)]
+
+    def dispatch(c):
+        xc = xb[4 * c : 4 * c + 4].reshape(128, 1536)
+        rows = jnp.dot(picks[c], xc, preferred_element_type=F32)
+        for j in range(8):
+            dsend[c, j] = rows[j * ROWS : (j + 1) * ROWS].astype(BF16)
+        copies = [go(dsend.at[c, up(x, 2, NX)], relay_x.at[c], q_s.at[c], q_r.at[c], before)]
+        for i, (p, d) in enumerate(hops[1:], 1):
+            copies.append(
+                go(
+                    dsend.at[c, p * NX + up(x, d, NX)], drecv.at[c, p * NX + x],
+                    d_s.at[c, i], d_r.at[c, i], to_expert(p, d),
+                )
             )
-            drecv[c, x] = dsend[c, x]
-        if c == 0:
-            with jax.named_scope("relay_down"):
-                ex2 += [second_hop(i, ex1[i]) for i in range(4, 6)]
-            with jax.named_scope("shared_weights"):
-                for m in shx:
-                    m.wait_recv()
-                sib_sh = go(shb.at[:, :, h], shb.at[:, :, h], sib_s.at[0], sib_r.at[0], sib)
-
+        drecv[c, x] = dsend[c, x]
+        return copies
+
+    def pass_on(c, copies):
+        copies[0].wait_recv()
+        copies[0] = go(
+            relay_x.at[c], drecv.at[c, up(x, 1, NX)], d_s.at[c, 0], d_r.at[c, 0], before
+        )
+
+    sent = {}
+    with jax.named_scope("dispatch"):
+        sent[1] = dispatch(1)
+    with jax.named_scope("relay_down"):
+        ex2 = [second_hop(i, ex1[i]) for i in range(4, 6)]
+    with jax.named_scope("gate_up_other"):
+        sib_g.wait_recv()
+        wgb[1, :, 0:256] = raw[1, :, 0, :]
+        wgb[1, :, 256:512] = raw[1, :, 1, :]
+    with jax.named_scope("pass_on"):
+        pass_on(1, sent[1])
+    with jax.named_scope("wait_rows"):
+        for d in (3, 5, 4, 0):
+            xz[d].wait_recv()
+    with jax.named_scope("dispatch"):
+        sent[0] = dispatch(0)
+    with jax.named_scope("shared_weights"):
+        for m in shx:
+            m.wait_recv()
+        sib_sh = go(shb.at[:, :, h], shb.at[:, :, h], sib_s.at[0], sib_r.at[0], sib)
     cz = [
         go(cache_hbm.at[:, up(z, d, NZ)], cmid_ref.at[z], cz_s.at[d], cz_r.at[d], zdev[d])
         for d in ZORDER
     ]
-    with jax.named_scope("exchange_sibling"):
-        for c in ex2[:4]:
-            c.wait_recv()
-        sib_g = go(raw.at[1, rows_g], raw.at[1, rows_g], sib_s.at[1], sib_r.at[1], sib)
-        for c in ex2[4:]:
+    with jax.named_scope("pass_on"):
+        pass_on(0, sent[0])
+    with jax.named_scope("down_sibling"):
+        for c in ex2:
             c.wait_recv()
         sib_d = go(wdb.at[1, rows_d], wdb.at[1, rows_d], sib_s.at[2], sib_r.at[2], sib)
     with jax.named_scope("shared"):
@@ -379,9 +398,6 @@
         shared = jnp.dot(act, sh, preferred_element_type=F32)
     with jax.named_scope("wait_exchange"):
         own_wd.wait()
-        sib_g.wait_recv()
-        wgb[1, :, 0:256] = raw[1, :, 0, :]
-        wgb[1, :, 256:512] = raw[1, :, 1, :]
         sib_d.wait_recv()
 
     back = []
@@ -399,42 +415,63 @@
                 acc = o if acc is None else acc + o
             for j in range(8):
                 rsend[c, j] = acc[j * ROWS : (j + 1) * ROWS].astype(BF16)
-            back.append(
-                [
+            copies = [
+                go(rsend.at[c, up(x, 2, NX)], relay_b.at[c], q_s.at[2 + c], q_r.at[2 + c], before)
+            ]
+            for i, (p, d) in enumerate(hops[1:], 1):
+                copies.append(
                     go(
                         rsend.at[c, p * NX + up(x, NX - d, NX)], rrecv.at[c, p * NX + x],
                         r_s.at[c, i], r_r.at[c, i], to_source(p, d),
                     )
-                    for i, (p, d) in enumerate(hops)
-                ]
+                )
+            back.append(copies)
+            rrecv[c, x] = rsend[c, x]
+    with jax.named_scope("pass_back"):
+        for c in range(2):
+            back[c][0].wait_recv()
+            back[c][0] = go(
+                relay_b.at[c], rrecv.at[c, up(x, 1, NX)], r_s.at[c, 0], r_r.at[c, 0], before
             )
-            rrecv[c, x] = rsend[c, x]
-    red = []
-    for c in range(2):
-        with jax.named_scope("wait_return"):
-            for m in back[c]:
-                m.wait_recv()
-        with jax.named_scope("combine"):
-            rows = jnp.concatenate([rrecv[c, j].astype(F32) for j in range(8)], axis=0).astype(BF16)
-            tot = shared[128 * c : 128 * c + 128] + jnp.dot(
-                weights[c], rows, preferred_element_type=F32
-            )
-            pz[4 * c : 4 * c + 4] = tot.astype(BF16).reshape(4, 32, 1536)
-            for o in ((1, 7), (3, 5, 2, 6))[c]:
-                red.append(
-                    go(pz.at[SLOT[o]], racc.at[SLOT[NZ - o]], z_s.at[o], z_r.at[o], zdev[o])
-                )
-            if c == 0:
-                by = go(pz.at[SLOT[4], high], relay_z, z_s.at[8], z_r.at[8], zdev[6])
-                red.append(
-                    go(pz.at[SLOT[4], low], racc.at[SLOT[4], low], z_s.at[4], z_r.at[4], zdev[4])
-                )
-        if c == 0:
-            with jax.named_scope("relay_sum"):
-                by.wait_recv()
-                red.append(
-                    go(relay_z, racc.at[SLOT[4], high], z_s.at[0], z_r.at[0], zdev[6])
-                )
+
+    def combined(c):
+        for m in back[c]:
+            m.wait_recv()
+        rows = jnp.concatenate([rrecv[c, j].astype(F32) for j in range(8)], axis=0).astype(BF16)
+        return shared[128 * c : 128 * c + 128] + jnp.dot(
+            weights[c], rows, preferred_element_type=F32
+        )
+
+    with jax.named_scope("combine_far"):
+        pz[0:4] = combined(0).astype(BF16).reshape(4, 32, 1536)
+        far = [
+            go(pz.at[SLOT[3]], relay_3.at[0], z_s.at[0], z_r.at[0], zdev[1]),
+            go(pz.at[SLOT[5]], relay_3.at[1], z_s.at[1], z_r.at[1], zdev[7]),
+            go(pz.at[SLOT[4], low], relay_4.at[0], z_s.at[2], z_r.at[2], zdev[2]),
+            go(pz.at[SLOT[4], high], relay_4.at[1], z_s.at[3], z_r.at[3], zdev[6]),
+        ]
+    with jax.named_scope("combine_near"):
+        tot = combined(1)
+    with jax.named_scope("wait_far"):
+        for m in far:
+            m.wait_recv()
+    with jax.named_scope("add_far"):
+        none = jnp.zeros((16, 1536), F32)
+        plus = (
+            tot[64:96] + relay_3[0].astype(F32)
+            + jnp.concatenate([relay_4[0].astype(F32), none], axis=0)
+        )
+        minus = (
+            tot[96:128] + relay_3[1].astype(F32)
+            + jnp.concatenate([none, relay_4[1].astype(F32)], axis=0)
+        )
+        pz[SLOT[2]] = plus.astype(BF16)
+        pz[SLOT[6]] = minus.astype(BF16)
+        pz[4:6] = tot[0:64].astype(BF16).reshape(2, 32, 1536)
+        red = [
+            go(pz.at[SLOT[o]], racc.at[SLOT[NZ - o] - 3], z_s.at[SLOT[o]], z_r.at[SLOT[o]], zdev[o])
+            for o in (2, 6, 1, 7)
+        ]
     racc[0] = pz[0]
     with jax.named_scope("cache_plane"):
         own_cache.wait()
@@ -452,7 +489,7 @@
         for c in red:
             c.wait_recv()
     out = mixed
-    for j in range(NZ):
+    for j in range(5):
         out = out + racc[j].astype(F32)
     out_ref[...] = out.astype(BF16)
     with jax.named_scope("drain"):
@@ -482,7 +519,7 @@
             sds((NY, NZ, NX, 8, 2, HD), BF16),
         ),
         in_specs=[hbm, hbm, hbm, vmem, vmem, hbm, vmem, vmem, vmem, vmem, vmem, hbm, hbm, hbm],
-        out_specs=(vmem, hbm, vmem),
+        out_specs=(vmem, hbm, hbm),
         scratch_shapes=[
             pltpu.VMEM((64, 768), BF16),
             pltpu.VMEM((320, 256), BF16),
@@ -503,13 +540,16 @@
             pltpu.VMEM((2, 256, 1536), BF16),
             pltpu.VMEM((4, 192, 2, 256), BF16),
             pltpu.VMEM((2, 64, 1536), BF16),
-            pltpu.VMEM((16, 1536), BF16),
+            pltpu.VMEM((2, ROWS, 1536), BF16),
+            pltpu.VMEM((2, ROWS, 1536), BF16),
+            pltpu.VMEM((2, 32, 1536), BF16),
+            pltpu.VMEM((2, 16, 1536), BF16),
             pltpu.VMEM((2, 8, ROWS, 1536), BF16),
             pltpu.VMEM((2, 8, ROWS, 1536), BF16),
             pltpu.VMEM((2, 8, ROWS, 1536), BF16),
             pltpu.VMEM((2, 8, ROWS, 1536), BF16),
             pltpu.VMEM((NZ, 32, 1536), BF16),
-            pltpu.VMEM((NZ, 32, 1536), BF16),
+            pltpu.VMEM((5, 32, 1536), BF16),
             dma((2, 4)), dma((2, 4)),
             dma((8,)), dma((8,)),
             dma((4,)), dma((4,)),
@@ -525,6 +565,7 @@
             dma((2, 4)), dma((2, 4)),
             dma((8,)), dma((8,)),
             dma((2, 7)), dma((2, 7)),
+            dma((4,)), dma((4,)),
             dma((2, 7)), dma((2, 7)),
             dma((9,)), dma((9,)),
             dma((8,)),

time: 107 us -> 114 us (1.065); the launches traced: 106 us -> 112 us
  Pallas kernels: 101 us -> 106 us
    pallas_call x1, Pallas kernels: 101 us -> 106 us  [shards(): pl.pallas_call(layer_kernel, out_shape=(sds((32, 1536), BF16), sds((NZ, N...]
where the time goes in v5:
time: 114 us; the launch traced here: 112 us
  Pallas kernels  106 us (93%)
  local copies, waits for them, and re-layouts  4.98 us (4%)
    pallas_call x1, Pallas kernels, shards(): pl.pallas_call(layer_kernel, out_shape=(sds((32, 1536), BF16), sds((NZ, N...  106 us
    gather x1, local copies, waits for them, and re-layouts, shards(): jnp.take(chand.reshape(128, 1, 8, 2, HD), block_table, axis=0, mode='clip')  3.44 us

profile of v5, /device:TPU:4, one launch (start us, length us, event | category | flops | bytes accessed | tf_op | source)
XLA Modules:
  0.0 111.7 jit_solution(3918320741310324311)
XLA Ops:
  0.6 0.0 copy-start
  0.6 106.0 %layer.1 = (bf16[32,1536]{1,0:T(8,128)(2,1)}, bf16[8,4,4,8,2,128]{5,4,3,2,1,0:T(2,128)(2,1)}, bf16[4,8,4,8,2,128]{5,4,3,2,1,0:T(2,128)(2,1)}) custom-call(bf16[64,768]{1,0:T(8,128)(2,1)} %q_hbm.1, bf16[64,256]{1,0:T(8,128)(2,1)} %k_hbm.1, bf16[64,256]{1,0:T(8,128)(2,1)} %v_hbm.1, s32[64]{0:T(128)} %len_ref.1, bf16[12,768]{1,0:T(8,128)(2,1)} %bitcast.14, ...), custom_call_target="tpu_custom_call" | custom-call | tf_op jit(solution)/shard_map/layer/pallas_call | solution.py:514
  106.7 0.0 copy-done
  106.7 3.4 %gather_fusion = bf16[128,8,2,128]{3,2,1,0:T(2,128)(2,1)} fusion(bf16[128,8,2,128]{3,2,1,0:T(2,128)(2,1)} %bitcast.12, s32[1024]{0:T(1024)S(1)} %pad_clamp_fusion), kind=kCustom, calls=%fused_computation | custom fusion | bytes 1049088 | tf_op jit(solution)/shard_map/jit(_take)/gather | solution.py:581
  110.2 1.5 %copy.18 = bf16[32,1536]{1,0:T(8,128)(2,1)} copy(bf16[32,1536]{1,0:T(8,128)(2,1)} %get-tuple-element.8) | data formatting | bytes 196608
  (1 shorter events, 0.0 us)
Async XLA Ops:
  0.6 106.1 %copy-start = (s32[128]{0:T(128)S(1)}, s32[128]{0:T(128)}, u32[]{:S(2)}) copy-start(s32[128]{0:T(128)} %param.29) | copy-start | bytes 1540

commit v6 on v5

--- a/solution.py
+++ b/solution.py
@@ -142,12 +142,12 @@
         pending.append(copy)
         return copy
 
+    owz = [go(owpad, owbuf.at[z, x], owz_s.at[d], owz_r.at[d], zdev[d]) for d in ZORDER]
     kv = []
     for by in range(1, 5):
         rows = pl.ds(64 * (4 - by), 64)
         kv.append(go(k_hbm, kwin.at[rows], kv_s.at[0, by - 1], kv_r.at[0, by - 1], ahead[by - 1]))
         kv.append(go(v_hbm, vwin.at[rows], kv_s.at[1, by - 1], kv_r.at[1, by - 1], ahead[by - 1]))
-    owz = [go(owpad, owbuf.at[z, x], owz_s.at[d], owz_r.at[d], zdev[d]) for d in ZORDER]
     shy = [
         go(shpad, shb.at[y, x, h], shy_s.at[d], shy_r.at[d], pdev[(d, 0)]) for d in (1, 3, 2)
     ]
@@ -192,9 +192,6 @@
         d: go(owbuf.at[:, x], owbuf.at[:, x], owx_s.at[d], owx_r.at[d], pdev[(0, d)])
         for d in (1, 3)
     }
-    rp = [
-        go(rpb.at[0], rpb.at[SLOT[NZ - d]], rp_s.at[d], rp_r.at[d], zdev[d]) for d in ZORDER
-    ]
     with jax.named_scope("wait_keys"):
         own_k.wait()
         own_v.wait()
@@ -219,8 +216,9 @@
         go(hbuf.at[y], hbuf.at[y], hy_s.at[d], hy_r.at[d], pdev[(d, 0)]) for d in (1, 3, 2)
     ]
 
-    with jax.named_scope("relay_gate"):
-        ex2 = [second_hop(i, ex1[i]) for i in range(4)]
+    rp = [
+        go(rpb.at[0], rpb.at[SLOT[NZ - d]], rp_s.at[d], rp_r.at[d], zdev[d]) for d in ZORDER
+    ]
     with jax.named_scope("gate_up"):
         own_wg.wait()
         wgb[0, 0:768, 0:256] = raw[0, 0:768, 0, :]
@@ -242,6 +240,8 @@
         go(shb.at[:, x, h], shb.at[:, x, h], shx_s.at[d], shx_r.at[d], pdev[(0, d)])
         for d in (1, 3, 2)
     ]
+    with jax.named_scope("relay_gate"):
+        ex2 = [second_hop(i, ex1[i]) for i in range(2)]
     with jax.named_scope("columns"):
         col, row = iota((384, 512), 0), iota((384, 512), 1)
         pick = jnp.where(row == lax.div(col, 12) * 16 + lax.rem(col, 12), 1.0, 0.0).astype(BF16)
@@ -264,7 +264,9 @@
             )
     rs.append(go(part.at[y, 1 - h], rbuf.at[y, h], rs_s.at[1, 0], rs_r.at[1, 0], sib))
     rbuf[y, h] = part[y, h]
-    ex1 += [first_hop(i) for i in range(4, 6)]
+    with jax.named_scope("relay_gate_rest"):
+        ex2 += [second_hop(i, ex1[i]) for i in range(2, 4)]
+        ex1 += [first_hop(i) for i in range(4, 6)]
     with jax.named_scope("gate_up_rest"):
         wgb[0, 768:1536, 0:256] = raw[0, 768:1536, 0, :]
         wgb[0, 768:1536, 256:512] = raw[0, 768:1536, 1, :]
@@ -280,10 +282,6 @@
     xz = {
         d: go(xb.at[0], xb.at[SLOT[NZ - d]], xz_s.at[d], xz_r.at[d], zdev[d]) for d in (2, 6, 1, 7)
     }
-    with jax.named_scope("gate_sibling"):
-        for c in ex2:
-            c.wait_recv()
-        sib_g = go(raw.at[1, rows_g], raw.at[1, rows_g], sib_s.at[1], sib_r.at[1], sib)
     with jax.named_scope("choose"):
         for c in rp:
             c.wait_recv()
@@ -360,12 +358,13 @@
     sent = {}
     with jax.named_scope("dispatch"):
         sent[1] = dispatch(1)
+    ex2g = ex2
+    with jax.named_scope("gate_sibling"):
+        for c in ex2g:
+            c.wait_recv()
+        sib_g = go(raw.at[1, rows_g], raw.at[1, rows_g], sib_s.at[1], sib_r.at[1], sib)
     with jax.named_scope("relay_down"):
         ex2 = [second_hop(i, ex1[i]) for i in range(4, 6)]
-    with jax.named_scope("gate_up_other"):
-        sib_g.wait_recv()
-        wgb[1, :, 0:256] = raw[1, :, 0, :]
-        wgb[1, :, 256:512] = raw[1, :, 1, :]
     with jax.named_scope("pass_on"):
         pass_on(1, sent[1])
     with jax.named_scope("wait_rows"):
@@ -381,6 +380,10 @@
         go(cache_hbm.at[:, up(z, d, NZ)], cmid_ref.at[z], cz_s.at[d], cz_r.at[d], zdev[d])
         for d in ZORDER
     ]
+    with jax.named_scope("gate_up_other"):
+        sib_g.wait_recv()
+        wgb[1, :, 0:256] = raw[1, :, 0, :]
+        wgb[1, :, 256:512] = raw[1, :, 1, :]
     with jax.named_scope("pass_on"):
         pass_on(0, sent[0])
     with jax.named_scope("down_sibling"):
@@ -452,6 +455,26 @@
         ]
     with jax.named_scope("combine_near"):
         tot = combined(1)
+        pz[4:6] = tot[0:64].astype(BF16).reshape(2, 32, 1536)
+
+        def to_line(o):
+            return go(
+                pz.at[SLOT[o]], racc.at[SLOT[NZ - o] - 3], z_s.at[SLOT[o]], z_r.at[SLOT[o]], zdev[o]
+            )
+
+        red = [to_line(1), to_line(7)]
+    with jax.named_scope("cache_plane"):
+        own_cache.wait()
+        for c in cz:
+            c.wait_recv()
+        cp = [
+            go(
+                cmid_ref.at[:, up(y, at[0], NY), up(x, at[1], NX)], chand_ref.at[y, :, x],
+                cp_s.at[i], cp_r.at[i], pdev[at],
+            )
+            for i, at in enumerate(plane)
+        ]
+        cp_own = here(cmid_ref.at[:, y, x], chand_ref.at[y, :, x])
     with jax.named_scope("wait_far"):
         for m in far:
             m.wait_recv()
@@ -467,24 +490,8 @@
         )
         pz[SLOT[2]] = plus.astype(BF16)
         pz[SLOT[6]] = minus.astype(BF16)
-        pz[4:6] = tot[0:64].astype(BF16).reshape(2, 32, 1536)
-        red = [
-            go(pz.at[SLOT[o]], racc.at[SLOT[NZ - o] - 3], z_s.at[SLOT[o]], z_r.at[SLOT[o]], zdev[o])
-            for o in (2, 6, 1, 7)
-        ]
+        red += [to_line(2), to_line(6)]
     racc[0] = pz[0]
-    with jax.named_scope("cache_plane"):
-        own_cache.wait()
-        for c in cz:
-            c.wait_recv()
-        cp = [
-            go(
-                cmid_ref.at[:, up(y, at[0], NY), up(x, at[1], NX)], chand_ref.at[y, :, x],
-                cp_s.at[i], cp_r.at[i], pdev[at],
-            )
-            for i, at in enumerate(plane)
-        ]
-        cp_own = here(cmid_ref.at[:, y, x], chand_ref.at[y, :, x])
     with jax.named_scope("wait_sum"):
         for c in red:
             c.wait_recv()

time: 114 us -> 106 us (0.930)
  Pallas kernels: 106 us -> 98.6 us
    pallas_call x1, Pallas kernels: 106 us -> 98.6 us  [shards(): pl.pallas_call(layer_kernel, out_shape=(sds((32, 1536), BF16), sds((NZ, N...]
where the time goes in v6:
time: 106 us; the launch traced here: 104 us
  Pallas kernels  98.6 us (93%)
  local copies, waits for them, and re-layouts  4.98 us (5%)
    pallas_call x1, Pallas kernels, shards(): pl.pallas_call(layer_kernel, out_shape=(sds((32, 1536), BF16), sds((NZ, N...  98.6 us
    gather x1, local copies, waits for them, and re-layouts, shards(): jnp.take(chand.reshape(128, 1, 8, 2, HD), block_table, axis=0, mode='clip')  3.43 us

profile of v6, /device:TPU:4, one launch (start us, length us, event | category | flops | bytes accessed | tf_op | source)
XLA Modules:
  0.0 104.3 jit_solution(2096340177945109488)
XLA Ops:
  0.6 0.0 copy-start
  0.6 98.6 %layer.1 = (bf16[32,1536]{1,0:T(8,128)(2,1)}, bf16[8,4,4,8,2,128]{5,4,3,2,1,0:T(2,128)(2,1)}, bf16[4,8,4,8,2,128]{5,4,3,2,1,0:T(2,128)(2,1)}) custom-call(bf16[64,768]{1,0:T(8,128)(2,1)} %q_hbm.1, bf16[64,256]{1,0:T(8,128)(2,1)} %k_hbm.1, bf16[64,256]{1,0:T(8,128)(2,1)} %v_hbm.1, s32[64]{0:T(128)} %len_ref.1, bf16[12,768]{1,0:T(8,128)(2,1)} %bitcast.14, ...), custom_call_target="tpu_custom_call" | custom-call | tf_op jit(solution)/shard_map/layer/pallas_call | solution.py:521
  99.3 0.0 copy-done
  99.3 3.4 %gather_fusion = bf16[128,8,2,128]{3,2,1,0:T(2,128)(2,1)} fusion(bf16[128,8,2,128]{3,2,1,0:T(2,128)(2,1)} %bitcast.12, s32[1024]{0:T(1024)S(1)} %pad_clamp_fusion), kind=kCustom, calls=%fused_computation | custom fusion | bytes 1049088 | tf_op jit(solution)/shard_map/jit(_take)/gather | solution.py:588
  102.7 1.5 %copy.18 = bf16[32,1536]{1,0:T(8,128)(2,1)} copy(bf16[32,1536]{1,0:T(8,128)(2,1)} %get-tuple-element.8) | data formatting | bytes 196608
  (1 shorter events, 0.0 us)
Async XLA Ops:
  0.6 98.6 %copy-start = (s32[128]{0:T(128)S(1)}, s32[128]{0:T(128)}, u32[]{:S(2)}) copy-start(s32[128]{0:T(128)} %param.29) | copy-start | bytes 1540

commit v7 on v6

--- a/solution.py
+++ b/solution.py
@@ -22,6 +22,7 @@
 OFF = (0, 3, 5, 4, 1, 7, 2, 6)
 SLOT = {o: k for k, o in enumerate(OFF)}
 ROWS = 24
+POOL = 48
 COLS = 8 * ROWS
 NT = (((1,), (1,)), ((), ()))
 
@@ -80,8 +81,8 @@
     out_ref, cmid_ref, chand_ref,
     qbuf, kwin, vwin, resbuf, owpad, owbuf, wc, hbuf, part, rbuf, xb, rpb, shpad, shb, raw, wgb, wdb,
     relay_g, relay_d, relay_x, relay_b, relay_3, relay_4, dsend, drecv, rsend, rrecv, pz, racc,
-    kv_s, kv_r, owz_s, owz_r, owx_s, owx_r, rp_s, rp_r, shy_s, shy_r, shx_s, shx_r, cz_s, cz_r, cp_s, cp_r,
-    e1_s, e1_r, e2_s, e2_r, sib_s, sib_r, hy_s, hy_r, rs_s, rs_r, xz_s, xz_r, d_s, d_r, q_s, q_r, r_s, r_r, z_s, z_r, loc,
+    pool, kv_r, owz_r, owx_r, rp_r, shy_r, shx_r, cz_r, cp_r, e1_r, e2_r, sib_r, hy_r,
+    rs_r, xz_r, d_r, q_r, r_r, z_r, loc,
 ):
     s, h, y, z, x = place()
     seqs = NY * NZ * NX
@@ -136,20 +137,23 @@
 
     pending = []
 
-    def go(*args):
-        copy = rcopy(*args)
+    def go(src, dst, recv, dev):
+        turn = len(pending)
+        if turn >= POOL:
+            pending[turn - POOL].wait_send()
+        copy = rcopy(src, dst, pool.at[turn % POOL], recv, dev)
         copy.start()
         pending.append(copy)
         return copy
 
-    owz = [go(owpad, owbuf.at[z, x], owz_s.at[d], owz_r.at[d], zdev[d]) for d in ZORDER]
+    owz = [go(owpad, owbuf.at[z, x], owz_r.at[d], zdev[d]) for d in ZORDER]
     kv = []
     for by in range(1, 5):
         rows = pl.ds(64 * (4 - by), 64)
-        kv.append(go(k_hbm, kwin.at[rows], kv_s.at[0, by - 1], kv_r.at[0, by - 1], ahead[by - 1]))
-        kv.append(go(v_hbm, vwin.at[rows], kv_s.at[1, by - 1], kv_r.at[1, by - 1], ahead[by - 1]))
+        kv.append(go(k_hbm, kwin.at[rows], kv_r.at[0, by - 1], ahead[by - 1]))
+        kv.append(go(v_hbm, vwin.at[rows], kv_r.at[1, by - 1], ahead[by - 1]))
     shy = [
-        go(shpad, shb.at[y, x, h], shy_s.at[d], shy_r.at[d], pdev[(d, 0)]) for d in (1, 3, 2)
+        go(shpad, shb.at[y, x, h], shy_r.at[d], pdev[(d, 0)]) for d in (1, 3, 2)
     ]
     sides = (pdev[(1, 0)], pdev[(3, 0)])
     rows_g, rows_d = pl.ds(h * 768, 768), pl.ds(h * 128, 128)
@@ -160,14 +164,14 @@
         return pl.ds(h * 128 + (i - 4) * 64, 64)
 
     def first_hop(i):
-        sem = e1_s.at[i], e1_r.at[i], sides[i % 2]
+        sem = e1_r.at[i], sides[i % 2]
         if i < 4:
             return go(wg_hbm.at[piece(i)], relay_g.at[i], *sem)
         return go(wd_hbm.at[piece(i)], relay_d.at[i - 4], *sem)
 
     def second_hop(i, arrived):
         arrived.wait_recv()
-        sem = e2_s.at[i], e2_r.at[i], sides[i % 2]
+        sem = e2_r.at[i], sides[i % 2]
         if i < 4:
             return go(relay_g.at[i], raw.at[1, piece(i)], *sem)
         return go(relay_d.at[i - 4], wdb.at[1, piece(i)], *sem)
@@ -189,7 +193,7 @@
         for c in owz:
             c.wait_recv()
     owx = {
-        d: go(owbuf.at[:, x], owbuf.at[:, x], owx_s.at[d], owx_r.at[d], pdev[(0, d)])
+        d: go(owbuf.at[:, x], owbuf.at[:, x], owx_r.at[d], pdev[(0, d)])
         for d in (1, 3)
     }
     with jax.named_scope("wait_keys"):
@@ -213,11 +217,11 @@
             for i in range(3):
                 hbuf[y, :, (3 * g + i) * HD : (3 * g + i + 1) * HD] = o[i * 64 : (i + 1) * 64]
     hy = [
-        go(hbuf.at[y], hbuf.at[y], hy_s.at[d], hy_r.at[d], pdev[(d, 0)]) for d in (1, 3, 2)
+        go(hbuf.at[y], hbuf.at[y], hy_r.at[d], pdev[(d, 0)]) for d in (1, 3, 2)
     ]
 
     rp = [
-        go(rpb.at[0], rpb.at[SLOT[NZ - d]], rp_s.at[d], rp_r.at[d], zdev[d]) for d in ZORDER
+        go(rpb.at[0], rpb.at[SLOT[NZ - d]], rp_r.at[d], zdev[d]) for d in ZORDER
     ]
     with jax.named_scope("gate_up"):
         own_wg.wait()
@@ -227,17 +231,17 @@
         left, right = up(x, 3, NX), up(x, 1, NX)
         owx[1].wait_recv()
         lower = owbuf.at[0:4, left]
-        fwd = [go(lower, lower, owx_s.at[0], owx_r.at[0], pdev[(0, 1)])]
+        fwd = [go(lower, lower, owx_r.at[0], pdev[(0, 1)])]
         owx[3].wait_recv()
         higher = owbuf.at[4:8, right]
-        fwd.append(go(higher, higher, owx_s.at[2], owx_r.at[2], pdev[(0, 3)]))
+        fwd.append(go(higher, higher, owx_r.at[2], pdev[(0, 3)]))
         for c in shy:
             c.wait_recv()
     with jax.named_scope("wait_far_columns"):
         for c in fwd:
             c.wait_recv()
     shx = [
-        go(shb.at[:, x, h], shb.at[:, x, h], shx_s.at[d], shx_r.at[d], pdev[(0, d)])
+        go(shb.at[:, x, h], shb.at[:, x, h], shx_r.at[d], pdev[(0, d)])
         for d in (1, 3, 2)
     ]
     with jax.named_scope("relay_gate"):
@@ -260,9 +264,9 @@
         yd = up(y, d, NY)
         for i, hd in enumerate((h, 1 - h)):
             rs.append(
-                go(part.at[yd, hd], rbuf.at[y, h], rs_s.at[i, d], rs_r.at[i, d], (seq_of(yd, z, x), hd))
+                go(part.at[yd, hd], rbuf.at[y, h], rs_r.at[i, d], (seq_of(yd, z, x), hd))
             )
-    rs.append(go(part.at[y, 1 - h], rbuf.at[y, h], rs_s.at[1, 0], rs_r.at[1, 0], sib))
+    rs.append(go(part.at[y, 1 - h], rbuf.at[y, h], rs_r.at[1, 0], sib))
     rbuf[y, h] = part[y, h]
     with jax.named_scope("relay_gate_rest"):
         ex2 += [second_hop(i, ex1[i]) for i in range(2, 4)]
@@ -280,8 +284,13 @@
         ms = jnp.mean(mixed * mixed, axis=-1, keepdims=True)
         xb[0] = (mixed * lax.rsqrt(ms + EPSILON) * gain_ref[...].reshape(1, 1536)).astype(BF16)
     xz = {
-        d: go(xb.at[0], xb.at[SLOT[NZ - d]], xz_s.at[d], xz_r.at[d], zdev[d]) for d in (2, 6, 1, 7)
+        d: go(xb.at[0], xb.at[SLOT[NZ - d]], xz_r.at[d], zdev[d]) for d in (2, 6, 1, 7)
     }
+    ex2g = ex2
+    with jax.named_scope("gate_sibling"):
+        for c in ex2g:
+            c.wait_recv()
+        sib_g = go(raw.at[1, rows_g], raw.at[1, rows_g], sib_r.at[1], sib)
     with jax.named_scope("choose"):
         for c in rp:
             c.wait_recv()
@@ -307,15 +316,15 @@
         xz[2].wait_recv()
         low = pl.ds(0, 16)
         xz[4] = go(
-            xb.at[SLOT[6], low], xb.at[SLOT[4], low], xz_s.at[4], xz_r.at[4], zdev[2]
+            xb.at[SLOT[6], low], xb.at[SLOT[4], low], xz_r.at[4], zdev[2]
         )
-        xz[3] = go(xb.at[SLOT[6]], xb.at[SLOT[5]], xz_s.at[3], xz_r.at[3], zdev[1])
+        xz[3] = go(xb.at[SLOT[6]], xb.at[SLOT[5]], xz_r.at[3], zdev[1])
         xz[6].wait_recv()
         high = pl.ds(16, 16)
         xz[0] = go(
-            xb.at[SLOT[2], high], xb.at[SLOT[4], high], xz_s.at[0], xz_r.at[0], zdev[6]
+            xb.at[SLOT[2], high], xb.at[SLOT[4], high], xz_r.at[0], zdev[6]
         )
-        xz[5] = go(xb.at[SLOT[2]], xb.at[SLOT[3]], xz_s.at[5], xz_r.at[5], zdev[7])
+        xz[5] = go(xb.at[SLOT[2]], xb.at[SLOT[3]], xz_r.at[5], zdev[7])
         xz[1].wait_recv()
         xz[7].wait_recv()
 
@@ -338,12 +347,12 @@
         rows = jnp.dot(picks[c], xc, preferred_element_type=F32)
         for j in range(8):
             dsend[c, j] = rows[j * ROWS : (j + 1) * ROWS].astype(BF16)
-        copies = [go(dsend.at[c, up(x, 2, NX)], relay_x.at[c], q_s.at[c], q_r.at[c], before)]
+        copies = [go(dsend.at[c, up(x, 2, NX)], relay_x.at[c], q_r.at[c], before)]
         for i, (p, d) in enumerate(hops[1:], 1):
             copies.append(
                 go(
                     dsend.at[c, p * NX + up(x, d, NX)], drecv.at[c, p * NX + x],
-                    d_s.at[c, i], d_r.at[c, i], to_expert(p, d),
+                    d_r.at[c, i], to_expert(p, d),
                 )
             )
         drecv[c, x] = dsend[c, x]
@@ -352,19 +361,18 @@
     def pass_on(c, copies):
         copies[0].wait_recv()
         copies[0] = go(
-            relay_x.at[c], drecv.at[c, up(x, 1, NX)], d_s.at[c, 0], d_r.at[c, 0], before
+            relay_x.at[c], drecv.at[c, up(x, 1, NX)], d_r.at[c, 0], before
         )
 
     sent = {}
     with jax.named_scope("dispatch"):
         sent[1] = dispatch(1)
-    ex2g = ex2
-    with jax.named_scope("gate_sibling"):
-        for c in ex2g:
-            c.wait_recv()
-        sib_g = go(raw.at[1, rows_g], raw.at[1, rows_g], sib_s.at[1], sib_r.at[1], sib)
     with jax.named_scope("relay_down"):
         ex2 = [second_hop(i, ex1[i]) for i in range(4, 6)]
+    with jax.named_scope("gate_up_other"):
+        sib_g.wait_recv()
+        wgb[1, :, 0:256] = raw[1, :, 0, :]
+        wgb[1, :, 256:512] = raw[1, :, 1, :]
     with jax.named_scope("pass_on"):
         pass_on(1, sent[1])
     with jax.named_scope("wait_rows"):
@@ -375,21 +383,17 @@
     with jax.named_scope("shared_weights"):
         for m in shx:
             m.wait_recv()
-        sib_sh = go(shb.at[:, :, h], shb.at[:, :, h], sib_s.at[0], sib_r.at[0], sib)
+        sib_sh = go(shb.at[:, :, h], shb.at[:, :, h], sib_r.at[0], sib)
     cz = [
-        go(cache_hbm.at[:, up(z, d, NZ)], cmid_ref.at[z], cz_s.at[d], cz_r.at[d], zdev[d])
+        go(cache_hbm.at[:, up(z, d, NZ)], cmid_ref.at[z], cz_r.at[d], zdev[d])
         for d in ZORDER
     ]
-    with jax.named_scope("gate_up_other"):
-        sib_g.wait_recv()
-        wgb[1, :, 0:256] = raw[1, :, 0, :]
-        wgb[1, :, 256:512] = raw[1, :, 1, :]
     with jax.named_scope("pass_on"):
         pass_on(0, sent[0])
     with jax.named_scope("down_sibling"):
         for c in ex2:
             c.wait_recv()
-        sib_d = go(wdb.at[1, rows_d], wdb.at[1, rows_d], sib_s.at[2], sib_r.at[2], sib)
+        sib_d = go(wdb.at[1, rows_d], wdb.at[1, rows_d], sib_r.at[2], sib)
     with jax.named_scope("shared"):
         sib_sh.wait_recv()
         xs = xb[...].reshape(256, 1536)
@@ -403,8 +407,8 @@
         own_wd.wait()
         sib_d.wait_recv()
 
-    back = []
-    for c in range(2):
+    back = {}
+    for c in (1, 0):
         with jax.named_scope("wait_dispatch"):
             for m in sent[c]:
                 m.wait_recv()
@@ -419,22 +423,22 @@
             for j in range(8):
                 rsend[c, j] = acc[j * ROWS : (j + 1) * ROWS].astype(BF16)
             copies = [
-                go(rsend.at[c, up(x, 2, NX)], relay_b.at[c], q_s.at[2 + c], q_r.at[2 + c], before)
+                go(rsend.at[c, up(x, 2, NX)], relay_b.at[c], q_r.at[2 + c], before)
             ]
             for i, (p, d) in enumerate(hops[1:], 1):
                 copies.append(
                     go(
                         rsend.at[c, p * NX + up(x, NX - d, NX)], rrecv.at[c, p * NX + x],
-                        r_s.at[c, i], r_r.at[c, i], to_source(p, d),
+                        r_r.at[c, i], to_source(p, d),
                     )
                 )
-            back.append(copies)
+            back[c] = copies
             rrecv[c, x] = rsend[c, x]
     with jax.named_scope("pass_back"):
-        for c in range(2):
+        for c in (1, 0):
             back[c][0].wait_recv()
             back[c][0] = go(
-                relay_b.at[c], rrecv.at[c, up(x, 1, NX)], r_s.at[c, 0], r_r.at[c, 0], before
+                relay_b.at[c], rrecv.at[c, up(x, 1, NX)], r_r.at[c, 0], before
             )
 
     def combined(c):
@@ -445,24 +449,24 @@
             weights[c], rows, preferred_element_type=F32
         )
 
+    with jax.named_scope("combine_near"):
+        tot = combined(1)
+        pz[4:6] = tot[0:64].astype(BF16).reshape(2, 32, 1536)
+
+        def to_line(o):
+            return go(
+                pz.at[SLOT[o]], racc.at[SLOT[NZ - o] - 3], z_r.at[SLOT[o]], zdev[o]
+            )
+
+        red = [to_line(1), to_line(7)]
     with jax.named_scope("combine_far"):
         pz[0:4] = combined(0).astype(BF16).reshape(4, 32, 1536)
         far = [
-            go(pz.at[SLOT[3]], relay_3.at[0], z_s.at[0], z_r.at[0], zdev[1]),
-            go(pz.at[SLOT[5]], relay_3.at[1], z_s.at[1], z_r.at[1], zdev[7]),
-            go(pz.at[SLOT[4], low], relay_4.at[0], z_s.at[2], z_r.at[2], zdev[2]),
-            go(pz.at[SLOT[4], high], relay_4.at[1], z_s.at[3], z_r.at[3], zdev[6]),
+            go(pz.at[SLOT[3]], relay_3.at[0], z_r.at[0], zdev[1]),
+            go(pz.at[SLOT[5]], relay_3.at[1], z_r.at[1], zdev[7]),
+            go(pz.at[SLOT[4], low], relay_4.at[0], z_r.at[2], zdev[2]),
+            go(pz.at[SLOT[4], high], relay_4.at[1], z_r.at[3], zdev[6]),
         ]
-    with jax.named_scope("combine_near"):
-        tot = combined(1)
-        pz[4:6] = tot[0:64].astype(BF16).reshape(2, 32, 1536)
-
-        def to_line(o):
-            return go(
-                pz.at[SLOT[o]], racc.at[SLOT[NZ - o] - 3], z_s.at[SLOT[o]], z_r.at[SLOT[o]], zdev[o]
-            )
-
-        red = [to_line(1), to_line(7)]
     with jax.named_scope("cache_plane"):
         own_cache.wait()
         for c in cz:
@@ -470,7 +474,7 @@
         cp = [
             go(
                 cmid_ref.at[:, up(y, at[0], NY), up(x, at[1], NX)], chand_ref.at[y, :, x],
-                cp_s.at[i], cp_r.at[i], pdev[at],
+                cp_r.at[i], pdev[at],
             )
             for i, at in enumerate(plane)
         ]
@@ -503,7 +507,7 @@
         cp_own.wait()
         for c in cp:
             c.wait_recv()
-        for c in pending:
+        for c in pending[-POOL:]:
             c.wait_send()
 
 
@@ -557,24 +561,25 @@
             pltpu.VMEM((2, 8, ROWS, 1536), BF16),
             pltpu.VMEM((NZ, 32, 1536), BF16),
             pltpu.VMEM((5, 32, 1536), BF16),
-            dma((2, 4)), dma((2, 4)),
-            dma((8,)), dma((8,)),
-            dma((4,)), dma((4,)),
-            dma((8,)), dma((8,)),
-            dma((4,)), dma((4,)),
-            dma((4,)), dma((4,)),
-            dma((8,)), dma((8,)),
-            dma((15,)), dma((15,)),
-            dma((6,)), dma((6,)),
-            dma((6,)), dma((6,)),
-            dma((3,)), dma((3,)),
-            dma((4,)), dma((4,)),
-            dma((2, 4)), dma((2, 4)),
-            dma((8,)), dma((8,)),
-            dma((2, 7)), dma((2, 7)),
-            dma((4,)), dma((4,)),
-            dma((2, 7)), dma((2, 7)),
-            dma((9,)), dma((9,)),
+            dma((POOL,)),
+            dma((2, 4)),
+            dma((8,)),
+            dma((4,)),
+            dma((8,)),
+            dma((4,)),
+            dma((4,)),
+            dma((8,)),
+            dma((15,)),
+            dma((6,)),
+            dma((6,)),
+            dma((3,)),
+            dma((4,)),
+            dma((2, 4)),
+            dma((8,)),
+            dma((2, 7)),
+            dma((4,)),
+            dma((2, 7)),
+            dma((9,)),
             dma((8,)),
         ],
         compiler_params=pltpu.CompilerParams(

time: 106 us -> 105 us (level)
  Pallas kernels: 98.6 us -> 96.9 us
    pallas_call x1, Pallas kernels: 98.6 us -> 96.9 us  [shards(): pl.pallas_call(layer_kernel, out_shape=(sds((32, 1536), BF16), sds((NZ, N...]
where the time goes in v7:
time: 105 us; the launch traced here: 103 us
  Pallas kernels  96.9 us (92%)
  local copies, waits for them, and re-layouts  4.98 us (5%)
    pallas_call x1, Pallas kernels, shards(): pl.pallas_call(layer_kernel, out_shape=(sds((32, 1536), BF16), sds((NZ, N...  96.9 us
    gather x1, local copies, waits for them, and re-layouts, shards(): jnp.take(chand.reshape(128, 1, 8, 2, HD), block_table, axis=0, mode='clip')  3.44 us

profile of v7, /device:TPU:4, one launch (start us, length us, event | category | flops | bytes accessed | tf_op | source)
XLA Modules:
  0.0 102.6 jit_solution(16288944721573019792)
XLA Ops:
  0.6 0.0 copy-start
  0.6 96.9 %layer.1 = (bf16[32,1536]{1,0:T(8,128)(2,1)}, bf16[8,4,4,8,2,128]{5,4,3,2,1,0:T(2,128)(2,1)}, bf16[4,8,4,8,2,128]{5,4,3,2,1,0:T(2,128)(2,1)}) custom-call(bf16[64,768]{1,0:T(8,128)(2,1)} %q_hbm.1, bf16[64,256]{1,0:T(8,128)(2,1)} %k_hbm.1, bf16[64,256]{1,0:T(8,128)(2,1)} %v_hbm.1, s32[64]{0:T(128)} %len_ref.1, bf16[12,768]{1,0:T(8,128)(2,1)} %bitcast.14, ...), custom_call_target="tpu_custom_call" | custom-call | tf_op jit(solution)/shard_map/layer/pallas_call | solution.py:525
  97.6 0.0 copy-done
  97.6 3.4 %gather_fusion = bf16[128,8,2,128]{3,2,1,0:T(2,128)(2,1)} fusion(bf16[128,8,2,128]{3,2,1,0:T(2,128)(2,1)} %bitcast.12, s32[1024]{0:T(1024)S(1)} %pad_clamp_fusion), kind=kCustom, calls=%fused_computation | custom fusion | bytes 1049088 | tf_op jit(solution)/shard_map/jit(_take)/gather | solution.py:593
  101.0 1.5 %copy.18 = bf16[32,1536]{1,0:T(8,128)(2,1)} copy(bf16[32,1536]{1,0:T(8,128)(2,1)} %get-tuple-element.8) | data formatting | bytes 196608
  (1 shorter events, 0.0 us)
Async XLA Ops:
  0.6 97.0 %copy-start = (s32[128]{0:T(128)S(1)}, s32[128]{0:T(128)}, u32[]{:S(2)}) copy-start(s32[128]{0:T(128)} %param.29) | copy-start | bytes 1540

commit v8 on v7

--- a/solution.py
+++ b/solution.py
@@ -79,7 +79,7 @@
     q_hbm, k_hbm, v_hbm, len_ref, ow_ref, res_hbm, gain_ref, ids_ref, log_ref,
     sgu_ref, sd_ref, wg_hbm, wd_hbm, cache_hbm,
     out_ref, cmid_ref, chand_ref,
-    qbuf, kwin, vwin, resbuf, owpad, owbuf, wc, hbuf, part, rbuf, xb, rpb, shpad, shb, raw, wgb, wdb,
+    qbuf, kwin, vwin, resbuf, owpad, owbuf, ocol, wc, hbuf, part, rbuf, xb, rpb, shpad, shb, raw, wgb, wdb,
     relay_g, relay_d, relay_x, relay_b, relay_3, relay_4, dsend, drecv, rsend, rrecv, pz, racc,
     pool, kv_r, owz_r, owx_r, rp_r, shy_r, shx_r, cz_r, cp_r, e1_r, e2_r, sib_r, hy_r,
     rs_r, xz_r, d_r, q_r, r_r, z_r, loc,
@@ -120,7 +120,7 @@
         owpad[...] = jnp.concatenate(
             [ow_ref[...].astype(F32), jnp.zeros((4, 768), F32)], axis=0
         ).astype(BF16)
-        owbuf[z, x] = owpad[...]
+        owbuf[z] = owpad[...]
         shpad[...] = jnp.concatenate(
             [
                 sgu_ref[...].astype(F32).reshape(8, 1536),
@@ -146,7 +146,7 @@
         pending.append(copy)
         return copy
 
-    owz = [go(owpad, owbuf.at[z, x], owz_r.at[d], zdev[d]) for d in ZORDER]
+    owz = [go(owpad, owbuf.at[z], owz_r.at[d], zdev[d]) for d in ZORDER]
     kv = []
     for by in range(1, 5):
         rows = pl.ds(64 * (4 - by), 64)
@@ -189,11 +189,16 @@
         seen = jnp.where((kpos >= first) & (kpos <= qcol), 0.0, NEGATIVE)
         seen3 = jnp.concatenate([seen, seen, seen], axis=0)
 
+    col, row = iota((96, 128), 0), iota((96, 128), 1)
+    pack = jnp.where(row == lax.div(col, 12) * 16 + lax.rem(col, 12), 1.0, 0.0).astype(BF16)
     with jax.named_scope("wait_first_columns"):
         for c in owz:
             c.wait_recv()
+    ocol[x] = jnp.dot(
+        pack, owbuf[...].reshape(128, 768), preferred_element_type=F32
+    ).astype(BF16)
     owx = {
-        d: go(owbuf.at[:, x], owbuf.at[:, x], owx_r.at[d], pdev[(0, d)])
+        d: go(ocol.at[x], ocol.at[x], owx_r.at[d], pdev[(0, d)])
         for d in (1, 3)
     }
     with jax.named_scope("wait_keys"):
@@ -230,10 +235,10 @@
     with jax.named_scope("wait_columns"):
         left, right = up(x, 3, NX), up(x, 1, NX)
         owx[1].wait_recv()
-        lower = owbuf.at[0:4, left]
+        lower = ocol.at[left, 0:48]
         fwd = [go(lower, lower, owx_r.at[0], pdev[(0, 1)])]
         owx[3].wait_recv()
-        higher = owbuf.at[4:8, right]
+        higher = ocol.at[right, 48:96]
         fwd.append(go(higher, higher, owx_r.at[2], pdev[(0, 3)]))
         for c in shy:
             c.wait_recv()
@@ -247,10 +252,13 @@
     with jax.named_scope("relay_gate"):
         ex2 = [second_hop(i, ex1[i]) for i in range(2)]
     with jax.named_scope("columns"):
-        col, row = iota((384, 512), 0), iota((384, 512), 1)
-        pick = jnp.where(row == lax.div(col, 12) * 16 + lax.rem(col, 12), 1.0, 0.0).astype(BF16)
+        col, row = iota((384, 384), 0), iota((384, 384), 1)
+        source = (
+            lax.div(lax.rem(col, 48), 12) * 96 + lax.div(col, 48) * 12 + lax.rem(col, 12)
+        )
+        order = jnp.where(row == source, 1.0, 0.0).astype(BF16)
         wc[...] = jnp.dot(
-            pick, owbuf[...].reshape(512, 768), preferred_element_type=F32
+            order, ocol[...].reshape(384, 768), preferred_element_type=F32
         ).astype(BF16)
 
     with jax.named_scope("wait_heads"):
@@ -388,12 +396,6 @@
         go(cache_hbm.at[:, up(z, d, NZ)], cmid_ref.at[z], cz_r.at[d], zdev[d])
         for d in ZORDER
     ]
-    with jax.named_scope("pass_on"):
-        pass_on(0, sent[0])
-    with jax.named_scope("down_sibling"):
-        for c in ex2:
-            c.wait_recv()
-        sib_d = go(wdb.at[1, rows_d], wdb.at[1, rows_d], sib_r.at[2], sib)
     with jax.named_scope("shared"):
         sib_sh.wait_recv()
         xs = xb[...].reshape(256, 1536)
@@ -403,12 +405,19 @@
         live = lax.rem(lax.div(iota((256, 512), 1), 4), 4) == 2
         act = jnp.where(live, act, 0.0).astype(BF16)
         shared = jnp.dot(act, sh, preferred_element_type=F32)
+    with jax.named_scope("down_sibling"):
+        for c in ex2:
+            c.wait_recv()
+        sib_d = go(wdb.at[1, rows_d], wdb.at[1, rows_d], sib_r.at[2], sib)
     with jax.named_scope("wait_exchange"):
         own_wd.wait()
         sib_d.wait_recv()
 
     back = {}
     for c in (1, 0):
+        if c == 0:
+            with jax.named_scope("pass_on"):
+                pass_on(0, sent[0])
         with jax.named_scope("wait_dispatch"):
             for m in sent[c]:
                 m.wait_recv()
@@ -457,8 +466,6 @@
             return go(
                 pz.at[SLOT[o]], racc.at[SLOT[NZ - o] - 3], z_r.at[SLOT[o]], zdev[o]
             )
-
-        red = [to_line(1), to_line(7)]
     with jax.named_scope("combine_far"):
         pz[0:4] = combined(0).astype(BF16).reshape(4, 32, 1536)
         far = [
@@ -467,6 +474,7 @@
             go(pz.at[SLOT[4], low], relay_4.at[0], z_r.at[2], zdev[2]),
             go(pz.at[SLOT[4], high], relay_4.at[1], z_r.at[3], zdev[6]),
         ]
+        red = [to_line(1), to_line(7)]
     with jax.named_scope("cache_plane"):
         own_cache.wait()
         for c in cz:
@@ -502,7 +510,7 @@
     out = mixed
     for j in range(5):
         out = out + racc[j].astype(F32)
-    out_ref[...] = out.astype(BF16)
+    out_ref[...] = out
     with jax.named_scope("drain"):
         cp_own.wait()
         for c in cp:
@@ -525,7 +533,7 @@
     layer_out, _, chand = pl.pallas_call(
         layer_kernel,
         out_shape=(
-            sds((32, 1536), BF16),
+            sds((32, 1536), F32),
             sds((NZ, NY, NX, 8, 2, HD), BF16),
             sds((NY, NZ, NX, 8, 2, HD), BF16),
         ),
@@ -537,7 +545,8 @@
             pltpu.VMEM((320, 256), BF16),
             pltpu.VMEM((32, 1536), BF16),
             pltpu.VMEM((16, 768), BF16),
-            pltpu.VMEM((NZ, NX, 16, 768), BF16),
+            pltpu.VMEM((NZ, 16, 768), BF16),
+            pltpu.VMEM((NX, 96, 768), BF16),
             pltpu.VMEM((384, 768), BF16),
             pltpu.VMEM((NY, 64, 768), BF16),
             pltpu.VMEM((NY, 2, 32, 384), BF16),
@@ -593,7 +602,7 @@
     cache_out = jnp.take(
         chand.reshape(128, 1, 8, 2, HD), block_table, axis=0, mode="clip"
     )
-    return layer_out, cache_out
+    return layer_out.astype(BF16), cache_out
 
 
 def solution(mesh):

time: 105 us -> 107 us (1.019); the launches traced: 103 us -> 107 us
  Pallas kernels: 96.9 us -> 101 us
  other arithmetic: 0.01 us -> 1.58 us
  local copies, waits for them, and re-layouts: 4.98 us -> 3.44 us
    pallas_call x1, Pallas kernels: 96.9 us -> 101 us  [shards(): pl.pallas_call(layer_kernel, out_shape=(sds((32, 1536), F32), sds((NZ, NY...]
    convert_element_type x0 -> x1, other arithmetic: none -> 1.58 us  [shards(): return (layer_out.astype(BF16), cache_out)]
    unnamed x3 -> x2, local copies, waits for them, and re-layouts: 1.54 us -> 0.01 us
where the time goes in v8:
time: 107 us
  Pallas kernels  101 us (94%)
  local copies, waits for them, and re-layouts  3.44 us (3%)
  other arithmetic  1.58 us (1%)
    pallas_call x1, Pallas kernels, shards(): pl.pallas_call(layer_kernel, out_shape=(sds((32, 1536), F32), sds((NZ, NY...  101 us
    gather x1, local copies, waits for them, and re-layouts, shards(): jnp.take(chand.reshape(128, 1, 8, 2, HD), block_table, axis=0, mode='clip')  3.44 us

profile of v8, /device:TPU:4, one launch (start us, length us, event | category | flops | bytes accessed | tf_op | source)
XLA Modules:
  0.0 106.7 jit_solution(1821613703829166614)
XLA Ops:
  0.6 0.0 copy-start
  0.6 101.1 %layer.1 = (f32[32,1536]{1,0:T(8,128)}, bf16[8,4,4,8,2,128]{5,4,3,2,1,0:T(2,128)(2,1)}, bf16[4,8,4,8,2,128]{5,4,3,2,1,0:T(2,128)(2,1)}) custom-call(bf16[64,768]{1,0:T(8,128)(2,1)} %q_hbm.1, bf16[64,256]{1,0:T(8,128)(2,1)} %k_hbm.1, bf16[64,256]{1,0:T(8,128)(2,1)} %v_hbm.1, s32[64]{0:T(128)} %len_ref.1, bf16[12,768]{1,0:T(8,128)(2,1)} %bitcast.14, ...), custom_call_target="tpu_custom_call" | custom-call | tf_op jit(solution)/shard_map/layer/pallas_call | solution.py:533
  101.7 1.6 %convert_element_type.3 = bf16[32,1536]{1,0:T(8,128)(2,1)} convert(f32[32,1536]{1,0:T(8,128)} %get-tuple-element.4) | non-fusion elementwise | flops 49152 | bytes 294912 | tf_op jit(solution)/shard_map/convert_element_type | solution.py:605
  103.3 0.0 copy-done
  103.3 3.4 %gather_fusion = bf16[128,8,2,128]{3,2,1,0:T(2,128)(2,1)} fusion(bf16[128,8,2,128]{3,2,1,0:T(2,128)(2,1)} %bitcast.12, s32[1024]{0:T(1024)S(1)} %pad_clamp_fusion), kind=kCustom, calls=%fused_computation | custom fusion | bytes 1049088 | tf_op jit(solution)/shard_map/jit(_take)/gather | solution.py:602
  (1 shorter events, 0.0 us)
Async XLA Ops:
  0.6 102.7 %copy-start = (s32[128]{0:T(128)S(1)}, s32[128]{0:T(128)}, u32[]{:S(2)}) copy-start(s32[128]{0:T(128)} %param.29) | copy-start | bytes 1540

commit v9 on v8

--- a/solution.py
+++ b/solution.py
@@ -228,6 +228,10 @@
     rp = [
         go(rpb.at[0], rpb.at[SLOT[NZ - d]], rp_r.at[d], zdev[d]) for d in ZORDER
     ]
+    cz = [
+        go(cache_hbm.at[:, up(z, d, NZ)], cmid_ref.at[z], cz_r.at[d], zdev[d])
+        for d in ZORDER
+    ]
     with jax.named_scope("gate_up"):
         own_wg.wait()
         wgb[0, 0:768, 0:256] = raw[0, 0:768, 0, :]
@@ -295,6 +299,18 @@
         d: go(xb.at[0], xb.at[SLOT[NZ - d]], xz_r.at[d], zdev[d]) for d in (2, 6, 1, 7)
     }
     ex2g = ex2
+    with jax.named_scope("cache_plane"):
+        own_cache.wait()
+        for c in cz:
+            c.wait_recv()
+        cp = [
+            go(
+                cmid_ref.at[:, up(y, at[0], NY), up(x, at[1], NX)], chand_ref.at[y, :, x],
+                cp_r.at[i], pdev[at],
+            )
+            for i, at in enumerate(plane)
+        ]
+        cp_own = here(cmid_ref.at[:, y, x], chand_ref.at[y, :, x])
     with jax.named_scope("gate_sibling"):
         for c in ex2g:
             c.wait_recv()
@@ -392,10 +408,6 @@
         for m in shx:
             m.wait_recv()
         sib_sh = go(shb.at[:, :, h], shb.at[:, :, h], sib_r.at[0], sib)
-    cz = [
-        go(cache_hbm.at[:, up(z, d, NZ)], cmid_ref.at[z], cz_r.at[d], zdev[d])
-        for d in ZORDER
-    ]
     with jax.named_scope("shared"):
         sib_sh.wait_recv()
         xs = xb[...].reshape(256, 1536)
@@ -405,6 +417,8 @@
         live = lax.rem(lax.div(iota((256, 512), 1), 4), 4) == 2
         act = jnp.where(live, act, 0.0).astype(BF16)
         shared = jnp.dot(act, sh, preferred_element_type=F32)
+    with jax.named_scope("pass_on"):
+        pass_on(0, sent[0])
     with jax.named_scope("down_sibling"):
         for c in ex2:
             c.wait_recv()
@@ -413,42 +427,44 @@
         own_wd.wait()
         sib_d.wait_recv()
 
+    def experts(c):
+        for m in sent[c]:
+            m.wait_recv()
+        rows = jnp.concatenate([drecv[c, j].astype(F32) for j in range(8)], axis=0).astype(BF16)
+        acc = None
+        for j in range(2):
+            gu = jnp.dot(rows, wgb[j], preferred_element_type=F32)
+            a = (silu(gu[:, :256]) * gu[:, 256:]).astype(BF16)
+            o = jnp.dot(a, wdb[j], preferred_element_type=F32)
+            acc = o if acc is None else acc + o
+        for j in range(8):
+            rsend[c, j] = acc[j * ROWS : (j + 1) * ROWS].astype(BF16)
+        rrecv[c, x] = rsend[c, x]
+
+    def give_back(c):
+        copies = [go(rsend.at[c, up(x, 2, NX)], relay_b.at[c], q_r.at[2 + c], before)]
+        for i, (p, d) in enumerate(hops[1:], 1):
+            copies.append(
+                go(
+                    rsend.at[c, p * NX + up(x, NX - d, NX)], rrecv.at[c, p * NX + x],
+                    r_r.at[c, i], to_source(p, d),
+                )
+            )
+        return copies
+
+    def pass_back(c, copies):
+        copies[0].wait_recv()
+        copies[0] = go(relay_b.at[c], rrecv.at[c, up(x, 1, NX)], r_r.at[c, 0], before)
+
     back = {}
-    for c in (1, 0):
-        if c == 0:
-            with jax.named_scope("pass_on"):
-                pass_on(0, sent[0])
-        with jax.named_scope("wait_dispatch"):
-            for m in sent[c]:
-                m.wait_recv()
-        with jax.named_scope("experts"):
-            rows = jnp.concatenate([drecv[c, j].astype(F32) for j in range(8)], axis=0).astype(BF16)
-            acc = None
-            for j in range(2):
-                gu = jnp.dot(rows, wgb[j], preferred_element_type=F32)
-                a = (silu(gu[:, :256]) * gu[:, 256:]).astype(BF16)
-                o = jnp.dot(a, wdb[j], preferred_element_type=F32)
-                acc = o if acc is None else acc + o
-            for j in range(8):
-                rsend[c, j] = acc[j * ROWS : (j + 1) * ROWS].astype(BF16)
-            copies = [
-                go(rsend.at[c, up(x, 2, NX)], relay_b.at[c], q_r.at[2 + c], before)
-            ]
-            for i, (p, d) in enumerate(hops[1:], 1):
-                copies.append(
-                    go(
-                        rsend.at[c, p * NX + up(x, NX - d, NX)], rrecv.at[c, p * NX + x],
-                        r_r.at[c, i], to_source(p, d),
-                    )
-                )
-            back[c] = copies
-            rrecv[c, x] = rsend[c, x]
-    with jax.named_scope("pass_back"):
-        for c in (1, 0):
-            back[c][0].wait_recv()
-            back[c][0] = go(
-                relay_b.at[c], rrecv.at[c, up(x, 1, NX)], r_r.at[c, 0], before
-            )
+    with jax.named_scope("experts_near"):
+        experts(1)
+    with jax.named_scope("experts_far"):
+        experts(0)
+        back[0] = give_back(0)
+    with jax.named_scope("pass_back_far"):
+        pass_back(0, back[0])
+        back[1] = give_back(1)
 
     def combined(c):
         for m in back[c]:
@@ -458,14 +474,6 @@
             weights[c], rows, preferred_element_type=F32
         )
 
-    with jax.named_scope("combine_near"):
-        tot = combined(1)
-        pz[4:6] = tot[0:64].astype(BF16).reshape(2, 32, 1536)
-
-        def to_line(o):
-            return go(
-                pz.at[SLOT[o]], racc.at[SLOT[NZ - o] - 3], z_r.at[SLOT[o]], zdev[o]
-            )
     with jax.named_scope("combine_far"):
         pz[0:4] = combined(0).astype(BF16).reshape(4, 32, 1536)
         far = [
@@ -474,19 +482,16 @@
             go(pz.at[SLOT[4], low], relay_4.at[0], z_r.at[2], zdev[2]),
             go(pz.at[SLOT[4], high], relay_4.at[1], z_r.at[3], zdev[6]),
         ]
-        red = [to_line(1), to_line(7)]
-    with jax.named_scope("cache_plane"):
-        own_cache.wait()
-        for c in cz:
-            c.wait_recv()
-        cp = [
-            go(
-                cmid_ref.at[:, up(y, at[0], NY), up(x, at[1], NX)], chand_ref.at[y, :, x],
-                cp_r.at[i], pdev[at],
+    with jax.named_scope("pass_back_near"):
+        pass_back(1, back[1])
+    with jax.named_scope("combine_near"):
+        tot = combined(1)
+        pz[4:6] = tot[0:64].astype(BF16).reshape(2, 32, 1536)
+
+        def to_line(o):
+            return go(
+                pz.at[SLOT[o]], racc.at[SLOT[NZ - o] - 3], z_r.at[SLOT[o]], zdev[o]
             )
-            for i, at in enumerate(plane)
-        ]
-        cp_own = here(cmid_ref.at[:, y, x], chand_ref.at[y, :, x])
     with jax.named_scope("wait_far"):
         for m in far:
             m.wait_recv()
@@ -502,7 +507,7 @@
         )
         pz[SLOT[2]] = plus.astype(BF16)
         pz[SLOT[6]] = minus.astype(BF16)
-        red += [to_line(2), to_line(6)]
+        red = [to_line(2), to_line(6), to_line(1), to_line(7)]
     racc[0] = pz[0]
     with jax.named_scope("wait_sum"):
         for c in red:
@@ -510,7 +515,7 @@
     out = mixed
     for j in range(5):
         out = out + racc[j].astype(F32)
-    out_ref[...] = out
+    out_ref[...] = out.astype(BF16)
     with jax.named_scope("drain"):
         cp_own.wait()
         for c in cp:
@@ -533,7 +538,7 @@
     layer_out, _, chand = pl.pallas_call(
         layer_kernel,
         out_shape=(
-            sds((32, 1536), F32),
+            sds((32, 1536), BF16),
             sds((NZ, NY, NX, 8, 2, HD), BF16),
             sds((NY, NZ, NX, 8, 2, HD), BF16),
         ),
@@ -602,7 +607,7 @@
     cache_out = jnp.take(
         chand.reshape(128, 1, 8, 2, HD), block_table, axis=0, mode="clip"
     )
-    return layer_out.astype(BF16), cache_out
+    return layer_out, cache_out
 
 
 def solution(mesh):

time: 107 us -> 102 us (0.953)
  Pallas kernels: 101 us -> 96.4 us
  other arithmetic: 1.58 us -> 0.01 us
  local copies, waits for them, and re-layouts: 3.44 us -> 4.98 us
    pallas_call x1, Pallas kernels: 101 us -> 96.4 us  [shards(): pl.pallas_call(layer_kernel, out_shape=(sds((32, 1536), BF16), sds((NZ, N...]
    convert_element_type x1 -> x0, other arithmetic: 1.58 us -> none  [shards(): return (layer_out.astype(BF16), cache_out)]
    unnamed x2 -> x3, local copies, waits for them, and re-layouts: 0.01 us -> 1.54 us
where the time goes in v9:
time: 102 us
  Pallas kernels  96.4 us (95%)
  local copies, waits for them, and re-layouts  4.98 us (5%)
    pallas_call x1, Pallas kernels, shards(): pl.pallas_call(layer_kernel, out_shape=(sds((32, 1536), BF16), sds((NZ, N...  96.4 us
    gather x1, local copies, waits for them, and re-layouts, shards(): jnp.take(chand.reshape(128, 1, 8, 2, HD), block_table, axis=0, mode='clip')  3.43 us

profile of v9, /device:TPU:4, one launch (start us, length us, event | category | flops | bytes accessed | tf_op | source)
XLA Modules:
  0.0 102.0 jit_solution(6182086872979222153)
XLA Ops:
  0.6 0.0 copy-start
  0.6 96.4 %layer.1 = (bf16[32,1536]{1,0:T(8,128)(2,1)}, bf16[8,4,4,8,2,128]{5,4,3,2,1,0:T(2,128)(2,1)}, bf16[4,8,4,8,2,128]{5,4,3,2,1,0:T(2,128)(2,1)}) custom-call(bf16[64,768]{1,0:T(8,128)(2,1)} %q_hbm.1, bf16[64,256]{1,0:T(8,128)(2,1)} %k_hbm.1, bf16[64,256]{1,0:T(8,128)(2,1)} %v_hbm.1, s32[64]{0:T(128)} %len_ref.1, bf16[12,768]{1,0:T(8,128)(2,1)} %bitcast.14, ...), custom_call_target="tpu_custom_call" | custom-call | tf_op jit(solution)/shard_map/layer/pallas_call | solution.py:538
  97.0 0.0 copy-done
  97.1 3.4 %gather_fusion = bf16[128,8,2,128]{3,2,1,0:T(2,128)(2,1)} fusion(bf16[128,8,2,128]{3,2,1,0:T(2,128)(2,1)} %bitcast.12, s32[1024]{0:T(1024)S(1)} %pad_clamp_fusion), kind=kCustom, calls=%fused_computation | custom fusion | bytes 1049088 | tf_op jit(solution)/shard_map/jit(_take)/gather | solution.py:607
  100.5 1.5 %copy.18 = bf16[32,1536]{1,0:T(8,128)(2,1)} copy(bf16[32,1536]{1,0:T(8,128)(2,1)} %get-tuple-element.8) | data formatting | bytes 196608
  (1 shorter events, 0.0 us)
Async XLA Ops:
  0.6 96.4 %copy-start = (s32[128]{0:T(128)S(1)}, s32[128]{0:T(128)}, u32[]{:S(2)}) copy-start(s32[128]{0:T(128)} %param.29) | copy-start | bytes 1540

commit v10 on v9

--- a/solution.py
+++ b/solution.py
@@ -77,10 +77,10 @@
 
 def layer_kernel(
     q_hbm, k_hbm, v_hbm, len_ref, ow_ref, res_hbm, gain_ref, ids_ref, log_ref,
-    sgu_ref, sd_ref, wg_hbm, wd_hbm, cache_hbm,
-    out_ref, cmid_ref, chand_ref,
+    sgu_ref, sd_ref, wg_hbm, wd_hbm, cache_hbm, table_ref,
+    out_ref, cmid_ref, cache_ref,
     qbuf, kwin, vwin, resbuf, owpad, owbuf, ocol, wc, hbuf, part, rbuf, xb, rpb, shpad, shb, raw, wgb, wdb,
-    relay_g, relay_d, relay_x, relay_b, relay_3, relay_4, dsend, drecv, rsend, rrecv, pz, racc,
+    chand_ref, taken, relay_g, relay_d, relay_x, relay_b, relay_3, relay_4, dsend, drecv, rsend, rrecv, pz, racc,
     pool, kv_r, owz_r, owx_r, rp_r, shy_r, shx_r, cz_r, cp_r, e1_r, e2_r, sib_r, hy_r,
     rs_r, xz_r, d_r, q_r, r_r, z_r, loc,
 ):
@@ -391,12 +391,12 @@
     sent = {}
     with jax.named_scope("dispatch"):
         sent[1] = dispatch(1)
-    with jax.named_scope("relay_down"):
-        ex2 = [second_hop(i, ex1[i]) for i in range(4, 6)]
     with jax.named_scope("gate_up_other"):
         sib_g.wait_recv()
         wgb[1, :, 0:256] = raw[1, :, 0, :]
         wgb[1, :, 256:512] = raw[1, :, 1, :]
+    with jax.named_scope("relay_down"):
+        ex2 = [second_hop(i, ex1[i]) for i in range(4, 6)]
     with jax.named_scope("pass_on"):
         pass_on(1, sent[1])
     with jax.named_scope("wait_rows"):
@@ -466,6 +466,19 @@
         pass_back(0, back[0])
         back[1] = give_back(1)
 
+    with jax.named_scope("cache_order"):
+        cp_own.wait()
+        for c in cp:
+            c.wait_recv()
+
+        def take(b, carry):
+            i = table_ref[b]
+            taken[b] = chand_ref[lax.div(i, 32), lax.rem(lax.div(i, 4), 8), lax.rem(i, 4)]
+            return carry
+
+        lax.fori_loop(0, 128, take, 0)
+        taken_out = here(taken, cache_ref)
+
     def combined(c):
         for m in back[c]:
             m.wait_recv()
@@ -517,9 +530,7 @@
         out = out + racc[j].astype(F32)
     out_ref[...] = out.astype(BF16)
     with jax.named_scope("drain"):
-        cp_own.wait()
-        for c in cp:
-            c.wait_recv()
+        taken_out.wait()
         for c in pending[-POOL:]:
             c.wait_send()
 
@@ -529,20 +540,21 @@
     route_logits, shared_gate_up, shared_down, expert_gate_up, expert_down, cache_blocks, block_table,
 ):
     hbm, vmem = pl.BlockSpec(memory_space=pltpu.HBM), pl.BlockSpec(memory_space=pltpu.VMEM)
+    smem = pl.BlockSpec(memory_space=pltpu.SMEM)
     dma = pltpu.SemaphoreType.DMA
     sgu = jnp.transpose(shared_gate_up, (1, 2, 0))
     wg = expert_gate_up.reshape(1536, 2, 256)
     wd = expert_down.reshape(256, 1536)
     cache = cache_blocks.reshape(NY, NZ, NX, 8, 2, HD)
     sds = jax.ShapeDtypeStruct
-    layer_out, _, chand = pl.pallas_call(
+    layer_out, _, taken = pl.pallas_call(
         layer_kernel,
         out_shape=(
             sds((32, 1536), BF16),
             sds((NZ, NY, NX, 8, 2, HD), BF16),
-            sds((NY, NZ, NX, 8, 2, HD), BF16),
+            sds((128, 8, 2, HD), BF16),
         ),
-        in_specs=[hbm, hbm, hbm, vmem, vmem, hbm, vmem, vmem, vmem, vmem, vmem, hbm, hbm, hbm],
+        in_specs=[hbm, hbm, hbm, vmem, vmem, hbm, vmem, vmem, vmem, vmem, vmem, hbm, hbm, hbm, smem],
         out_specs=(vmem, hbm, hbm),
         scratch_shapes=[
             pltpu.VMEM((64, 768), BF16),
@@ -563,6 +575,8 @@
             pltpu.VMEM((2, 1536, 2, 256), BF16),
             pltpu.VMEM((2, 1536, 512), BF16),
             pltpu.VMEM((2, 256, 1536), BF16),
+            pltpu.VMEM((NY, NZ, NX, 8, 2, HD), BF16),
+            pltpu.VMEM((128, 8, 2, HD), BF16),
             pltpu.VMEM((4, 192, 2, 256), BF16),
             pltpu.VMEM((2, 64, 1536), BF16),
             pltpu.VMEM((2, ROWS, 1536), BF16),
@@ -594,7 +608,7 @@
             dma((4,)),
             dma((2, 7)),
             dma((9,)),
-            dma((8,)),
+            dma((9,)),
         ],
         compiler_params=pltpu.CompilerParams(
             collective_id=0, has_side_effects=True, vmem_limit_bytes=56 << 20
@@ -602,11 +616,9 @@
         name="layer",
     )(
         queries, key_vectors, value_vectors, lengths, out_weight.T, residual, norm_gain,
-        route_ids.T, route_logits.T, sgu, shared_down, wg, wd, cache,
+        route_ids.T, route_logits.T, sgu, shared_down, wg, wd, cache, block_table,
     )
-    cache_out = jnp.take(
-        chand.reshape(128, 1, 8, 2, HD), block_table, axis=0, mode="clip"
-    )
+    cache_out = taken.reshape(128, 1, 8, 2, HD)
     return layer_out, cache_out
 
 

time: 102 us -> 100 us (0.980)
  Pallas kernels: 96.4 us -> 94.9 us
  local copies, waits for them, and re-layouts: 4.98 us -> 3.73 us
    gather x1 -> x0, local copies, waits for them, and re-layouts: 3.43 us -> none  [shards(): jnp.take(chand.reshape(128, 1, 8, 2, HD), block_table, axis=0, mode='clip')]
    unnamed x3 -> x2, local copies, waits for them, and re-layouts: 1.54 us -> 3.73 us
    pallas_call x1, Pallas kernels: 96.4 us -> 94.9 us  [shards(): pl.pallas_call(layer_kernel, out_shape=(sds((32, 1536), BF16), sds((NZ, N...]
where the time goes in v10:
time: 100 us; the launch traced here: 99.3 us
  Pallas kernels  94.9 us (95%)
  local copies, waits for them, and re-layouts  3.73 us (4%)
    pallas_call x1, Pallas kernels, shards(): pl.pallas_call(layer_kernel, out_shape=(sds((32, 1536), BF16), sds((NZ, N...  94.9 us
    unnamed x2, local copies, waits for them, and re-layouts  3.73 us

profile of v10, /device:TPU:4, one launch (start us, length us, event | category | flops | bytes accessed | tf_op | source)
XLA Modules:
  0.0 99.3 jit_solution(12364760204850271740)
XLA Ops:
  0.6 94.9 %layer.1 = (bf16[32,1536]{1,0:T(8,128)(2,1)}, bf16[8,4,4,8,2,128]{5,4,3,2,1,0:T(2,128)(2,1)}, bf16[128,8,2,128]{3,2,1,0:T(2,128)(2,1)}) custom-call(bf16[64,768]{1,0:T(8,128)(2,1)} %q_hbm.1, bf16[64,256]{1,0:T(8,128)(2,1)} %k_hbm.1, bf16[64,256]{1,0:T(8,128)(2,1)} %v_hbm.1, s32[64]{0:T(128)} %len_ref.1, bf16[12,768]{1,0:T(8,128)(2,1)} %bitcast.14, ...), custom_call_target="tpu_custom_call" | custom-call | tf_op jit(solution)/shard_map/layer/pallas_call | solution.py:550
  95.6 1.5 %copy.20 = bf16[32,1536]{1,0:T(8,128)(2,1)} copy(bf16[32,1536]{1,0:T(8,128)(2,1)} %get-tuple-element.10) | data formatting | bytes 196608
  97.1 2.2 %copy.21 = bf16[128,1,8,2,128]{4,3,2,1,0:T(2,128)(2,1)} copy(bf16[128,1,8,2,128]{4,3,2,1,0:T(2,128)(2,1)} %bitcast.12) | data formatting | bytes 1048576

commit v11 on v10

--- a/solution.py
+++ b/solution.py
@@ -298,7 +298,6 @@
     xz = {
         d: go(xb.at[0], xb.at[SLOT[NZ - d]], xz_r.at[d], zdev[d]) for d in (2, 6, 1, 7)
     }
-    ex2g = ex2
     with jax.named_scope("cache_plane"):
         own_cache.wait()
         for c in cz:
@@ -311,10 +310,6 @@
             for i, at in enumerate(plane)
         ]
         cp_own = here(cmid_ref.at[:, y, x], chand_ref.at[y, :, x])
-    with jax.named_scope("gate_sibling"):
-        for c in ex2g:
-            c.wait_recv()
-        sib_g = go(raw.at[1, rows_g], raw.at[1, rows_g], sib_r.at[1], sib)
     with jax.named_scope("choose"):
         for c in rp:
             c.wait_recv()
@@ -391,12 +386,6 @@
     sent = {}
     with jax.named_scope("dispatch"):
         sent[1] = dispatch(1)
-    with jax.named_scope("gate_up_other"):
-        sib_g.wait_recv()
-        wgb[1, :, 0:256] = raw[1, :, 0, :]
-        wgb[1, :, 256:512] = raw[1, :, 1, :]
-    with jax.named_scope("relay_down"):
-        ex2 = [second_hop(i, ex1[i]) for i in range(4, 6)]
     with jax.named_scope("pass_on"):
         pass_on(1, sent[1])
     with jax.named_scope("wait_rows"):
@@ -404,6 +393,13 @@
             xz[d].wait_recv()
     with jax.named_scope("dispatch"):
         sent[0] = dispatch(0)
+    with jax.named_scope("relay_down"):
+        ex2d = [second_hop(i, ex1[i]) for i in range(4, 6)]
+    ex2g = ex2
+    with jax.named_scope("gate_sibling"):
+        for c in ex2g:
+            c.wait_recv()
+        sib_g = go(raw.at[1, rows_g], raw.at[1, rows_g], sib_r.at[1], sib)
     with jax.named_scope("shared_weights"):
         for m in shx:
             m.wait_recv()
@@ -417,10 +413,14 @@
         live = lax.rem(lax.div(iota((256, 512), 1), 4), 4) == 2
         act = jnp.where(live, act, 0.0).astype(BF16)
         shared = jnp.dot(act, sh, preferred_element_type=F32)
+    with jax.named_scope("gate_up_other"):
+        sib_g.wait_recv()
+        wgb[1, :, 0:256] = raw[1, :, 0, :]
+        wgb[1, :, 256:512] = raw[1, :, 1, :]
     with jax.named_scope("pass_on"):
         pass_on(0, sent[0])
     with jax.named_scope("down_sibling"):
-        for c in ex2:
+        for c in ex2d:
             c.wait_recv()
         sib_d = go(wdb.at[1, rows_d], wdb.at[1, rows_d], sib_r.at[2], sib)
     with jax.named_scope("wait_exchange"):

time: 100 us -> 102 us (1.020)
  the two profiles are of different devices: /device:TPU:4 before, /device:TPU:1 now
where the time goes in v11:
time: 102 us
  Pallas kernels  97.7 us (96%)
  local copies, waits for them, and re-layouts  3.73 us (4%)
    pallas_call x1, Pallas kernels, shards(): pl.pallas_call(layer_kernel, out_shape=(sds((32, 1536), BF16), sds((NZ, N...  97.7 us
    unnamed x2, local copies, waits for them, and re-layouts  3.73 us

profile of v11, /device:TPU:1, one launch (start us, length us, event | category | flops | bytes accessed | tf_op | source)
XLA Modules:
  0.0 102.1 jit_solution(16582831938522799940)
XLA Ops:
  0.6 97.7 %layer.1 = (bf16[32,1536]{1,0:T(8,128)(2,1)}, bf16[8,4,4,8,2,128]{5,4,3,2,1,0:T(2,128)(2,1)}, bf16[128,8,2,128]{3,2,1,0:T(2,128)(2,1)}) custom-call(bf16[64,768]{1,0:T(8,128)(2,1)} %q_hbm.1, bf16[64,256]{1,0:T(8,128)(2,1)} %k_hbm.1, bf16[64,256]{1,0:T(8,128)(2,1)} %v_hbm.1, s32[64]{0:T(128)} %len_ref.1, bf16[12,768]{1,0:T(8,128)(2,1)} %bitcast.14, ...), custom_call_target="tpu_custom_call" | custom-call | tf_op jit(solution)/shard_map/layer/pallas_call | solution.py:550
  98.3 1.5 %copy.20 = bf16[32,1536]{1,0:T(8,128)(2,1)} copy(bf16[32,1536]{1,0:T(8,128)(2,1)} %get-tuple-element.10) | data formatting | bytes 196608
  99.9 2.2 %copy.21 = bf16[128,1,8,2,128]{4,3,2,1,0:T(2,128)(2,1)} copy(bf16[128,1,8,2,128]{4,3,2,1,0:T(2,128)(2,1)} %bitcast.12) | data formatting | bytes 1048576
